TPU v7x, 512 devices: a whole 4x8x8 slice. The times are simulated.
512 devices in a mesh: seq: 64 (over x, z, core), head: 8 (over y).
Axes of the slice: x: 4, y: 8, z: 8, core: 2. Of those that a mesh axis runs over, the one named last changes fastest.
Arguments:
- rotated_queries: bfloat16 [32768, 4096], P(('seq', 'head')), may hold values from -6 to 6
- rotated_keys: bfloat16 [32768, 2048], P(('seq', 'head')), may hold values from -6 to 6
- value_matrix: bfloat16 [32768, 2048], P(('seq', 'head')), may hold values from -6 to 6
- output_rows: bfloat16 [32768, 4096], P(('seq', 'head')), may hold values from -6 to 6
- output_gradient: bfloat16 [32768, 4096], P(('seq', 'head')), may hold values from -6 to 6
- softmax_log_total: float32 [32, 32768], P(None, ('seq', 'head')), may hold values from 4 to 7
- doc_ids: int32 [32768], replicated, may hold values from 0 to 32, never falling along the last dimension, each value on 1 to 2048 neighbouring positions
Outputs:
- query_grad: bfloat16 [32768, 4096], P('seq', 'head')
- key_grad: bfloat16 [32768, 2048], P('seq', 'head')
- value_grad: bfloat16 [32768, 2048], P('seq', 'head')
Inputs may be any that keep to these rules, and one draw needn't show every extreme that they name: `doc_ids`: ids never fall from one token to the next; no document is longer than 2048 tokens.
All inputs are finite; a program needn't handle non-finite values.
Results may differ from a plain program's by a relative error of at most 0.0055.
Values may be sent and summed in bfloat16 or wider, within the bound.
No kernel may reach another device: no remote copies, remote signals or barrier semaphores. Data moves between devices by JAX's collectives and lax.ppermute only.
A program may use at most 64 MiB of HBM per device.

v0:
```python
import jax
import jax.numpy as jnp
from jax import lax
from jax.sharding import PartitionSpec as P

HEAD_SIZE = 128
LOOKBACK_SPAN = 1024


score_scale = 168.0 ** (-0.5)


def shifted(value, axis, steps):
    count = lax.axis_size(axis)
    leading, last = (max(0, -steps), min(count, count - steps))
    return lax.ppermute(value, axis, [(source, source + steps) for source in range(leading, last)])


def tile_mask(doc_ids, query_start, key_start, row_count, number_of_tokens):
    query_pos = query_start + jnp.arange(row_count, dtype=jnp.int32)
    key_pos = key_start + jnp.arange(row_count, dtype=jnp.int32)
    query_doc = lax.dynamic_slice_in_dim(
        doc_ids, jnp.clip(query_start, 0, number_of_tokens - row_count), row_count, 0
    )
    key_doc = lax.dynamic_slice_in_dim(
        doc_ids, jnp.clip(key_start, 0, number_of_tokens - row_count), row_count, 0
    )
    gap = query_pos[:, None] - key_pos[None, :]
    inside = (
        (key_pos[None, :] >= 0)
        & (query_pos[:, None] < number_of_tokens)
        & (gap >= 0)
        & (gap < LOOKBACK_SPAN)
    )
    return inside & (query_doc[:, None] == key_doc[None, :])


def tile_terms(
    query_piece, gradient_piece, logsumexp_piece, delta_piece, key_piece, value_piece, allowed
):
    row_count = query_piece.shape[0]
    col_count = key_piece.shape[0]
    key_heads = key_piece.shape[1] // HEAD_SIZE
    query_group_width = logsumexp_piece.shape[0] // key_heads
    query_four = query_piece.reshape(row_count, key_heads, query_group_width, HEAD_SIZE)
    grad_four = gradient_piece.reshape(row_count, key_heads, query_group_width, HEAD_SIZE)
    key_three = key_piece.reshape(col_count, key_heads, HEAD_SIZE)
    value_three = value_piece.reshape(col_count, key_heads, HEAD_SIZE)
    lse_three = logsumexp_piece.reshape(key_heads, query_group_width, row_count)[..., None]
    delta_three = delta_piece.reshape(key_heads, query_group_width, row_count)[..., None]
    scores = (
        jnp.einsum("rgad,cgd->garc", query_four, key_three, preferred_element_type=jnp.float32)
        * score_scale
    )
    prob_full = jnp.where(allowed[None, None], jnp.exp(scores - lse_three), 0.0)
    probability_narrow = prob_full.astype(jnp.bfloat16)
    prob_grad = jnp.einsum(
        "rgad,cgd->garc", grad_four, value_three, preferred_element_type=jnp.float32
    )
    score_gradient = (score_scale * prob_full * (prob_grad - delta_three)).astype(jnp.bfloat16)
    query_part = jnp.einsum(
        "garc,cgd->rgad", score_gradient, key_three, preferred_element_type=jnp.float32
    ).reshape(row_count, -1)
    key_portion = jnp.einsum(
        "plmw,mplo->wpo", score_gradient, query_four, preferred_element_type=jnp.float32
    ).reshape(col_count, -1)
    value_portion = jnp.einsum(
        "plmw,mplo->wpo", probability_narrow, grad_four, preferred_element_type=jnp.float32
    ).reshape(col_count, -1)
    return (query_part, key_portion, value_portion)


def on_device(
    rotated_queries,
    rotated_keys,
    value_matrix,
    output_rows,
    output_gradient,
    softmax_log_total,
    doc_ids,
):
    heads_all = softmax_log_total.shape[0]
    local_tokens = rotated_queries.shape[0]
    delta_rows = jnp.einsum(
        "thd,thd->ht",
        output_gradient.astype(jnp.float32).reshape(local_tokens, heads_all, HEAD_SIZE),
        output_rows.astype(jnp.float32).reshape(local_tokens, heads_all, HEAD_SIZE),
    )
    queries, keys, values, grads = (
        lax.all_to_all(rotated_queries, "head", split_axis=1, concat_axis=0, tiled=True),
        lax.all_to_all(rotated_keys, "head", split_axis=1, concat_axis=0, tiled=True),
        lax.all_to_all(value_matrix, "head", split_axis=1, concat_axis=0, tiled=True),
        lax.all_to_all(output_gradient, "head", split_axis=1, concat_axis=0, tiled=True),
    )
    lse_block, delta_block = (
        lax.all_to_all(softmax_log_total, "head", split_axis=0, concat_axis=1, tiled=True),
        lax.all_to_all(delta_rows, "head", split_axis=0, concat_axis=1, tiled=True),
    )
    row_count = queries.shape[0]
    number_of_tokens = doc_ids.shape[0]
    shard_index = lax.axis_index("seq")
    own_start = shard_index * row_count
    reach_count = LOOKBACK_SPAN // row_count

    def terms(
        query_piece,
        gradient_piece,
        logsumexp_piece,
        delta_piece,
        key_piece,
        value_piece,
        query_start,
        key_start,
    ):
        allowed = tile_mask(doc_ids, query_start, key_start, row_count, number_of_tokens)
        return tile_terms(
            query_piece,
            gradient_piece,
            logsumexp_piece,
            delta_piece,
            key_piece,
            value_piece,
            allowed,
        )

    query_grad, key_grad, value_grad = terms(
        queries, grads, lse_block, delta_block, keys, values, own_start, own_start
    )
    far_parts = []
    for offset in range(1, reach_count + 1):
        near_keys, near_values = shifted((keys, values), "seq", offset)
        query_part, key_portion, value_portion = terms(
            queries,
            grads,
            lse_block,
            delta_block,
            near_keys,
            near_values,
            own_start,
            own_start - offset * row_count,
        )
        query_grad = query_grad + query_part
        far_parts.append((key_portion, value_portion))
    for offset in range(1, reach_count + 1):
        back_keys, back_values = shifted(
            (far_parts[offset - 1][0], far_parts[offset - 1][1]), "seq", -offset
        )
        key_grad = key_grad + back_keys
        value_grad = value_grad + back_values
    return (
        query_grad.astype(jnp.bfloat16),
        key_grad.astype(jnp.bfloat16),
        value_grad.astype(jnp.bfloat16),
    )


def solution(mesh):
    return jax.shard_map(
        on_device,
        mesh=mesh,
        in_specs=(
            P(("seq", "head"), None),
            P(("seq", "head"), None),
            P(("seq", "head"), None),
            P(("seq", "head"), None),
            P(("seq", "head"), None),
            P(None, ("seq", "head")),
            P(),
        ),
        out_specs=(P("seq", "head"), P("seq", "head"), P("seq", "head")),
        check_vma=False,
    )
```

profile of v0, /device:TPU:7, one launch (start us, length us, event | category | flops | bytes accessed | tf_op | source)
XLA Modules:
  0.0 161.7 jit_solution(17015188861388783501)
XLA Ops:
  0.7 1.5 reshape.412
  2.2 6.8 %all-to-all-start.2 = ((f32[8,1,256]{2,1,0:T(1,128)}), f32[8,1,256]{2,1,0:T(1,128)S(1)}, u32[]{:S(2)}, u32[]{:S(2)}) async-start(f32[8,1,256]{2,1,0:T(1,128)} %reshape.412), calls=%async_computation.2 | async-start | bytes 16384 | tf_op jit(solution)/shard_map/all_to_all | solution.py:96
  9.0 1.1 copy.221
  10.1 1.1 copy.220
  12.4 3.2 %all-to-all-done.2 = f32[8,1,256]{2,1,0:T(1,128)S(1)} async-done(((f32[8,1,256]{2,1,0:T(1,128)}), f32[8,1,256]{2,1,0:T(1,128)S(1)}, u32[]{:S(2)}, u32[]{:S(2)}) %all-to-all-start.2) | async-done | bytes 8224 | tf_op jit(solution)/shard_map/all_to_all | solution.py:96
  15.6 3.5 %all-to-all-start.5 = ((f32[8,1,256]{2,1,0:T(1,128)}), f32[8,1,256]{2,1,0:T(1,128)S(1)}, u32[]{:S(2)}, u32[]{:S(2)}) async-start(f32[8,1,256]{2,1,0:T(1,128)} %reshape.410), calls=%async_computation.5 | async-start | bytes 16384 | tf_op jit(solution)/shard_map/all_to_all | solution.py:97
  19.0 1.7 %copy.231 = bf16[8,8,8,256]{3,2,0,1:T(8,128)(2,1)} copy(bf16[8,8,8,256]{3,2,1,0:T(8,128)(2,1)} %bitcast.207) | data formatting | bytes 524288 | tf_op jit(solution)/shard_map/all_to_all | solution.py:91
  20.7 4.9 %all-to-all-done.5 = f32[8,1,256]{2,1,0:T(1,128)S(1)} async-done(((f32[8,1,256]{2,1,0:T(1,128)}), f32[8,1,256]{2,1,0:T(1,128)S(1)}, u32[]{:S(2)}, u32[]{:S(2)}) %all-to-all-start.5) | async-done | bytes 8224 | tf_op jit(solution)/shard_map/all_to_all | solution.py:97
  25.6 3.4 %all-to-all-start = ((bf16[64,8,256]{2,0,1:T(8,128)(2,1)}), bf16[64,8,256]{2,0,1:T(8,128)(2,1)S(1)}, u32[]{:S(2)}, u32[]{:S(2)}) async-start(bf16[64,8,256]{2,0,1:T(8,128)(2,1)} %bitcast.180), calls=%async_computation | async-start | bytes 524288 | tf_op jit(solution)/shard_map/all_to_all | solution.py:91
  29.8 8.6 %all-to-all-done = bf16[64,8,256]{2,0,1:T(8,128)(2,1)S(1)} async-done(((bf16[64,8,256]{2,0,1:T(8,128)(2,1)}), bf16[64,8,256]{2,0,1:T(8,128)(2,1)S(1)}, u32[]{:S(2)}, u32[]{:S(2)}) %all-to-all-start) | async-done | bytes 262176 | tf_op jit(solution)/shard_map/all_to_all | solution.py:91
  38.4 3.4 %all-to-all-start.3 = ((bf16[64,8,256]{2,0,1:T(8,128)(2,1)}), bf16[64,8,256]{2,0,1:T(8,128)(2,1)S(1)}, u32[]{:S(2)}, u32[]{:S(2)}) async-start(bf16[64,8,256]{2,0,1:T(8,128)(2,1)} %bitcast.179), calls=%async_computation.3 | async-start | bytes 524288 | tf_op jit(solution)/shard_map/all_to_all | solution.py:92
  42.7 8.4 %all-to-all-done.3 = bf16[64,8,256]{2,0,1:T(8,128)(2,1)S(1)} async-done(((bf16[64,8,256]{2,0,1:T(8,128)(2,1)}), bf16[64,8,256]{2,0,1:T(8,128)(2,1)S(1)}, u32[]{:S(2)}, u32[]{:S(2)}) %all-to-all-start.3) | async-done | bytes 262176 | tf_op jit(solution)/shard_map/all_to_all | solution.py:92
  51.1 3.5 %all-to-all-start.1 = ((bf16[64,8,512]{2,0,1:T(8,128)(2,1)}), bf16[64,8,512]{2,0,1:T(8,128)(2,1)S(1)}, u32[]{:S(2)}, u32[]{:S(2)}) async-start(bf16[64,8,512]{2,0,1:T(8,128)(2,1)} %bitcast.178), calls=%async_computation.1 | async-start | bytes 1048576 | tf_op jit(solution)/shard_map/all_to_all | solution.py:90
  54.6 0.9 copy.228
  55.4 11.2 %all-to-all-done.1 = bf16[64,8,512]{2,0,1:T(8,128)(2,1)S(1)} async-done(((bf16[64,8,512]{2,0,1:T(8,128)(2,1)}), bf16[64,8,512]{2,0,1:T(8,128)(2,1)S(1)}, u32[]{:S(2)}, u32[]{:S(2)}) %all-to-all-start.1) | async-done | bytes 524320 | tf_op jit(solution)/shard_map/all_to_all | solution.py:90
  66.6 3.5 %all-to-all-start.4 = ((bf16[64,8,512]{2,0,1:T(8,128)(2,1)}), bf16[64,8,512]{2,0,1:T(8,128)(2,1)S(1)}, u32[]{:S(2)}, u32[]{:S(2)}) async-start(bf16[64,8,512]{2,0,1:T(8,128)(2,1)} %bitcast.177), calls=%async_computation.4 | async-start | bytes 1048576 | tf_op jit(solution)/shard_map/all_to_all | solution.py:93
  70.2 0.9 fusion.44
  71.1 4.0 %collective-permute-start.3 = (bf16[512,256]{1,0:T(8,128)(2,1)S(1)}, bf16[512,256]{1,0:T(8,128)(2,1)}, u32[]{:S(2)}, u32[]{:S(2)}) collective-permute-start(bf16[512,256]{1,0:T(8,128)(2,1)S(1)} %bitcast.198), channel_id=1, source_target_pairs={{0,16},{8,24},{16,32},{24,40},{32,48},{40,56},{48,64},{56,72},{64,... | collective-permute-start | bytes 786440 | tf_op jit(solution)/shard_map/ppermute | solution.py:16
  75.1 10.6 %collective-permute-start.1 = (bf16[512,256]{1,0:T(8,128)(2,1)S(1)}, bf16[512,256]{1,0:T(8,128)(2,1)S(1)}, u32[]{:S(2)}, u32[]{:S(2)}) collective-permute-start(bf16[512,256]{1,0:T(8,128)(2,1)S(1)} %bitcast.199), channel_id=1, source_target_pairs={{0,8},{8,16},{16,24},{24,32},{32,40},{40,48},{48,56},{56,64},{64,7... | collective-permute-start | bytes 786440 | tf_op jit(solution)/shard_map/ppermute | solution.py:16
  85.7 4.0 %collective-permute-start.2 = (bf16[512,256]{1,0:T(8,128)(2,1)S(1)}, bf16[512,256]{1,0:T(8,128)(2,1)S(1)}, u32[]{:S(2)}, u32[]{:S(2)}) collective-permute-start(bf16[512,256]{1,0:T(8,128)(2,1)S(1)} %bitcast.195), channel_id=1, source_target_pairs={{0,16},{8,24},{16,32},{24,40},{32,48},{40,56},{48,64},{56,72},{64,... | collective-permute-start | bytes 786440 | tf_op jit(solution)/shard_map/ppermute | solution.py:16
  89.7 2.2 %collective-permute-start = (bf16[512,256]{1,0:T(8,128)(2,1)S(1)}, bf16[512,256]{1,0:T(8,128)(2,1)S(1)}, u32[]{:S(2)}, u32[]{:S(2)}) collective-permute-start(bf16[512,256]{1,0:T(8,128)(2,1)S(1)} %bitcast.196), channel_id=1, source_target_pairs={{0,8},{8,16},{16,24},{24,32},{32,40},{40,48},{48,56},{56,64},{64,7... | collective-permute-start | bytes 786440 | tf_op jit(solution)/shard_map/ppermute | solution.py:16
  91.9 2.5 %fusion.34 = (pred[512,512]{0,1:T(8,128)(4,1)S(1)}, pred[512,512]{0,1:T(8,128)(4,1)}, pred[512,512]{0,1:T(8,128)(4,1)S(1)}) fusion(s32[512]{0:T(512)S(1)} %get-tuple-element.23, s32[512]{0:T(512)S(1)} %get-tuple-element.16, s32[512]{0:T(512)S(1)} %get-tuple-element.25, s32[512]{0:T(512)S(1)} %get-tuple-element.15, pred[512]{0:T(512)(128)(4,1)S(1)} %get-tuple-element.21, ...), kind=kLoop, calls=%fused_computation.46 | loop fusion | flops 6291456 | bytes 800768 | tf_op jit(solution)/shard_map/and | solution.py:35
  97.7 1.8 %copy.147 = bf16[512,256]{0,1:T(8,128)(2,1)} copy(bf16[512,256]{1,0:T(8,128)(2,1)} %collective-permute-done.3) | data formatting | bytes 524288 | tf_op jit(solution)/shard_map/ppermute | solution.py:16
  99.5 0.8 copy.140
  103.2 1.6 %fusion.9 = bf16[2,2,512,512]{2,3,1,0:T(8,128)(2,1)S(1)} fusion(f32[2,512,512,2]{2,1,3,0:T(8,128)S(1)} %fusion.45, bf16[512,2,2,128]{0,3,2,1:T(8,128)(2,1)S(1)} %copy.161, f32[2,2,512]{2,1,0:T(2,128)S(1)} %sub.103, f32[2,2,512]{2,1,0:T(2,128)S(1)} %sub.100, pred[512,512]{0,1:T(8,128)(4,1)S(1)} %get-tuple-element.20, bf16[512,2,128,1]{2,1,0,3:T(2,128)(2,1)S(1)} %bitcast.211), kind=kOutput, calls=%fused_computation.14 | convolution fusion | flops 275775488 | bytes 7356416 | tf_op jit(solution)/shard_map/rgad,cgd->garc/dot_general | solution.py:57
  105.2 1.6 fusion.48
  106.8 1.4 fusion.51
  109.0 1.9 %fusion.15 = f32[2,512,128,1]{1,2,3,0:T(8,128)} fusion(bf16[512,2,2,128]{0,3,2,1:T(8,128)(2,1)S(1)} %copy.161, f32[2,512,512,2]{2,1,3,0:T(8,128)S(1)} %fusion.47, f32[2,2,512]{2,1,0:T(2,128)S(1)} %sub.100, pred[512,512]{0,1:T(8,128)(4,1)S(1)} %get-tuple-element.18), kind=kOutput, calls=%fused_computation.21 | convolution fusion | flops 272629760 | bytes 5513216 | tf_op jit(solution)/shard_map/plmw,mplo->wpo/dot_general | solution.py:67
  110.8 2.8 %fusion.1 = bf16[2,2,512,512]{2,3,1,0:T(8,128)(2,1)S(1)} fusion(f32[2,512,512,2]{2,1,3,0:T(8,128)S(1)} %fusion.47, bf16[512,2,128,1]{0,2,3,1:T(8,128)(2,1)S(1)} %bitcast.210, bf16[512,2,2,128]{0,3,2,1:T(8,128)(2,1)} %copy-done.3, f32[2,2,512]{2,1,0:T(2,128)S(1)} %sub.103, f32[2,2,512]{2,1,0:T(2,128)S(1)} %sub.100, pred[512,512]{0,1:T(8,128)(4,1)} %copy-done.6), kind=kOutput, calls=%fused_computation.2 | convolution fusion | flops 275775488 | bytes 7356416 | tf_op jit(solution)/shard_map/rgad,cgd->garc/dot_general | solution.py:57
  113.6 2.1 %copy.168 = f32[512,256]{1,0:T(8,128)} copy(f32[512,256]{0,1:T(8,128)} %bitcast.205) | data formatting | bytes 1048576 | tf_op jit(solution)/shard_map/reshape | solution.py:69
  115.7 1.6 fusion.50
  117.3 2.1 %copy.159 = f32[512,256]{1,0:T(8,128)} copy(f32[512,256]{0,1:T(8,128)} %bitcast.194) | data formatting | bytes 1048576 | tf_op jit(solution)/shard_map/reshape | solution.py:66
  119.4 4.2 %collective-permute-start.5 = (f32[512,256]{1,0:T(8,128)}, f32[512,256]{1,0:T(8,128)}, u32[]{:S(2)}, u32[]{:S(2)}) collective-permute-start(f32[512,256]{1,0:T(8,128)} %copy.159), channel_id=1, source_target_pairs={{16,0},{24,8},{32,16},{40,24},{48,32},{56,40},{64,48},{72,56},{80,... | collective-permute-start | bytes 1572872 | tf_op jit(solution)/shard_map/ppermute | solution.py:16
  123.6 4.3 %collective-permute-start.7 = (f32[512,256]{1,0:T(8,128)}, f32[512,256]{1,0:T(8,128)}, u32[]{:S(2)}, u32[]{:S(2)}) collective-permute-start(f32[512,256]{1,0:T(8,128)} %copy.168), channel_id=1, source_target_pairs={{16,0},{24,8},{32,16},{40,24},{48,32},{56,40},{64,48},{72,56},{80,... | collective-permute-start | bytes 1572872 | tf_op jit(solution)/shard_map/ppermute | solution.py:16
  128.7 1.9 %fusion.17 = f32[2,512,128,1]{1,2,3,0:T(8,128)} fusion(bf16[512,2,2,128]{0,3,2,1:T(8,128)(2,1)S(1)} %copy-done.4, f32[2,512,512,2]{2,1,3,0:T(8,128)S(1)} %fusion.46, f32[2,2,512]{2,1,0:T(2,128)S(1)} %sub.100, pred[512,512]{0,1:T(8,128)(4,1)S(1)} %copy-done.5), kind=kOutput, calls=%fused_computation.22 | convolution fusion | flops 272629760 | bytes 5513216 | tf_op jit(solution)/shard_map/plmw,mplo->wpo/dot_general | solution.py:67
  130.6 3.0 %fusion.5 = bf16[2,2,512,512]{2,3,1,0:T(8,128)(2,1)} fusion(f32[2,512,512,2]{2,1,3,0:T(8,128)S(1)} %fusion.46, bf16[512,2,128,1]{0,2,3,1:T(8,128)(2,1)S(1)} %bitcast.209, bf16[512,2,2,128]{0,3,2,1:T(8,128)(2,1)S(1)} %copy-done.4, f32[2,2,512]{2,1,0:T(2,128)S(1)} %sub.103, f32[2,2,512]{2,1,0:T(2,128)S(1)} %sub.100, pred[512,512]{0,1:T(8,128)(4,1)S(1)} %copy-done.5), kind=kOutput, calls=%fused_computation.8 | convolution fusion | flops 275775488 | bytes 7356416 | tf_op jit(solution)/shard_map/rgad,cgd->garc/dot_general | solution.py:57
  133.6 2.0 %copy.164 = f32[512,256]{1,0:T(8,128)} copy(f32[512,256]{0,1:T(8,128)} %bitcast.204) | data formatting | bytes 1048576 | tf_op jit(solution)/shard_map/reshape | solution.py:69
  135.7 3.2 %fusion.49 = f32[2,512,128,1]{1,2,3,0:T(8,128)} fusion(bf16[2,2,512,512]{2,3,1,0:T(8,128)(2,1)} %fusion.5, bf16[512,2,2,128]{0,3,2,1:T(8,128)(2,1)S(1)} %copy.152), kind=kOutput, calls=%fused_computation.72 | convolution fusion | flops 268435456 | bytes 3145728 | tf_op jit(solution)/shard_map/plmw,mplo->wpo/dot_general | solution.py:64
  138.9 2.1 %copy.155 = f32[512,256]{1,0:T(8,128)} copy(f32[512,256]{0,1:T(8,128)} %bitcast.193) | data formatting | bytes 1048576 | tf_op jit(solution)/shard_map/reshape | solution.py:66
  140.9 3.9 %collective-permute-start.4 = (f32[512,256]{1,0:T(8,128)}, f32[512,256]{1,0:T(8,128)}, u32[]{:S(2)}, u32[]{:S(2)}) collective-permute-start(f32[512,256]{1,0:T(8,128)} %copy.155), channel_id=1, source_target_pairs={{8,0},{16,8},{24,16},{32,24},{40,32},{48,40},{56,48},{64,56},{72,6... | collective-permute-start | bytes 1572872 | tf_op jit(solution)/shard_map/ppermute | solution.py:16
  144.8 1.9 %collective-permute-start.6 = (f32[512,256]{1,0:T(8,128)}, f32[512,256]{1,0:T(8,128)}, u32[]{:S(2)}, u32[]{:S(2)}) collective-permute-start(f32[512,256]{1,0:T(8,128)} %copy.164), channel_id=1, source_target_pairs={{8,0},{16,8},{24,16},{32,24},{40,32},{48,40},{56,48},{64,56},{72,6... | collective-permute-start | bytes 1572872 | tf_op jit(solution)/shard_map/ppermute | solution.py:16
  146.7 2.3 %convolution_add_fusion.1 = f32[2,2,512,128]{2,3,1,0:T(8,128)S(1)} fusion(f32[2,2,512,128]{2,3,1,0:T(8,128)} %fusion.51, bf16[512,2,128,1]{0,2,3,1:T(8,128)(2,1)S(1)} %bitcast.182, bf16[2,2,512,512]{2,3,1,0:T(8,128)(2,1)} %fusion.5), kind=kOutput, calls=%fused_computation.34 | convolution fusion | flops 268697600 | bytes 4456448 | tf_op jit(solution)/shard_map/garc,cgd->rgad/dot_general | solution.py:61
  149.5 1.0 copy.169
  150.5 1.2 copy.156
  151.7 3.3 %fusion.19 = f32[2,512,128,1]{1,2,3,0:T(8,128)S(1)} fusion(bf16[512,2,2,128]{0,3,2,1:T(8,128)(2,1)} %copy-done.3, f32[2,512,512,2]{2,1,3,0:T(8,128)} %copy-done, f32[2,2,512]{2,1,0:T(2,128)S(1)} %sub.100, pred[512,512]{0,1:T(8,128)(4,1)S(1)} %get-tuple-element.20), kind=kOutput, calls=%fused_computation.23 | convolution fusion | flops 272629760 | bytes 5513216 | tf_op jit(solution)/shard_map/plmw,mplo->wpo/dot_general | solution.py:67
  155.3 2.0 %add_convert_fusion.1 = bf16[512,256]{1,0:T(8,128)(2,1)} fusion(f32[512,256]{1,0:T(8,128)} %collective-permute-done.5, f32[512,256]{1,0:T(8,128)S(1)} %copy.156, f32[512,256]{1,0:T(8,128)} %collective-permute-done.4), kind=kLoop, calls=%fused_computation.50 | loop fusion | flops 393216 | bytes 1835008 | tf_op jit(solution)/shard_map/convert_element_type | solution.py:152
  157.3 2.4 %collective-permute-done.6 = f32[512,256]{1,0:T(8,128)} collective-permute-done((f32[512,256]{1,0:T(8,128)}, f32[512,256]{1,0:T(8,128)}, u32[]{:S(2)}, u32[]{:S(2)}) %collective-permute-start.6) | collective-permute-done | bytes 524320 | tf_op jit(solution)/shard_map/ppermute | solution.py:16
  159.7 2.0 %add_convert_fusion = bf16[512,256]{1,0:T(8,128)(2,1)} fusion(f32[512,256]{1,0:T(8,128)} %collective-permute-done.7, f32[512,256]{1,0:T(8,128)S(1)} %copy.165, f32[512,256]{1,0:T(8,128)} %collective-permute-done.6), kind=kLoop, calls=%fused_computation.49 | loop fusion | flops 393216 | bytes 1835008 | tf_op jit(solution)/shard_map/convert_element_type | solution.py:153
  (61 shorter events, 11.2 us)
Async XLA Ops:
  0.6 53.9 %copy-start.1 = (bf16[64,4096]{1,0:T(8,128)(2,1)S(1)}, bf16[64,4096]{1,0:T(8,128)(2,1)}, u32[]{:S(2)}) copy-start(bf16[64,4096]{1,0:T(8,128)(2,1)} %param.11) | copy-start | bytes 1572868
  0.6 28.4 %copy-start.7 = (bf16[64,2048]{1,0:T(8,128)(2,1)S(1)}, bf16[64,2048]{1,0:T(8,128)(2,1)}, u32[]{:S(2)}) copy-start(bf16[64,2048]{1,0:T(8,128)(2,1)} %param.9) | copy-start | bytes 786436
  0.7 41.2 %copy-start.2 = (bf16[64,4096]{1,0:T(8,128)(2,1)S(1)}, bf16[64,4096]{1,0:T(8,128)(2,1)}, u32[]{:S(2)}) copy-start(bf16[64,4096]{1,0:T(8,128)(2,1)} %param.7) | copy-start | bytes 1572868
  2.2 13.4 %all-to-all-start.2 = ((f32[8,1,256]{2,1,0:T(1,128)}), f32[8,1,256]{2,1,0:T(1,128)S(1)}, u32[]{:S(2)}, u32[]{:S(2)}) async-start(f32[8,1,256]{2,1,0:T(1,128)} %reshape.412), calls=%async_computation.2 | async-start | bytes 16384 | tf_op jit(solution)/shard_map/all_to_all | solution.py:96
  15.6 10.1 %all-to-all-start.5 = ((f32[8,1,256]{2,1,0:T(1,128)}), f32[8,1,256]{2,1,0:T(1,128)S(1)}, u32[]{:S(2)}, u32[]{:S(2)}) async-start(f32[8,1,256]{2,1,0:T(1,128)} %reshape.410), calls=%async_computation.5 | async-start | bytes 16384 | tf_op jit(solution)/shard_map/all_to_all | solution.py:97
  25.6 12.8 %all-to-all-start = ((bf16[64,8,256]{2,0,1:T(8,128)(2,1)}), bf16[64,8,256]{2,0,1:T(8,128)(2,1)S(1)}, u32[]{:S(2)}, u32[]{:S(2)}) async-start(bf16[64,8,256]{2,0,1:T(8,128)(2,1)} %bitcast.180), calls=%async_computation | async-start | bytes 524288 | tf_op jit(solution)/shard_map/all_to_all | solution.py:91
  38.4 12.7 %all-to-all-start.3 = ((bf16[64,8,256]{2,0,1:T(8,128)(2,1)}), bf16[64,8,256]{2,0,1:T(8,128)(2,1)S(1)}, u32[]{:S(2)}, u32[]{:S(2)}) async-start(bf16[64,8,256]{2,0,1:T(8,128)(2,1)} %bitcast.179), calls=%async_computation.3 | async-start | bytes 524288 | tf_op jit(solution)/shard_map/all_to_all | solution.py:92
  51.1 15.5 %all-to-all-start.1 = ((bf16[64,8,512]{2,0,1:T(8,128)(2,1)}), bf16[64,8,512]{2,0,1:T(8,128)(2,1)S(1)}, u32[]{:S(2)}, u32[]{:S(2)}) async-start(bf16[64,8,512]{2,0,1:T(8,128)(2,1)} %bitcast.178), calls=%async_computation.1 | async-start | bytes 1048576 | tf_op jit(solution)/shard_map/all_to_all | solution.py:90
  66.6 34.9 %all-to-all-start.4 = ((bf16[64,8,512]{2,0,1:T(8,128)(2,1)}), bf16[64,8,512]{2,0,1:T(8,128)(2,1)S(1)}, u32[]{:S(2)}, u32[]{:S(2)}) async-start(bf16[64,8,512]{2,0,1:T(8,128)(2,1)} %bitcast.177), calls=%async_computation.4 | async-start | bytes 1048576 | tf_op jit(solution)/shard_map/all_to_all | solution.py:93
  71.1 26.6 %collective-permute-start.3 = (bf16[512,256]{1,0:T(8,128)(2,1)S(1)}, bf16[512,256]{1,0:T(8,128)(2,1)}, u32[]{:S(2)}, u32[]{:S(2)}) collective-permute-start(bf16[512,256]{1,0:T(8,128)(2,1)S(1)} %bitcast.198), channel_id=1, source_target_pairs={{0,16},{8,24},{16,32},{24,40},{32,48},{40,56},{48,64},{56,72},{64,... | collective-permute-start | bytes 786440 | tf_op jit(solution)/shard_map/ppermute | solution.py:16
  75.1 24.4 %collective-permute-start.1 = (bf16[512,256]{1,0:T(8,128)(2,1)S(1)}, bf16[512,256]{1,0:T(8,128)(2,1)S(1)}, u32[]{:S(2)}, u32[]{:S(2)}) collective-permute-start(bf16[512,256]{1,0:T(8,128)(2,1)S(1)} %bitcast.199), channel_id=1, source_target_pairs={{0,8},{8,16},{16,24},{24,32},{32,40},{40,48},{48,56},{56,64},{64,7... | collective-permute-start | bytes 786440 | tf_op jit(solution)/shard_map/ppermute | solution.py:16
  85.7 14.7 %collective-permute-start.2 = (bf16[512,256]{1,0:T(8,128)(2,1)S(1)}, bf16[512,256]{1,0:T(8,128)(2,1)S(1)}, u32[]{:S(2)}, u32[]{:S(2)}) collective-permute-start(bf16[512,256]{1,0:T(8,128)(2,1)S(1)} %bitcast.195), channel_id=1, source_target_pairs={{0,16},{8,24},{16,32},{24,40},{32,48},{40,56},{48,64},{56,72},{64,... | collective-permute-start | bytes 786440 | tf_op jit(solution)/shard_map/ppermute | solution.py:16
  89.7 10.8 %collective-permute-start = (bf16[512,256]{1,0:T(8,128)(2,1)S(1)}, bf16[512,256]{1,0:T(8,128)(2,1)S(1)}, u32[]{:S(2)}, u32[]{:S(2)}) collective-permute-start(bf16[512,256]{1,0:T(8,128)(2,1)S(1)} %bitcast.196), channel_id=1, source_target_pairs={{0,8},{8,16},{16,24},{24,32},{32,40},{40,48},{48,56},{56,64},{64,7... | collective-permute-start | bytes 786440 | tf_op jit(solution)/shard_map/ppermute | solution.py:16
  94.4 14.5 %copy-start.6 = (pred[512,512]{0,1:T(8,128)(4,1)}, pred[512,512]{0,1:T(8,128)(4,1)S(1)}, u32[]{:S(2)}) copy-start(pred[512,512]{0,1:T(8,128)(4,1)S(1)} %get-tuple-element.18) | copy-start | bytes 786436
  101.5 1.7 %copy-start.10 = (bf16[512,2,128]{2,1,0:T(2,128)(2,1)S(1)}, bf16[512,2,128]{2,1,0:T(2,128)(2,1)}, u32[]{:S(2)}) copy-start(bf16[512,2,128]{2,1,0:T(2,128)(2,1)} %reshape.378) | copy-start | bytes 786436
  102.4 6.5 %copy-start.3 = (bf16[512,2,2,128]{0,3,2,1:T(8,128)(2,1)}, bf16[512,2,2,128]{0,3,2,1:T(8,128)(2,1)S(1)}, u32[]{:S(2)}) copy-start(bf16[512,2,2,128]{0,3,2,1:T(8,128)(2,1)S(1)} %copy.161) | copy-start | bytes 1572868
  103.2 2.0 %copy-start = (f32[2,512,512,2]{2,1,3,0:T(8,128)}, f32[2,512,512,2]{2,1,3,0:T(8,128)S(1)}, u32[]{:S(2)}) copy-start(f32[2,512,512,2]{2,1,3,0:T(8,128)S(1)} %fusion.45) | copy-start | bytes 12582916
  108.9 1.9 %copy-start.9 = (bf16[512,256]{0,1:T(8,128)(2,1)S(1)}, bf16[512,256]{0,1:T(8,128)(2,1)}, u32[]{:S(2)}) copy-start(bf16[512,256]{0,1:T(8,128)(2,1)} %copy.147) | copy-start | bytes 786436
  119.4 9.3 %copy-start.4 = (bf16[512,2,2,128]{0,3,2,1:T(8,128)(2,1)S(1)}, bf16[512,2,2,128]{0,3,2,1:T(8,128)(2,1)}, u32[]{:S(2)}) copy-start(bf16[512,2,2,128]{0,3,2,1:T(8,128)(2,1)} %copy-done.3) | copy-start | bytes 1572868
  119.4 9.3 %copy-start.5 = (pred[512,512]{0,1:T(8,128)(4,1)S(1)}, pred[512,512]{0,1:T(8,128)(4,1)}, u32[]{:S(2)}) copy-start(pred[512,512]{0,1:T(8,128)(4,1)} %get-tuple-element.19) | copy-start | bytes 786436
  119.4 35.9 %collective-permute-start.5 = (f32[512,256]{1,0:T(8,128)}, f32[512,256]{1,0:T(8,128)}, u32[]{:S(2)}, u32[]{:S(2)}) collective-permute-start(f32[512,256]{1,0:T(8,128)} %copy.159), channel_id=1, source_target_pairs={{16,0},{24,8},{32,16},{40,24},{48,32},{56,40},{64,48},{72,56},{80,... | collective-permute-start | bytes 1572872 | tf_op jit(solution)/shard_map/ppermute | solution.py:16
  123.6 33.7 %collective-permute-start.7 = (f32[512,256]{1,0:T(8,128)}, f32[512,256]{1,0:T(8,128)}, u32[]{:S(2)}, u32[]{:S(2)}) collective-permute-start(f32[512,256]{1,0:T(8,128)} %copy.168), channel_id=1, source_target_pairs={{16,0},{24,8},{32,16},{40,24},{48,32},{56,40},{64,48},{72,56},{80,... | collective-permute-start | bytes 1572872 | tf_op jit(solution)/shard_map/ppermute | solution.py:16
  128.7 1.9 %copy-start.8 = (bf16[512,256]{0,1:T(8,128)(2,1)S(1)}, bf16[512,256]{0,1:T(8,128)(2,1)}, u32[]{:S(2)}) copy-start(bf16[512,256]{0,1:T(8,128)(2,1)} %copy.140) | copy-start | bytes 786436
  140.9 14.4 %collective-permute-start.4 = (f32[512,256]{1,0:T(8,128)}, f32[512,256]{1,0:T(8,128)}, u32[]{:S(2)}, u32[]{:S(2)}) collective-permute-start(f32[512,256]{1,0:T(8,128)} %copy.155), channel_id=1, source_target_pairs={{8,0},{16,8},{24,16},{32,24},{40,32},{48,40},{56,48},{64,56},{72,6... | collective-permute-start | bytes 1572872 | tf_op jit(solution)/shard_map/ppermute | solution.py:16
  144.8 14.9 %collective-permute-start.6 = (f32[512,256]{1,0:T(8,128)}, f32[512,256]{1,0:T(8,128)}, u32[]{:S(2)}, u32[]{:S(2)}) collective-permute-start(f32[512,256]{1,0:T(8,128)} %copy.164), channel_id=1, source_target_pairs={{8,0},{16,8},{24,16},{32,24},{40,32},{48,40},{56,48},{64,56},{72,6... | collective-permute-start | bytes 1572872 | tf_op jit(solution)/shard_map/ppermute | solution.py:16
where the time goes:
time: 164 us; the launch traced here: 162 us
  starting transfers between devices  59.2 us (36%)
  waiting for transfers between devices  38.7 us (24%)
  matrix products  27.4 us (17%)
  local copies, waits for them, and re-layouts  26.2 us (16%)
  other arithmetic  9.1 us (6%)
    ppermute x8, starting transfers between devices, shifted(): lax.ppermute(value, axis, [(source, source + steps) for source in range(l...  35.1 us
    all_to_all x1, waiting for transfers between devices, on_device(): lax.all_to_all(rotated_queries, 'head', split_axis=1, concat_axis=0, tile...  11.2 us
    all_to_all x1, waiting for transfers between devices, on_device(): lax.all_to_all(rotated_keys, 'head', split_axis=1, concat_axis=0, tiled=T...  8.63 us
    all_to_all x1, waiting for transfers between devices, on_device(): lax.all_to_all(value_matrix, 'head', split_axis=1, concat_axis=0, tiled=T...  8.39 us
    dot_general x3, matrix products, tile_terms(): jnp.einsum('rgad,cgd->garc', grad_four, value_three, preferred_element_ty...  7.44 us
    dot_general x3, matrix products, tile_terms(): jnp.einsum('plmw,mplo->wpo', probability_narrow, grad_four, preferred_ele...  7.1 us
    all_to_all x1, starting transfers between devices, on_device(): lax.all_to_all(softmax_log_total, 'head', split_axis=0, concat_axis=1, ti...  6.82 us
    dot_general x3, matrix products, tile_terms(): jnp.einsum('plmw,mplo->wpo', score_gradient, query_four, preferred_elemen...  6.41 us
  transfers between devices with their start and end apart: 14, of which 6 were waited for; matrix products, arithmetic and copies ran while one was open for 26% of the time, Pallas kernels for 0%

commit v1 on v0

v1 whole, which is shorter than its diff:
```python
import math

import jax
import jax.numpy as jnp
from jax import lax
from jax.experimental import pallas as pl
from jax.experimental.pallas import tpu as pltpu
from jax.sharding import Mesh
from jax.sharding import PartitionSpec as P

HEAD_SIZE = 128
LOOKBACK_SPAN = 1024
CORES = 2
PIECE = 64
META_ROWS = 16
TILE = 256

score_scale = 168.0 ** (-0.5)
log2_e = math.log2(math.e)

f32 = jnp.float32
bf16 = jnp.bfloat16


def dot_t(left, right):
    return lax.dot_general(left, right, (((1,), (1,)), ((), ())), preferred_element_type=f32)


def dot_n(left, right):
    return lax.dot_general(left, right, (((1,), (0,)), ((), ())), preferred_element_type=f32)


def t_dot(left, right):
    return lax.dot_general(left, right, (((0,), (0,)), ((), ())), preferred_element_type=f32)


def pack_keys_kernel(key_ref, value_ref, out_ref):
    for at in range(CORES * out_ref.shape[1]):
        columns = slice(at * HEAD_SIZE, (at + 1) * HEAD_SIZE)
        out_ref[at % CORES, at // CORES, 0:PIECE, :] = key_ref[:, columns]
        out_ref[at % CORES, at // CORES, PIECE : 2 * PIECE, :] = value_ref[:, columns]


def pack_keys(keys, values, groups, steps=2):
    width = keys.shape[1] // steps
    return pl.pallas_call(
        pack_keys_kernel,
        grid=(steps,),
        in_specs=[pl.BlockSpec((PIECE, width), lambda i: (0, i))] * 2,
        out_specs=pl.BlockSpec((CORES, groups // steps, 2 * PIECE, HEAD_SIZE), lambda i: (0, i, 0, 0)),
        out_shape=jax.ShapeDtypeStruct((CORES, groups, 2 * PIECE, HEAD_SIZE), bf16),
        name="pack_keys",
    )(keys, values)


def three_parts(value):
    high = value.astype(bf16)
    rest = value - high.astype(f32)
    middle = rest.astype(bf16)
    return [high, middle, (rest - middle.astype(f32)).astype(bf16)]


def pack_queries_kernel(parity_ref, query_ref, grad_ref, row_ref, lse_ref, out_ref):
    groups = out_ref.shape[1]
    receivers = CORES * groups
    heads = 2 * receivers
    width = heads * HEAD_SIZE
    for at in range(receivers):
        for a in range(2):
            columns = slice((2 * at + a) * HEAD_SIZE, (2 * at + a + 1) * HEAD_SIZE)
            core, group = at % CORES, at // CORES
            out_ref[core, group, a * PIECE : (a + 1) * PIECE, :] = query_ref[:, columns]
            out_ref[core, group, (2 + a) * PIECE : (3 + a) * PIECE, :] = grad_ref[:, columns]
    product = grad_ref[...].astype(f32) * row_ref[...].astype(f32)
    product_high = product.astype(bf16)
    product_low = (product - product_high.astype(f32)).astype(bf16)
    which = lax.broadcasted_iota(jnp.int32, (heads, width), 1) // HEAD_SIZE
    member = jnp.where(which == lax.broadcasted_iota(jnp.int32, (heads, width), 0), 1.0, 0.0).astype(bf16)
    delta = dot_t(member, product_high) + dot_t(member, product_low)
    parts = three_parts(lse_ref[...]) + three_parts(delta)
    rows = jnp.concatenate([p.astype(f32) for p in parts], axis=0)
    rows = jnp.concatenate([rows, rows], axis=1)
    lane = lax.broadcasted_iota(jnp.int32, rows.shape, 1) // PIECE
    rows = jnp.where(lane == parity_ref[0], rows, 0.0).astype(bf16)
    total = receivers * META_ROWS
    row_at = lax.broadcasted_iota(jnp.int32, (total, 6 * heads), 0)
    column_at = lax.broadcasted_iota(jnp.int32, (total, 6 * heads), 1)
    receiver = (row_at // META_ROWS) % groups * CORES + row_at // (META_ROWS * groups)
    t = row_at % META_ROWS
    source = ((t // 6) * 3 + t % 3) * heads + 2 * receiver + (t // 3) % 2
    pick = jnp.where((t < 12) & (column_at == source), 1.0, 0.0).astype(bf16)
    meta = dot_n(pick, rows).astype(bf16)
    out_ref[:, :, 4 * PIECE : 4 * PIECE + META_ROWS, :] = meta.reshape(CORES, groups, META_ROWS, HEAD_SIZE)


def pack_queries(parity, queries, grads, rows, lse, groups, steps=4):
    width = queries.shape[1] // steps
    height = 4 * PIECE + META_ROWS
    return pl.pallas_call(
        pack_queries_kernel,
        grid=(steps,),
        in_specs=[pl.BlockSpec(memory_space=pltpu.SMEM)]
        + [pl.BlockSpec((PIECE, width), lambda i: (0, i))] * 3
        + [pl.BlockSpec((lse.shape[0] // steps, PIECE), lambda i: (i, 0))],
        out_specs=pl.BlockSpec((CORES, groups // steps, height, HEAD_SIZE), lambda i: (0, i, 0, 0)),
        out_shape=jax.ShapeDtypeStruct((CORES, groups, height, HEAD_SIZE), bf16),
        name="pack_queries",
    )(parity, queries, grads, rows, lse)


def sweep(causal, key_base, kv_ref, q_ref, lo_ref, meta_ref, dk_ref, dv_ref, dq_ref):
    pieces = TILE // PIECE
    tiles = LOOKBACK_SPAN // TILE

    meta = q_ref[:, 4 * PIECE : 4 * PIECE + META_ROWS, :].astype(f32)
    for p in range(LOOKBACK_SPAN // HEAD_SIZE):
        both = meta[2 * p] + meta[2 * p + 1]
        for r in range(4):
            one = both[3 * r : 3 * r + 1] + both[3 * r + 1 : 3 * r + 2] + both[3 * r + 2 : 3 * r + 3]
            meta_ref[p, r : r + 1, :] = one * log2_e if r < 2 else one

    dk_ref[...] = jnp.zeros_like(dk_ref)
    dv_ref[...] = jnp.zeros_like(dv_ref)

    def step(outer, inner):
        kt, qt = (inner, outer) if causal else (outer, inner)
        ks = kt * pieces
        qs = qt * pieces
        key = kv_ref[pl.ds(ks, pieces), 0:PIECE, :].reshape(TILE, HEAD_SIZE)
        value = kv_ref[pl.ds(ks, pieces), PIECE : 2 * PIECE, :].reshape(TILE, HEAD_SIZE)
        krows = pl.ds(pl.multiple_of(kt * TILE, TILE), TILE)
        qrows = pl.ds(pl.multiple_of(qt * TILE, TILE), TILE)
        key_at = lax.broadcasted_iota(jnp.int32, (TILE, TILE), 0)
        allowed = key_at >= lo_ref[qt] - (key_base + kt * TILE)
        if causal:
            query_at = lax.broadcasted_iota(jnp.int32, (TILE, TILE), 1)
            allowed = allowed & (key_at - query_at <= (qt - kt) * TILE)
        lanes = TILE // HEAD_SIZE
        dk = dk_ref[krows, :]
        dv = dv_ref[krows, :]
        for a in range(2):
            query = q_ref[pl.ds(qs, pieces), a * PIECE : (a + 1) * PIECE, :].reshape(TILE, HEAD_SIZE)
            grad = q_ref[pl.ds(qs, pieces), (2 + a) * PIECE : (3 + a) * PIECE, :].reshape(TILE, HEAD_SIZE)
            lse = jnp.concatenate([meta_ref[qt * lanes + i, a : a + 1, :] for i in range(lanes)], axis=1)
            delta = jnp.concatenate([meta_ref[qt * lanes + i, 2 + a : 3 + a, :] for i in range(lanes)], axis=1)
            scores = dot_t(key, query)
            prob = jnp.where(allowed, jnp.exp2(scores * (score_scale * log2_e) - lse), 0.0)
            prob_grad = dot_t(value, grad)
            score_grad = ((prob * score_scale) * (prob_grad - delta)).astype(bf16)
            dv = dv + dot_n(prob.astype(bf16), grad)
            dk = dk + dot_n(score_grad, query)
            dq_ref[a, qrows, :] = dq_ref[a, qrows, :] + t_dot(score_grad, key)
        dk_ref[krows, :] = dk
        dv_ref[krows, :] = dv

    for outer in range(tiles):
        lax.fori_loop(0, outer + 1, lambda inner, c, outer=outer: (step(outer, inner), c)[1], 0)


def cross_kernel(core_ref, kv_ref, q_ref, lo_ref, dq_ref, near_ref, far_ref, meta_ref, dk_ref, dv_ref):
    dq_ref[...] = jnp.zeros_like(dq_ref)
    sweep(False, 0, kv_ref, q_ref, lo_ref, meta_ref, dk_ref, dv_ref, dq_ref)
    half = LOOKBACK_SPAN // CORES
    near = pl.ds(pl.multiple_of(core_ref[0] * half, half), half)
    far = pl.ds(pl.multiple_of((1 - core_ref[0]) * half, half), half)
    near_ref[0] = dk_ref[near, :].astype(bf16)
    near_ref[1] = dv_ref[near, :].astype(bf16)
    far_ref[0] = dk_ref[far, :].astype(bf16)
    far_ref[1] = dv_ref[far, :].astype(bf16)


def own_kernel(kv_ref, q_ref, lo_ref, part_ref, out_ref, meta_ref, dk_ref, dv_ref, dq_ref):
    dq_ref[...] = part_ref[...]
    sweep(True, LOOKBACK_SPAN, kv_ref, q_ref, lo_ref, meta_ref, dk_ref, dv_ref, dq_ref)
    for core in range(CORES):
        block = slice(core * HALF, (core + 1) * HALF)
        out_ref[core, 0] = dq_ref[0, block, :].astype(bf16)
        out_ref[core, 1] = dq_ref[1, block, :].astype(bf16)
        out_ref[core, 2] = dk_ref[block, :].astype(bf16)
        out_ref[core, 3] = dv_ref[block, :].astype(bf16)


def vmem_spec():
    return pl.BlockSpec(memory_space=pltpu.VMEM)


def smem_spec():
    return pl.BlockSpec(memory_space=pltpu.SMEM)


SPAN_SCRATCH = [
    pltpu.VMEM((LOOKBACK_SPAN // HEAD_SIZE, 4, HEAD_SIZE), f32),
    pltpu.VMEM((LOOKBACK_SPAN, HEAD_SIZE), f32),
    pltpu.VMEM((LOOKBACK_SPAN, HEAD_SIZE), f32),
]
HALF = LOOKBACK_SPAN // CORES


def cost():
    pairs = LOOKBACK_SPAN * LOOKBACK_SPAN
    return pl.CostEstimate(flops=pairs * 5 * 2 * HEAD_SIZE, transcendentals=pairs, bytes_accessed=4 << 20)


def cross_terms(core, kv, q, lo):
    return pl.pallas_call(
        cross_kernel,
        in_specs=[smem_spec()] + [vmem_spec()] * 3,
        out_specs=[vmem_spec()] * 3,
        out_shape=[
            jax.ShapeDtypeStruct((2, LOOKBACK_SPAN, HEAD_SIZE), f32),
            jax.ShapeDtypeStruct((2, HALF, HEAD_SIZE), bf16),
            jax.ShapeDtypeStruct((2, HALF, HEAD_SIZE), bf16),
        ],
        scratch_shapes=SPAN_SCRATCH,
        compiler_params=pltpu.CompilerParams(vmem_limit_bytes=40 << 20),
        cost_estimate=cost(),
        name="cross_terms",
    )(core, kv, q, lo)


def own_terms(kv, q, lo, part):
    return pl.pallas_call(
        own_kernel,
        in_specs=[vmem_spec()] * 4,
        out_specs=vmem_spec(),
        out_shape=jax.ShapeDtypeStruct((CORES, 4, HALF, HEAD_SIZE), bf16),
        scratch_shapes=SPAN_SCRATCH + [pltpu.VMEM((2, LOOKBACK_SPAN, HEAD_SIZE), f32)],
        compiler_params=pltpu.CompilerParams(vmem_limit_bytes=40 << 20),
        cost_estimate=cost(),
        name="own_terms",
    )(kv, q, lo, part)


def join_kernel(core_ref, own_ref, near_ref, far_ref, dq_ref, dk_ref, dv_ref):
    for core in range(CORES):
        for a in range(2):
            at = 2 * core + a
            dq_ref[:, at * HEAD_SIZE : (at + 1) * HEAD_SIZE] = own_ref[core, a]

    for core in range(CORES):

        @pl.when(core_ref[0] == core)
        def _():
            for i, out_ref in enumerate((dk_ref, dv_ref)):
                for k in range(CORES):
                    back_ref = near_ref if k == core else far_ref
                    total = own_ref[k, 2 + i].astype(f32) + back_ref[i].astype(f32)
                    out_ref[:, k * HEAD_SIZE : (k + 1) * HEAD_SIZE] = total.astype(bf16)


def join(core, own, back_near, back_far):
    return pl.pallas_call(
        join_kernel,
        in_specs=[smem_spec()] + [vmem_spec()] * 3,
        out_specs=[vmem_spec()] * 3,
        out_shape=[
            jax.ShapeDtypeStruct((HALF, 4 * HEAD_SIZE), bf16),
            jax.ShapeDtypeStruct((HALF, 2 * HEAD_SIZE), bf16),
            jax.ShapeDtypeStruct((HALF, 2 * HEAD_SIZE), bf16),
        ],
        compiler_params=pltpu.CompilerParams(vmem_limit_bytes=16 << 20),
        name="join",
    )(core, own, back_near, back_far)


def first_allowed(doc_ids, chip):
    padded = jnp.concatenate([jnp.full((LOOKBACK_SPAN,), -1, jnp.int32), doc_ids])
    window = lax.dynamic_slice_in_dim(padded, chip * LOOKBACK_SPAN, 2 * LOOKBACK_SPAN, 0)
    own = window[LOOKBACK_SPAN:]
    document_start = jnp.sum((window[:, None] < own[None, :]).astype(jnp.int32), axis=0)
    reach_start = jnp.arange(1, LOOKBACK_SPAN + 1, dtype=jnp.int32)
    return jnp.maximum(document_start, reach_start).reshape(LOOKBACK_SPAN // TILE, 1, TILE)


def exchange(value):
    value = value.reshape((-1,) + value.shape[2:])
    return lax.all_to_all(value, ("core", "head"), split_axis=0, concat_axis=0, tiled=True)


def on_device(queries, keys, values, rows, grads, lse, doc_ids):
    chips = lax.axis_size("chip")
    groups = lax.axis_size("head")
    chip = lax.axis_index("chip")
    core = lax.axis_index("core").astype(jnp.int32).reshape(1)
    parity = (lax.axis_index("head") % 2).astype(jnp.int32).reshape(1)
    lo = first_allowed(doc_ids, chip)
    kv = exchange(pack_keys(keys, values, groups))
    packed = pack_queries(parity, queries, grads, rows, lse, groups)
    kv, packed = lax.optimization_barrier((kv, packed))
    q = exchange(packed)
    kv_before = lax.ppermute(kv, "chip", [(c, c + 1) for c in range(chips - 1)])
    dq_part, near, far = cross_terms(core, kv_before, q, lo)
    back_near = lax.ppermute(near, "chip", [(c + 1, c) for c in range(chips - 1)])
    back_far = lax.ppermute(
        far,
        ("chip", "core"),
        [(CORES * (c + 1) + k, CORES * c + 1 - k) for c in range(chips - 1) for k in range(CORES)],
    )
    own = own_terms(kv, q, lo, dq_part)
    own = lax.all_to_all(own, "core", split_axis=0, concat_axis=0, tiled=True)
    return join(core, own, back_near, back_far)


def solution(mesh):
    seq, head = mesh.devices.shape
    fine = Mesh(mesh.devices.reshape(seq // CORES, CORES, head), ("chip", "core", "head"))
    tokens = ("chip", "core", "head")
    return jax.shard_map(
        on_device,
        mesh=fine,
        in_specs=(P(tokens), P(tokens), P(tokens), P(tokens), P(tokens), P(None, tokens), P()),
        out_specs=(P(("chip", "core"), "head"),) * 3,
        check_vma=False,
    )
```

time: 164 us -> 94.5 us (0.58)
  starting transfers between devices: 59.2 us -> 30.6 us
  matrix products: 27.4 us -> 0 us
  local copies, waits for them, and re-layouts: 26.2 us -> 0.03 us
  Pallas kernels: 0 us -> 23.5 us
  other arithmetic: 9.1 us -> 0.99 us
  waiting for transfers between devices: 38.7 us -> 33.3 us
  blocking collectives: 0 us -> 4.51 us
    dot_general x15 -> x0, matrix products: 27.4 us -> none  [the longest x3 7.44 us: tile_terms(): jnp.einsum('rgad,cgd->garc', grad_four, value_three, preferred_element_ty...]
    pallas_call x0 -> x5, Pallas kernels: none -> 23.5 us  [the longest x1 8.1 us: own_terms(): pl.pallas_call(own_kernel, in_specs=[vmem_spec()] * 4, out_specs=vmem_spe...]
    all_to_all x6 -> x2, waiting for transfers between devices: 36.3 us -> 15.2 us  [exchange(): lax.all_to_all(value, ('core', 'head'), split_axis=0, concat_axis=0, tile...]
    ppermute x8 -> x3, starting transfers between devices: 35.1 us -> 17.2 us  [the longest x1 10.9 us: on_device(): lax.ppermute(near, 'chip', [(c + 1, c) for c in range(chips - 1)])]
    ppermute x8 -> x3, waiting for transfers between devices: 2.4 us -> 18.1 us  [the longest x1 18.1 us: on_device(): kv_before = lax.ppermute(kv, 'chip', [(c, c + 1) for c in range(chips - 1)])]
    reshape x13 -> x0, local copies, waits for them, and re-layouts: 12.4 us -> none  [the longest x3 5.36 us: tile_terms(): key_portion = jnp.einsum('plmw,mplo->wpo', score_gradient, query_four, pr...]
    all_to_all x6 -> x2, starting transfers between devices: 24.1 us -> 13.4 us  [exchange(): lax.all_to_all(value, ('core', 'head'), split_axis=0, concat_axis=0, tile...]
    unnamed x29 -> x2, local copies, waits for them, and re-layouts: 5.98 us -> 0.01 us
  transfers between devices with their start and end apart: 14 -> 5, of which waited for: 6 -> 3; matrix products, arithmetic and copies ran while one was open for 26% -> 1% of each run, Pallas kernels for 0% -> 13%
where the time goes in v1:
time: 94.5 us; the launch traced here: 93.6 us
  waiting for transfers between devices  33.3 us (35%)
  starting transfers between devices  30.6 us (32%)
  Pallas kernels  23.5 us (25%)
  blocking collectives  4.51 us (5%)
  other arithmetic  0.99 us (1%)
    ppermute x1, waiting for transfers between devices, on_device(): kv_before = lax.ppermute(kv, 'chip', [(c, c + 1) for c in range(chips - 1)])  18.1 us
    all_to_all x2, waiting for transfers between devices, exchange(): lax.all_to_all(value, ('core', 'head'), split_axis=0, concat_axis=0, tile...  15.2 us
    all_to_all x2, starting transfers between devices, exchange(): lax.all_to_all(value, ('core', 'head'), split_axis=0, concat_axis=0, tile...  13.4 us
    ppermute x1, starting transfers between devices, on_device(): lax.ppermute(near, 'chip', [(c + 1, c) for c in range(chips - 1)])  10.9 us
    pallas_call x1, Pallas kernels, own_terms(): pl.pallas_call(own_kernel, in_specs=[vmem_spec()] * 4, out_specs=vmem_spe...  8.1 us
    pallas_call x1, Pallas kernels, cross_terms(): pl.pallas_call(cross_kernel, in_specs=[smem_spec()] + [vmem_spec()] * 3,...  8 us
    all_to_all x1, blocking collectives, on_device(): own = lax.all_to_all(own, 'core', split_axis=0, concat_axis=0, tiled=True)  4.51 us
    pallas_call x1, Pallas kernels, pack_queries(): pl.pallas_call(pack_queries_kernel, grid=(steps,), in_specs=[pl.BlockSpec...  4.29 us
  transfers between devices with their start and end apart: 5, of which 3 were waited for; matrix products, arithmetic and copies ran while one was open for 1% of the time, Pallas kernels for 13%

profile of v1, /device:TPU:7, one launch (start us, length us, event | category | flops | bytes accessed | tf_op | source)
XLA Modules:
  0.0 93.6 jit_solution(3573512470286722942)
XLA Ops:
  0.6 1.9 %pack_keys.1 = bf16[2,8,128,128]{3,2,1,0:T(8,128)(2,1)} custom-call(bf16[64,2048]{1,0:T(8,128)(2,1)} %key_ref.1, bf16[64,2048]{1,0:T(8,128)(2,1)} %value_ref.1), custom_call_target="tpu_custom_call" | custom-call | tf_op jit(solution)/shard_map/pack_keys/pallas_call | solution.py:46
  2.5 7.8 %all-to-all-start = ((bf16[16,128,128]{2,1,0:T(8,128)(2,1)}), bf16[16,128,128]{2,1,0:T(8,128)(2,1)S(1)}, u32[]{:S(2)}, u32[]{:S(2)}) async-start(bf16[16,128,128]{2,1,0:T(8,128)(2,1)} %bitcast.6), calls=%async_computation | async-start | bytes 1048576 | tf_op jit(solution)/shard_map/all_to_all | solution.py:277
  10.3 4.3 %pack_queries.1 = bf16[2,8,272,128]{3,2,1,0:T(8,128)(2,1)} custom-call(s32[1]{0:T(128)} %bitcast.2.parity_ref, bf16[64,4096]{1,0:T(8,128)(2,1)} %query_ref.1, bf16[64,4096]{1,0:T(8,128)(2,1)} %grad_ref.1, bf16[64,4096]{1,0:T(8,128)(2,1)} %row_ref.1, f32[32,64]{1,0:T(8,128)} %lse_ref.1), custom_call_target="tpu_custom_call" | custom-call | tf_op jit(solution)/shard_map/pack_queries/pallas_call | solution.py:99
  14.6 10.5 %all-to-all-done.kv_ref = bf16[16,128,128]{2,1,0:T(8,128)(2,1)S(1)} async-done(((bf16[16,128,128]{2,1,0:T(8,128)(2,1)}), bf16[16,128,128]{2,1,0:T(8,128)(2,1)S(1)}, u32[]{:S(2)}, u32[]{:S(2)}) %all-to-all-start) | async-done | bytes 524320 | tf_op jit(solution)/shard_map/all_to_all | solution.py:277
  25.1 0.0 copy-start
  25.1 5.6 %all-to-all-start.1 = ((bf16[16,272,128]{2,1,0:T(8,128)(2,1)}), bf16[16,272,128]{2,1,0:T(8,128)(2,1)S(1)}, u32[]{:S(2)}, u32[]{:S(2)}) async-start(bf16[16,272,128]{2,1,0:T(8,128)(2,1)} %bitcast.5), calls=%async_computation.1 | async-start | bytes 2228224 | tf_op jit(solution)/shard_map/all_to_all | solution.py:277
  30.6 0.0 copy-done
  30.7 4.0 %collective-permute-start = (bf16[16,128,128]{2,1,0:T(8,128)(2,1)S(1)}, bf16[16,128,128]{2,1,0:T(8,128)(2,1)S(1)}, u32[]{:S(2)}, u32[]{:S(2)}) collective-permute-start(bf16[16,128,128]{2,1,0:T(8,128)(2,1)S(1)} %all-to-all-done.kv_ref), channel_id=1, source_target_pairs={{0,16},{16,32},{32,48},{48,64},{64,80},{80,96},{96,112},{112,128},... | collective-permute-start | bytes 1572872 | tf_op jit(solution)/shard_map/ppermute | solution.py:291
  34.7 1.0 %convert_reduce_fusion = s32[1024]{0:T(1024)S(1)} fusion(s32[1024]{0:T(1024)S(1)} %pad_dynamic-slice_fusion, s32[2048]{0:T(1024)S(1)} %pad_dynamic-slice_fusion.1), kind=kLoop, calls=%fused_computation | loop fusion | flops 6290432 | bytes 16384 | tf_op jit(solution)/shard_map/reduce_sum | solution.py:270
  35.7 18.1 %collective-permute-done.kv_ref = bf16[16,128,128]{2,1,0:T(8,128)(2,1)S(1)} collective-permute-done((bf16[16,128,128]{2,1,0:T(8,128)(2,1)S(1)}, bf16[16,128,128]{2,1,0:T(8,128)(2,1)S(1)}, u32[]{:S(2)}, u32[]{:S(2)}) %collective-permute-start) | collective-permute-done | bytes 524320 | tf_op jit(solution)/shard_map/ppermute | solution.py:291
  53.8 4.8 %all-to-all-done.1.q_ref = bf16[16,272,128]{2,1,0:T(8,128)(2,1)S(1)} async-done(((bf16[16,272,128]{2,1,0:T(8,128)(2,1)}), bf16[16,272,128]{2,1,0:T(8,128)(2,1)S(1)}, u32[]{:S(2)}, u32[]{:S(2)}) %all-to-all-start.1) | async-done | bytes 1114144 | tf_op jit(solution)/shard_map/all_to_all | solution.py:277
  58.5 8.0 %cross_terms.1 = (f32[2,1024,128]{2,1,0:T(8,128)S(1)}, bf16[2,512,128]{2,1,0:T(8,128)(2,1)S(1)}, bf16[2,512,128]{2,1,0:T(8,128)(2,1)S(1)}) custom-call(s32[1]{0:T(128)} %bitcast.core_ref, bf16[16,128,128]{2,1,0:T(8,128)(2,1)S(1)} %collective-permute-done.kv_ref, bf16[16,272,128]{2,1,0:T(8,128)(2,1)S(1)} %all-to-all-done.1.q_ref, ...), custom_call_target="tpu_custom_call" | custom-call | flops 1342177280 | bytes 4194304 | tf_op jit(solution)/shard_map/cross_terms/pallas_call | solution.py:205
  66.6 10.9 %collective-permute-start.1 = (bf16[2,512,128]{2,1,0:T(8,128)(2,1)S(1)}, bf16[2,512,128]{2,1,0:T(8,128)(2,1)S(1)}, u32[]{:S(2)}, u32[]{:S(2)}) collective-permute-start(bf16[2,512,128]{2,1,0:T(8,128)(2,1)S(1)} %get-tuple-element.11), channel_id=1, source_target_pairs={{16,0},{32,16},{48,32},{64,48},{80,64},{96,80},{112,96},{128,112},... | collective-permute-start | bytes 786440 | tf_op jit(solution)/shard_map/ppermute | solution.py:293
  77.5 2.3 %collective-permute-start.2 = (bf16[2,512,128]{2,1,0:T(8,128)(2,1)S(1)}, bf16[2,512,128]{2,1,0:T(8,128)(2,1)S(1)}, u32[]{:S(2)}, u32[]{:S(2)}) collective-permute-start(bf16[2,512,128]{2,1,0:T(8,128)(2,1)S(1)} %get-tuple-element.12), channel_id=1, source_target_pairs={{16,8},{24,0},{32,24},{40,16},{48,40},{56,32},{64,56},{72,48},{80,... | collective-permute-start | bytes 786440 | tf_op jit(solution)/shard_map/ppermute | solution.py:294
  79.8 8.1 %own_terms.1 = bf16[2,4,512,128]{3,2,1,0:T(8,128)(2,1)S(1)} custom-call(bf16[16,128,128]{2,1,0:T(8,128)(2,1)S(1)} %all-to-all-done.kv_ref, bf16[16,272,128]{2,1,0:T(8,128)(2,1)S(1)} %all-to-all-done.1.q_ref, s32[4,1,256]{2,1,0:T(1,128)S(1)} %add_maximum_fusion.lo_ref, f32[2,1024,128]{2,1,0:T(8,128)S(1)} %get-tuple-element.10.part_ref), custom_call_target="tpu_custom_call" | custom-call | flops 1342177280 | bytes 4194304 | tf_op jit(solution)/shard_map/own_terms/pallas_call | solution.py:222
  87.9 4.5 %all_to_all.15.own_ref = bf16[2,4,512,128]{3,2,1,0:T(8,128)(2,1)S(1)} all-to-all(bf16[2,4,512,128]{3,2,1,0:T(8,128)(2,1)S(1)} %own_terms.1), channel_id=1, replica_groups=mesh['chip'=32,'core'=2,'head'=8] {'core'}, dimensions={0} | all-to-all | bytes 2097152 | tf_op jit(solution)/shard_map/all_to_all | solution.py:300
  92.4 0.0 collective-permute-done.1.near_ref
  92.4 0.0 collective-permute-done.2.far_ref
  92.4 1.2 %join.1 = (bf16[512,512]{1,0:T(8,128)(2,1)}, bf16[512,256]{1,0:T(8,128)(2,1)}, bf16[512,256]{1,0:T(8,128)(2,1)}) custom-call(s32[1]{0:T(128)} %bitcast.core_ref, bf16[2,4,512,128]{3,2,1,0:T(8,128)(2,1)S(1)} %all_to_all.15.own_ref, bf16[2,512,128]{2,1,0:T(8,128)(2,1)S(1)} %collective-permute-done.1.near_ref, ...), custom_call_target="tpu_custom_call" | custom-call | tf_op jit(solution)/shard_map/join/pallas_call | solution.py:252
  (3 shorter events, 0.0 us)
Async XLA Ops:
  2.5 22.6 %all-to-all-start = ((bf16[16,128,128]{2,1,0:T(8,128)(2,1)}), bf16[16,128,128]{2,1,0:T(8,128)(2,1)S(1)}, u32[]{:S(2)}, u32[]{:S(2)}) async-start(bf16[16,128,128]{2,1,0:T(8,128)(2,1)} %bitcast.6), calls=%async_computation | async-start | bytes 1048576 | tf_op jit(solution)/shard_map/all_to_all | solution.py:277
  25.1 5.6 %copy-start = (s32[32768]{0:T(1024)S(1)}, s32[32768]{0:T(1024)}, u32[]{:S(2)}) copy-start(s32[32768]{0:T(1024)} %param.13) | copy-start | bytes 393220
  25.1 33.5 %all-to-all-start.1 = ((bf16[16,272,128]{2,1,0:T(8,128)(2,1)}), bf16[16,272,128]{2,1,0:T(8,128)(2,1)S(1)}, u32[]{:S(2)}, u32[]{:S(2)}) async-start(bf16[16,272,128]{2,1,0:T(8,128)(2,1)} %bitcast.5), calls=%async_computation.1 | async-start | bytes 2228224 | tf_op jit(solution)/shard_map/all_to_all | solution.py:277
  30.7 23.1 %collective-permute-start = (bf16[16,128,128]{2,1,0:T(8,128)(2,1)S(1)}, bf16[16,128,128]{2,1,0:T(8,128)(2,1)S(1)}, u32[]{:S(2)}, u32[]{:S(2)}) collective-permute-start(bf16[16,128,128]{2,1,0:T(8,128)(2,1)S(1)} %all-to-all-done.kv_ref), channel_id=1, source_target_pairs={{0,16},{16,32},{32,48},{48,64},{64,80},{80,96},{96,112},{112,128},... | collective-permute-start | bytes 1572872 | tf_op jit(solution)/shard_map/ppermute | solution.py:291
  66.6 25.8 %collective-permute-start.1 = (bf16[2,512,128]{2,1,0:T(8,128)(2,1)S(1)}, bf16[2,512,128]{2,1,0:T(8,128)(2,1)S(1)}, u32[]{:S(2)}, u32[]{:S(2)}) collective-permute-start(bf16[2,512,128]{2,1,0:T(8,128)(2,1)S(1)} %get-tuple-element.11), channel_id=1, source_target_pairs={{16,0},{32,16},{48,32},{64,48},{80,64},{96,80},{112,96},{128,112},... | collective-permute-start | bytes 786440 | tf_op jit(solution)/shard_map/ppermute | solution.py:293
  77.5 14.9 %collective-permute-start.2 = (bf16[2,512,128]{2,1,0:T(8,128)(2,1)S(1)}, bf16[2,512,128]{2,1,0:T(8,128)(2,1)S(1)}, u32[]{:S(2)}, u32[]{:S(2)}) collective-permute-start(bf16[2,512,128]{2,1,0:T(8,128)(2,1)S(1)} %get-tuple-element.12), channel_id=1, source_target_pairs={{16,8},{24,0},{32,24},{40,16},{48,40},{56,32},{64,56},{72,48},{80,... | collective-permute-start | bytes 786440 | tf_op jit(solution)/shard_map/ppermute | solution.py:294

commit v2 on v1

--- a/solution.py
+++ b/solution.py
@@ -13,7 +13,7 @@
 CORES = 2
 PIECE = 64
 META_ROWS = 16
-TILE = 256
+CHUNK = 128
 
 score_scale = 168.0 ** (-0.5)
 log2_e = math.log2(math.e)
@@ -108,58 +108,60 @@
     )(parity, queries, grads, rows, lse)
 
 
-def sweep(causal, key_base, kv_ref, q_ref, lo_ref, meta_ref, dk_ref, dv_ref, dq_ref):
-    pieces = TILE // PIECE
-    tiles = LOOKBACK_SPAN // TILE
-
-    meta = q_ref[:, 4 * PIECE : 4 * PIECE + META_ROWS, :].astype(f32)
-    for p in range(LOOKBACK_SPAN // HEAD_SIZE):
-        both = meta[2 * p] + meta[2 * p + 1]
-        for r in range(4):
-            one = both[3 * r : 3 * r + 1] + both[3 * r + 1 : 3 * r + 2] + both[3 * r + 2 : 3 * r + 3]
-            meta_ref[p, r : r + 1, :] = one * log2_e if r < 2 else one
-
-    dk_ref[...] = jnp.zeros_like(dk_ref)
-    dv_ref[...] = jnp.zeros_like(dv_ref)
-
-    def step(outer, inner):
-        kt, qt = (inner, outer) if causal else (outer, inner)
-        ks = kt * pieces
-        qs = qt * pieces
-        key = kv_ref[pl.ds(ks, pieces), 0:PIECE, :].reshape(TILE, HEAD_SIZE)
-        value = kv_ref[pl.ds(ks, pieces), PIECE : 2 * PIECE, :].reshape(TILE, HEAD_SIZE)
-        krows = pl.ds(pl.multiple_of(kt * TILE, TILE), TILE)
-        qrows = pl.ds(pl.multiple_of(qt * TILE, TILE), TILE)
-        key_at = lax.broadcasted_iota(jnp.int32, (TILE, TILE), 0)
-        allowed = key_at >= lo_ref[qt] - (key_base + kt * TILE)
+def sweep(causal, key_base, kv_ref, q_ref, lo_ref, dk_ref, dv_ref, dq_ref, part_ref):
+    pieces = CHUNK // PIECE
+    chunks = LOOKBACK_SPAN // CHUNK
+    order = range(chunks - 1, -1, -1) if causal else range(chunks)
+    for n, at in enumerate(order):
+        first, last = (0, at + 1) if causal else (at, chunks)
+        strip = slice(first * CHUNK, last * CHUNK)
+        height = (last - first) * CHUNK
+        sources = slice(first * pieces, last * pieces)
+        key = kv_ref[sources, 0:PIECE, :].reshape(height, HEAD_SIZE)
+        value = kv_ref[sources, PIECE : 2 * PIECE, :].reshape(height, HEAD_SIZE)
+        sources = slice(at * pieces, (at + 1) * pieces)
+
+        def both(row):
+            return jnp.concatenate(
+                [q_ref[sources, (row + a) * PIECE : (row + a + 1) * PIECE, :].reshape(CHUNK, HEAD_SIZE) for a in range(2)]
+            )
+
+        query = both(0)
+        grad = both(2)
+        meta = q_ref[sources, 4 * PIECE : 4 * PIECE + META_ROWS, :].astype(f32)
+        meta = meta[0] + meta[1]
+        rows = [meta[3 * r : 3 * r + 1] + meta[3 * r + 1 : 3 * r + 2] + meta[3 * r + 2 : 3 * r + 3] for r in range(4)]
+        lse = jnp.concatenate(rows[0:2], axis=1) * log2_e
+        delta = jnp.concatenate(rows[2:4], axis=1)
+        lo = lo_ref[at] - (key_base + first * CHUNK)
+        lo = jnp.concatenate([lo, lo], axis=1)
+        key_at = lax.broadcasted_iota(jnp.int32, (height, 2 * CHUNK), 0)
+        allowed = key_at >= lo
         if causal:
-            query_at = lax.broadcasted_iota(jnp.int32, (TILE, TILE), 1)
-            allowed = allowed & (key_at - query_at <= (qt - kt) * TILE)
-        lanes = TILE // HEAD_SIZE
-        dk = dk_ref[krows, :]
-        dv = dv_ref[krows, :]
+            query_at = lax.broadcasted_iota(jnp.int32, (1, 2 * CHUNK), 1) % CHUNK + at * CHUNK
+            allowed = allowed & (key_at <= query_at)
+        scores = dot_t(key, query)
+        prob = jnp.where(allowed, jnp.exp2(scores * (score_scale * log2_e) - lse), 0.0)
+        prob_grad = dot_t(value, grad)
+        score_grad = ((prob * score_scale) * (prob_grad - delta)).astype(bf16)
+        dv = dot_n(prob.astype(bf16), grad)
+        dk = dot_n(score_grad, query)
+        if n == 0:
+            dv_ref[strip, :] = dv
+            dk_ref[strip, :] = dk
+        else:
+            dv_ref[strip, :] += dv
+            dk_ref[strip, :] += dk
+        dq = t_dot(score_grad, key)
         for a in range(2):
-            query = q_ref[pl.ds(qs, pieces), a * PIECE : (a + 1) * PIECE, :].reshape(TILE, HEAD_SIZE)
-            grad = q_ref[pl.ds(qs, pieces), (2 + a) * PIECE : (3 + a) * PIECE, :].reshape(TILE, HEAD_SIZE)
-            lse = jnp.concatenate([meta_ref[qt * lanes + i, a : a + 1, :] for i in range(lanes)], axis=1)
-            delta = jnp.concatenate([meta_ref[qt * lanes + i, 2 + a : 3 + a, :] for i in range(lanes)], axis=1)
-            scores = dot_t(key, query)
-            prob = jnp.where(allowed, jnp.exp2(scores * (score_scale * log2_e) - lse), 0.0)
-            prob_grad = dot_t(value, grad)
-            score_grad = ((prob * score_scale) * (prob_grad - delta)).astype(bf16)
-            dv = dv + dot_n(prob.astype(bf16), grad)
-            dk = dk + dot_n(score_grad, query)
-            dq_ref[a, qrows, :] = dq_ref[a, qrows, :] + t_dot(score_grad, key)
-        dk_ref[krows, :] = dk
-        dv_ref[krows, :] = dv
-
-    for outer in range(tiles):
-        lax.fori_loop(0, outer + 1, lambda inner, c, outer=outer: (step(outer, inner), c)[1], 0)
-
-
-def cross_kernel(core_ref, kv_ref, q_ref, lo_ref, dq_ref, near_ref, far_ref, meta_ref, dk_ref, dv_ref):
-    dq_ref[...] = jnp.zeros_like(dq_ref)
-    sweep(False, 0, kv_ref, q_ref, lo_ref, meta_ref, dk_ref, dv_ref, dq_ref)
+            mine = dq[a * CHUNK : (a + 1) * CHUNK]
+            if part_ref is not None:
+                mine = mine + part_ref[a, at * CHUNK : (at + 1) * CHUNK, :]
+            dq_ref[a, at * CHUNK : (at + 1) * CHUNK, :] = mine
+
+
+def cross_kernel(core_ref, kv_ref, q_ref, lo_ref, dq_ref, near_ref, far_ref, dk_ref, dv_ref):
+    sweep(False, 0, kv_ref, q_ref, lo_ref, dk_ref, dv_ref, dq_ref, None)
     half = LOOKBACK_SPAN // CORES
     near = pl.ds(pl.multiple_of(core_ref[0] * half, half), half)
     far = pl.ds(pl.multiple_of((1 - core_ref[0]) * half, half), half)
@@ -169,9 +171,8 @@
     far_ref[1] = dv_ref[far, :].astype(bf16)
 
 
-def own_kernel(kv_ref, q_ref, lo_ref, part_ref, out_ref, meta_ref, dk_ref, dv_ref, dq_ref):
-    dq_ref[...] = part_ref[...]
-    sweep(True, LOOKBACK_SPAN, kv_ref, q_ref, lo_ref, meta_ref, dk_ref, dv_ref, dq_ref)
+def own_kernel(kv_ref, q_ref, lo_ref, part_ref, out_ref, dk_ref, dv_ref, dq_ref):
+    sweep(True, LOOKBACK_SPAN, kv_ref, q_ref, lo_ref, dk_ref, dv_ref, dq_ref, part_ref)
     for core in range(CORES):
         block = slice(core * HALF, (core + 1) * HALF)
         out_ref[core, 0] = dq_ref[0, block, :].astype(bf16)
@@ -189,7 +190,6 @@
 
 
 SPAN_SCRATCH = [
-    pltpu.VMEM((LOOKBACK_SPAN // HEAD_SIZE, 4, HEAD_SIZE), f32),
     pltpu.VMEM((LOOKBACK_SPAN, HEAD_SIZE), f32),
     pltpu.VMEM((LOOKBACK_SPAN, HEAD_SIZE), f32),
 ]
@@ -269,7 +269,7 @@
     own = window[LOOKBACK_SPAN:]
     document_start = jnp.sum((window[:, None] < own[None, :]).astype(jnp.int32), axis=0)
     reach_start = jnp.arange(1, LOOKBACK_SPAN + 1, dtype=jnp.int32)
-    return jnp.maximum(document_start, reach_start).reshape(LOOKBACK_SPAN // TILE, 1, TILE)
+    return jnp.maximum(document_start, reach_start).reshape(LOOKBACK_SPAN // CHUNK, 1, CHUNK)
 
 
 def exchange(value):

time: 94.5 us -> 86.4 us (0.914)
  Pallas kernels: 23.5 us -> 15 us
    pallas_call x1, Pallas kernels: 8.1 us -> 3.85 us  [own_terms(): pl.pallas_call(own_kernel, in_specs=[vmem_spec()] * 4, out_specs=vmem_spe...]
    pallas_call x1, Pallas kernels: 8 us -> 3.76 us  [cross_terms(): pl.pallas_call(cross_kernel, in_specs=[smem_spec()] + [vmem_spec()] * 3,...]
  transfers between devices with their start and end apart: 5 -> 5, of which waited for: 3 -> 4; matrix products, arithmetic and copies ran while one was open for 1% -> 1% of each run, Pallas kernels for 13% -> 9%
where the time goes in v2:
time: 86.4 us; the launch traced here: 85.9 us
  waiting for transfers between devices  34.1 us (39%)
  starting transfers between devices  30.6 us (35%)
  Pallas kernels  15 us (17%)
  blocking collectives  4.5 us (5%)
  other arithmetic  0.99 us (1%)
    ppermute x1, waiting for transfers between devices, on_device(): kv_before = lax.ppermute(kv, 'chip', [(c, c + 1) for c in range(chips - 1)])  18.1 us
    all_to_all x2, waiting for transfers between devices, exchange(): lax.all_to_all(value, ('core', 'head'), split_axis=0, concat_axis=0, tile...  15.2 us
    all_to_all x2, starting transfers between devices, exchange(): lax.all_to_all(value, ('core', 'head'), split_axis=0, concat_axis=0, tile...  13.4 us
    ppermute x1, starting transfers between devices, on_device(): lax.ppermute(near, 'chip', [(c + 1, c) for c in range(chips - 1)])  10.9 us
    all_to_all x1, blocking collectives, on_device(): own = lax.all_to_all(own, 'core', split_axis=0, concat_axis=0, tiled=True)  4.5 us
    pallas_call x1, Pallas kernels, pack_queries(): pl.pallas_call(pack_queries_kernel, grid=(steps,), in_specs=[pl.BlockSpec...  4.29 us
    ppermute x1, starting transfers between devices, on_device(): kv_before = lax.ppermute(kv, 'chip', [(c, c + 1) for c in range(chips - 1)])  4.03 us
    pallas_call x1, Pallas kernels, own_terms(): pl.pallas_call(own_kernel, in_specs=[vmem_spec()] * 4, out_specs=vmem_spe...  3.85 us
  transfers between devices with their start and end apart: 5, of which 4 were waited for; matrix products, arithmetic and copies ran while one was open for 1% of the time, Pallas kernels for 9%

profile of v2, /device:TPU:7, one launch (start us, length us, event | category | flops | bytes accessed | tf_op | source)
XLA Modules:
  0.0 85.9 jit_solution(16587234969754324234)
XLA Ops:
  0.6 1.9 %pack_keys.1 = bf16[2,8,128,128]{3,2,1,0:T(8,128)(2,1)} custom-call(bf16[64,2048]{1,0:T(8,128)(2,1)} %key_ref.1, bf16[64,2048]{1,0:T(8,128)(2,1)} %value_ref.1), custom_call_target="tpu_custom_call" | custom-call | tf_op jit(solution)/shard_map/pack_keys/pallas_call | solution.py:46
  2.5 7.8 %all-to-all-start = ((bf16[16,128,128]{2,1,0:T(8,128)(2,1)}), bf16[16,128,128]{2,1,0:T(8,128)(2,1)S(1)}, u32[]{:S(2)}, u32[]{:S(2)}) async-start(bf16[16,128,128]{2,1,0:T(8,128)(2,1)} %bitcast.6), calls=%async_computation | async-start | bytes 1048576 | tf_op jit(solution)/shard_map/all_to_all | solution.py:277
  10.3 4.3 %pack_queries.1 = bf16[2,8,272,128]{3,2,1,0:T(8,128)(2,1)} custom-call(s32[1]{0:T(128)} %bitcast.2.parity_ref, bf16[64,4096]{1,0:T(8,128)(2,1)} %query_ref.1, bf16[64,4096]{1,0:T(8,128)(2,1)} %grad_ref.1, bf16[64,4096]{1,0:T(8,128)(2,1)} %row_ref.1, f32[32,64]{1,0:T(8,128)} %lse_ref.1), custom_call_target="tpu_custom_call" | custom-call | tf_op jit(solution)/shard_map/pack_queries/pallas_call | solution.py:99
  14.6 10.5 %all-to-all-done.kv_ref = bf16[16,128,128]{2,1,0:T(8,128)(2,1)S(1)} async-done(((bf16[16,128,128]{2,1,0:T(8,128)(2,1)}), bf16[16,128,128]{2,1,0:T(8,128)(2,1)S(1)}, u32[]{:S(2)}, u32[]{:S(2)}) %all-to-all-start) | async-done | bytes 524320 | tf_op jit(solution)/shard_map/all_to_all | solution.py:277
  25.1 0.0 copy-start
  25.1 5.6 %all-to-all-start.1 = ((bf16[16,272,128]{2,1,0:T(8,128)(2,1)}), bf16[16,272,128]{2,1,0:T(8,128)(2,1)S(1)}, u32[]{:S(2)}, u32[]{:S(2)}) async-start(bf16[16,272,128]{2,1,0:T(8,128)(2,1)} %bitcast.5), calls=%async_computation.1 | async-start | bytes 2228224 | tf_op jit(solution)/shard_map/all_to_all | solution.py:277
  30.6 0.0 copy-done
  30.7 4.0 %collective-permute-start = (bf16[16,128,128]{2,1,0:T(8,128)(2,1)S(1)}, bf16[16,128,128]{2,1,0:T(8,128)(2,1)S(1)}, u32[]{:S(2)}, u32[]{:S(2)}) collective-permute-start(bf16[16,128,128]{2,1,0:T(8,128)(2,1)S(1)} %all-to-all-done.kv_ref), channel_id=1, source_target_pairs={{0,16},{16,32},{32,48},{48,64},{64,80},{80,96},{96,112},{112,128},... | collective-permute-start | bytes 1572872 | tf_op jit(solution)/shard_map/ppermute | solution.py:291
  34.7 1.0 %convert_reduce_fusion = s32[1024]{0:T(1024)S(1)} fusion(s32[1024]{0:T(1024)S(1)} %pad_dynamic-slice_fusion, s32[2048]{0:T(1024)S(1)} %pad_dynamic-slice_fusion.1), kind=kLoop, calls=%fused_computation | loop fusion | flops 6290432 | bytes 16384 | tf_op jit(solution)/shard_map/reduce_sum | solution.py:270
  35.7 18.1 %collective-permute-done.kv_ref = bf16[16,128,128]{2,1,0:T(8,128)(2,1)S(1)} collective-permute-done((bf16[16,128,128]{2,1,0:T(8,128)(2,1)S(1)}, bf16[16,128,128]{2,1,0:T(8,128)(2,1)S(1)}, u32[]{:S(2)}, u32[]{:S(2)}) %collective-permute-start) | collective-permute-done | bytes 524320 | tf_op jit(solution)/shard_map/ppermute | solution.py:291
  53.8 4.8 %all-to-all-done.1.q_ref = bf16[16,272,128]{2,1,0:T(8,128)(2,1)S(1)} async-done(((bf16[16,272,128]{2,1,0:T(8,128)(2,1)}), bf16[16,272,128]{2,1,0:T(8,128)(2,1)S(1)}, u32[]{:S(2)}, u32[]{:S(2)}) %all-to-all-start.1) | async-done | bytes 1114144 | tf_op jit(solution)/shard_map/all_to_all | solution.py:277
  58.5 3.8 %cross_terms.1 = (f32[2,1024,128]{2,1,0:T(8,128)S(1)}, bf16[2,512,128]{2,1,0:T(8,128)(2,1)S(1)}, bf16[2,512,128]{2,1,0:T(8,128)(2,1)S(1)}) custom-call(s32[1]{0:T(128)} %bitcast.core_ref, bf16[16,128,128]{2,1,0:T(8,128)(2,1)S(1)} %collective-permute-done.kv_ref, bf16[16,272,128]{2,1,0:T(8,128)(2,1)S(1)} %all-to-all-done.1.q_ref, ...), custom_call_target="tpu_custom_call" | custom-call | flops 1342177280 | bytes 4194304 | tf_op jit(solution)/shard_map/cross_terms/pallas_call | solution.py:205
  62.3 10.9 %collective-permute-start.1 = (bf16[2,512,128]{2,1,0:T(8,128)(2,1)S(1)}, bf16[2,512,128]{2,1,0:T(8,128)(2,1)S(1)}, u32[]{:S(2)}, u32[]{:S(2)}) collective-permute-start(bf16[2,512,128]{2,1,0:T(8,128)(2,1)S(1)} %get-tuple-element.11), channel_id=1, source_target_pairs={{16,0},{32,16},{48,32},{64,48},{80,64},{96,80},{112,96},{128,112},... | collective-permute-start | bytes 786440 | tf_op jit(solution)/shard_map/ppermute | solution.py:293
  73.2 2.3 %collective-permute-start.2 = (bf16[2,512,128]{2,1,0:T(8,128)(2,1)S(1)}, bf16[2,512,128]{2,1,0:T(8,128)(2,1)S(1)}, u32[]{:S(2)}, u32[]{:S(2)}) collective-permute-start(bf16[2,512,128]{2,1,0:T(8,128)(2,1)S(1)} %get-tuple-element.12), channel_id=1, source_target_pairs={{16,8},{24,0},{32,24},{40,16},{48,40},{56,32},{64,56},{72,48},{80,... | collective-permute-start | bytes 786440 | tf_op jit(solution)/shard_map/ppermute | solution.py:294
  75.5 3.9 %own_terms.1 = bf16[2,4,512,128]{3,2,1,0:T(8,128)(2,1)S(1)} custom-call(bf16[16,128,128]{2,1,0:T(8,128)(2,1)S(1)} %all-to-all-done.kv_ref, bf16[16,272,128]{2,1,0:T(8,128)(2,1)S(1)} %all-to-all-done.1.q_ref, s32[8,1,128]{2,1,0:T(1,128)S(1)} %add_maximum_fusion.lo_ref, f32[2,1024,128]{2,1,0:T(8,128)S(1)} %get-tuple-element.10.part_ref), custom_call_target="tpu_custom_call" | custom-call | flops 1342177280 | bytes 4194304 | tf_op jit(solution)/shard_map/own_terms/pallas_call | solution.py:222
  79.4 4.5 %all_to_all.15.own_ref = bf16[2,4,512,128]{3,2,1,0:T(8,128)(2,1)S(1)} all-to-all(bf16[2,4,512,128]{3,2,1,0:T(8,128)(2,1)S(1)} %own_terms.1), channel_id=1, replica_groups=mesh['chip'=32,'core'=2,'head'=8] {'core'}, dimensions={0} | all-to-all | bytes 2097152 | tf_op jit(solution)/shard_map/all_to_all | solution.py:300
  83.9 0.0 collective-permute-done.1.near_ref
  83.9 0.8 collective-permute-done.2.far_ref
  84.7 1.2 %join.1 = (bf16[512,512]{1,0:T(8,128)(2,1)}, bf16[512,256]{1,0:T(8,128)(2,1)}, bf16[512,256]{1,0:T(8,128)(2,1)}) custom-call(s32[1]{0:T(128)} %bitcast.core_ref, bf16[2,4,512,128]{3,2,1,0:T(8,128)(2,1)S(1)} %all_to_all.15.own_ref, bf16[2,512,128]{2,1,0:T(8,128)(2,1)S(1)} %collective-permute-done.1.near_ref, ...), custom_call_target="tpu_custom_call" | custom-call | tf_op jit(solution)/shard_map/join/pallas_call | solution.py:252
  (3 shorter events, 0.0 us)
Async XLA Ops:
  2.5 22.6 %all-to-all-start = ((bf16[16,128,128]{2,1,0:T(8,128)(2,1)}), bf16[16,128,128]{2,1,0:T(8,128)(2,1)S(1)}, u32[]{:S(2)}, u32[]{:S(2)}) async-start(bf16[16,128,128]{2,1,0:T(8,128)(2,1)} %bitcast.6), calls=%async_computation | async-start | bytes 1048576 | tf_op jit(solution)/shard_map/all_to_all | solution.py:277
  25.1 5.6 %copy-start = (s32[32768]{0:T(1024)S(1)}, s32[32768]{0:T(1024)}, u32[]{:S(2)}) copy-start(s32[32768]{0:T(1024)} %param.13) | copy-start | bytes 393220
  25.1 33.5 %all-to-all-start.1 = ((bf16[16,272,128]{2,1,0:T(8,128)(2,1)}), bf16[16,272,128]{2,1,0:T(8,128)(2,1)S(1)}, u32[]{:S(2)}, u32[]{:S(2)}) async-start(bf16[16,272,128]{2,1,0:T(8,128)(2,1)} %bitcast.5), calls=%async_computation.1 | async-start | bytes 2228224 | tf_op jit(solution)/shard_map/all_to_all | solution.py:277
  30.7 23.1 %collective-permute-start = (bf16[16,128,128]{2,1,0:T(8,128)(2,1)S(1)}, bf16[16,128,128]{2,1,0:T(8,128)(2,1)S(1)}, u32[]{:S(2)}, u32[]{:S(2)}) collective-permute-start(bf16[16,128,128]{2,1,0:T(8,128)(2,1)S(1)} %all-to-all-done.kv_ref), channel_id=1, source_target_pairs={{0,16},{16,32},{32,48},{48,64},{64,80},{80,96},{96,112},{112,128},... | collective-permute-start | bytes 1572872 | tf_op jit(solution)/shard_map/ppermute | solution.py:291
  62.3 21.6 %collective-permute-start.1 = (bf16[2,512,128]{2,1,0:T(8,128)(2,1)S(1)}, bf16[2,512,128]{2,1,0:T(8,128)(2,1)S(1)}, u32[]{:S(2)}, u32[]{:S(2)}) collective-permute-start(bf16[2,512,128]{2,1,0:T(8,128)(2,1)S(1)} %get-tuple-element.11), channel_id=1, source_target_pairs={{16,0},{32,16},{48,32},{64,48},{80,64},{96,80},{112,96},{128,112},... | collective-permute-start | bytes 786440 | tf_op jit(solution)/shard_map/ppermute | solution.py:293
  73.2 11.4 %collective-permute-start.2 = (bf16[2,512,128]{2,1,0:T(8,128)(2,1)S(1)}, bf16[2,512,128]{2,1,0:T(8,128)(2,1)S(1)}, u32[]{:S(2)}, u32[]{:S(2)}) collective-permute-start(bf16[2,512,128]{2,1,0:T(8,128)(2,1)S(1)} %get-tuple-element.12), channel_id=1, source_target_pairs={{16,8},{24,0},{32,24},{40,16},{48,40},{56,32},{64,56},{72,48},{80,... | collective-permute-start | bytes 786440 | tf_op jit(solution)/shard_map/ppermute | solution.py:294

commit v3 on v2

--- a/solution.py
+++ b/solution.py
@@ -1,3 +1,4 @@
+import functools
 import math
 
 import jax
@@ -108,13 +109,11 @@
     )(parity, queries, grads, rows, lse)
 
 
-def sweep(causal, key_base, kv_ref, q_ref, lo_ref, dk_ref, dv_ref, dq_ref, part_ref):
+def sweep(strips, causal, key_base, kv_ref, q_ref, lo_ref, dk_ref, dv_ref, dq_ref, part_ref):
     pieces = CHUNK // PIECE
-    chunks = LOOKBACK_SPAN // CHUNK
-    order = range(chunks - 1, -1, -1) if causal else range(chunks)
-    for n, at in enumerate(order):
-        first, last = (0, at + 1) if causal else (at, chunks)
-        strip = slice(first * CHUNK, last * CHUNK)
+    base = strips[0][1]
+    for n, (at, first, last) in enumerate(strips):
+        strip = slice((first - base) * CHUNK, (last - base) * CHUNK)
         height = (last - first) * CHUNK
         sources = slice(first * pieces, last * pieces)
         key = kv_ref[sources, 0:PIECE, :].reshape(height, HEAD_SIZE)
@@ -160,19 +159,32 @@
             dq_ref[a, at * CHUNK : (at + 1) * CHUNK, :] = mine
 
 
-def cross_kernel(core_ref, kv_ref, q_ref, lo_ref, dq_ref, near_ref, far_ref, dk_ref, dv_ref):
-    sweep(False, 0, kv_ref, q_ref, lo_ref, dk_ref, dv_ref, dq_ref, None)
-    half = LOOKBACK_SPAN // CORES
-    near = pl.ds(pl.multiple_of(core_ref[0] * half, half), half)
-    far = pl.ds(pl.multiple_of((1 - core_ref[0]) * half, half), half)
-    near_ref[0] = dk_ref[near, :].astype(bf16)
-    near_ref[1] = dv_ref[near, :].astype(bf16)
-    far_ref[0] = dk_ref[far, :].astype(bf16)
-    far_ref[1] = dv_ref[far, :].astype(bf16)
+def cross_kernel(near, core_ref, kv_ref, q_ref, lo_ref, *refs):
+    part_ref = None if near else refs[0]
+    dq_ref, out_ref, dk_ref, dv_ref = refs[-4:]
+    chunks = LOOKBACK_SPAN // CHUNK
+    for block in range(CORES):
+
+        @pl.when(core_ref[0] == (block if near else 1 - block))
+        def _():
+            start, end = block * chunks // CORES, (block + 1) * chunks // CORES
+            sweep(
+                [(at, max(at, start), end) for at in range(end)],
+                False, 0, kv_ref, q_ref, lo_ref, dk_ref, dv_ref, dq_ref, part_ref,
+            )
+            rest = slice(end * CHUNK, LOOKBACK_SPAN)
+            if end < chunks:
+                dq_ref[:, rest, :] = jnp.zeros_like(dq_ref[:, rest, :]) if near else part_ref[:, rest, :]
+            out_ref[0] = dk_ref[...].astype(bf16)
+            out_ref[1] = dv_ref[...].astype(bf16)
 
 
 def own_kernel(kv_ref, q_ref, lo_ref, part_ref, out_ref, dk_ref, dv_ref, dq_ref):
-    sweep(True, LOOKBACK_SPAN, kv_ref, q_ref, lo_ref, dk_ref, dv_ref, dq_ref, part_ref)
+    chunks = LOOKBACK_SPAN // CHUNK
+    sweep(
+        [(at, 0, at + 1) for at in range(chunks - 1, -1, -1)],
+        True, LOOKBACK_SPAN, kv_ref, q_ref, lo_ref, dk_ref, dv_ref, dq_ref, part_ref,
+    )
     for core in range(CORES):
         block = slice(core * HALF, (core + 1) * HALF)
         out_ref[core, 0] = dq_ref[0, block, :].astype(bf16)
@@ -189,11 +201,11 @@
     return pl.BlockSpec(memory_space=pltpu.SMEM)
 
 
-SPAN_SCRATCH = [
-    pltpu.VMEM((LOOKBACK_SPAN, HEAD_SIZE), f32),
-    pltpu.VMEM((LOOKBACK_SPAN, HEAD_SIZE), f32),
-]
 HALF = LOOKBACK_SPAN // CORES
+
+
+def rows_scratch(rows):
+    return [pltpu.VMEM((rows, HEAD_SIZE), f32)] * 2
 
 
 def cost():
@@ -201,21 +213,20 @@
     return pl.CostEstimate(flops=pairs * 5 * 2 * HEAD_SIZE, transcendentals=pairs, bytes_accessed=4 << 20)
 
 
-def cross_terms(core, kv, q, lo):
-    return pl.pallas_call(
-        cross_kernel,
-        in_specs=[smem_spec()] + [vmem_spec()] * 3,
-        out_specs=[vmem_spec()] * 3,
+def cross_terms(near, core, kv, q, lo, *part):
+    return pl.pallas_call(
+        functools.partial(cross_kernel, near),
+        in_specs=[smem_spec()] + [vmem_spec()] * (3 + len(part)),
+        out_specs=[vmem_spec()] * 2,
         out_shape=[
             jax.ShapeDtypeStruct((2, LOOKBACK_SPAN, HEAD_SIZE), f32),
             jax.ShapeDtypeStruct((2, HALF, HEAD_SIZE), bf16),
-            jax.ShapeDtypeStruct((2, HALF, HEAD_SIZE), bf16),
         ],
-        scratch_shapes=SPAN_SCRATCH,
+        scratch_shapes=rows_scratch(HALF),
         compiler_params=pltpu.CompilerParams(vmem_limit_bytes=40 << 20),
         cost_estimate=cost(),
-        name="cross_terms",
-    )(core, kv, q, lo)
+        name="cross_near" if near else "cross_far",
+    )(core, kv, q, lo, *part)
 
 
 def own_terms(kv, q, lo, part):
@@ -224,43 +235,54 @@
         in_specs=[vmem_spec()] * 4,
         out_specs=vmem_spec(),
         out_shape=jax.ShapeDtypeStruct((CORES, 4, HALF, HEAD_SIZE), bf16),
-        scratch_shapes=SPAN_SCRATCH + [pltpu.VMEM((2, LOOKBACK_SPAN, HEAD_SIZE), f32)],
+        scratch_shapes=rows_scratch(LOOKBACK_SPAN) + [pltpu.VMEM((2, LOOKBACK_SPAN, HEAD_SIZE), f32)],
         compiler_params=pltpu.CompilerParams(vmem_limit_bytes=40 << 20),
         cost_estimate=cost(),
         name="own_terms",
     )(kv, q, lo, part)
 
 
-def join_kernel(core_ref, own_ref, near_ref, far_ref, dq_ref, dk_ref, dv_ref):
+def join_kernel(near, core_ref, own_ref, back_ref, *refs):
+    dk_ref, dv_ref = refs[-2:]
+    for k in range(CORES):
+
+        @pl.when(core_ref[0] == (k if near else 1 - k))
+        def _():
+            columns = slice(k * HEAD_SIZE, (k + 1) * HEAD_SIZE)
+            for i, out_ref in enumerate((dk_ref, dv_ref)):
+                if not near:
+                    others = slice((1 - k) * HEAD_SIZE, (2 - k) * HEAD_SIZE)
+                    out_ref[:, others] = refs[i][:, others]
+                out_ref[:, columns] = (own_ref[k, 2 + i].astype(f32) + back_ref[i].astype(f32)).astype(bf16)
+
+
+def join(near, core, own, back, *halves):
+    return pl.pallas_call(
+        functools.partial(join_kernel, near),
+        in_specs=[smem_spec()] + [vmem_spec()] * (2 + len(halves)),
+        out_specs=[vmem_spec()] * 2,
+        out_shape=[jax.ShapeDtypeStruct((HALF, 2 * HEAD_SIZE), bf16)] * 2,
+        compiler_params=pltpu.CompilerParams(vmem_limit_bytes=16 << 20),
+        name="join_near" if near else "join_far",
+    )(core, own, back, *halves)
+
+
+def join_queries_kernel(own_ref, dq_ref):
     for core in range(CORES):
         for a in range(2):
             at = 2 * core + a
             dq_ref[:, at * HEAD_SIZE : (at + 1) * HEAD_SIZE] = own_ref[core, a]
 
-    for core in range(CORES):
-
-        @pl.when(core_ref[0] == core)
-        def _():
-            for i, out_ref in enumerate((dk_ref, dv_ref)):
-                for k in range(CORES):
-                    back_ref = near_ref if k == core else far_ref
-                    total = own_ref[k, 2 + i].astype(f32) + back_ref[i].astype(f32)
-                    out_ref[:, k * HEAD_SIZE : (k + 1) * HEAD_SIZE] = total.astype(bf16)
-
-
-def join(core, own, back_near, back_far):
-    return pl.pallas_call(
-        join_kernel,
-        in_specs=[smem_spec()] + [vmem_spec()] * 3,
-        out_specs=[vmem_spec()] * 3,
-        out_shape=[
-            jax.ShapeDtypeStruct((HALF, 4 * HEAD_SIZE), bf16),
-            jax.ShapeDtypeStruct((HALF, 2 * HEAD_SIZE), bf16),
-            jax.ShapeDtypeStruct((HALF, 2 * HEAD_SIZE), bf16),
-        ],
+
+def join_queries(own):
+    return pl.pallas_call(
+        join_queries_kernel,
+        in_specs=[vmem_spec()],
+        out_specs=vmem_spec(),
+        out_shape=jax.ShapeDtypeStruct((HALF, 4 * HEAD_SIZE), bf16),
         compiler_params=pltpu.CompilerParams(vmem_limit_bytes=16 << 20),
-        name="join",
-    )(core, own, back_near, back_far)
+        name="join_queries",
+    )(own)
 
 
 def first_allowed(doc_ids, chip):
@@ -289,8 +311,9 @@
     kv, packed = lax.optimization_barrier((kv, packed))
     q = exchange(packed)
     kv_before = lax.ppermute(kv, "chip", [(c, c + 1) for c in range(chips - 1)])
-    dq_part, near, far = cross_terms(core, kv_before, q, lo)
+    dq_part, near = cross_terms(True, core, kv_before, q, lo)
     back_near = lax.ppermute(near, "chip", [(c + 1, c) for c in range(chips - 1)])
+    dq_part, far = cross_terms(False, core, kv_before, q, lo, dq_part)
     back_far = lax.ppermute(
         far,
         ("chip", "core"),
@@ -298,7 +321,10 @@
     )
     own = own_terms(kv, q, lo, dq_part)
     own = lax.all_to_all(own, "core", split_axis=0, concat_axis=0, tiled=True)
-    return join(core, own, back_near, back_far)
+    query_grad = join_queries(own)
+    halves = join(True, core, own, back_near)
+    key_grad, value_grad = join(False, core, own, back_far, *halves)
+    return query_grad, key_grad, value_grad
 
 
 def solution(mesh):

time: 86.4 us -> 87.3 us (1.010)
  Pallas kernels: 15 us -> 16 us
    pallas_call x2 -> x5, Pallas kernels: 4.96 us -> 6.05 us  [the longest x2 4.18 us: cross_terms(): pl.pallas_call(functools.partial(cross_kernel, near), in_specs=[smem_spec...]
  transfers between devices with their start and end apart: 5 -> 5, of which waited for: 4 -> 3; matrix products, arithmetic and copies ran while one was open for 1% -> 1% of each run, Pallas kernels for 9% -> 12%
where the time goes in v3:
time: 87.3 us; the launch traced here: 86.4 us
  waiting for transfers between devices  33.3 us (38%)
  starting transfers between devices  30.8 us (35%)
  Pallas kernels  16 us (18%)
  blocking collectives  4.49 us (5%)
  other arithmetic  0.99 us (1%)
    ppermute x1, waiting for transfers between devices, on_device(): kv_before = lax.ppermute(kv, 'chip', [(c, c + 1) for c in range(chips - 1)])  18.1 us
    all_to_all x2, waiting for transfers between devices, exchange(): lax.all_to_all(value, ('core', 'head'), split_axis=0, concat_axis=0, tile...  15.3 us
    all_to_all x2, starting transfers between devices, exchange(): lax.all_to_all(value, ('core', 'head'), split_axis=0, concat_axis=0, tile...  13.4 us
    ppermute x1, starting transfers between devices, on_device(): lax.ppermute(near, 'chip', [(c + 1, c) for c in range(chips - 1)])  10.9 us
    all_to_all x1, blocking collectives, on_device(): own = lax.all_to_all(own, 'core', split_axis=0, concat_axis=0, tiled=True)  4.49 us
    pallas_call x1, Pallas kernels, pack_queries(): pl.pallas_call(pack_queries_kernel, grid=(steps,), in_specs=[pl.BlockSpec...  4.27 us
    pallas_call x2, Pallas kernels, cross_terms(): pl.pallas_call(functools.partial(cross_kernel, near), in_specs=[smem_spec...  4.18 us
    ppermute x1, starting transfers between devices, on_device(): kv_before = lax.ppermute(kv, 'chip', [(c, c + 1) for c in range(chips - 1)])  4.03 us
  transfers between devices with their start and end apart: 5, of which 3 were waited for; matrix products, arithmetic and copies ran while one was open for 1% of the time, Pallas kernels for 12%

profile of v3, /device:TPU:7, one launch (start us, length us, event | category | flops | bytes accessed | tf_op | source)
XLA Modules:
  0.0 86.4 jit_solution(8146833694111871817)
XLA Ops:
  0.6 1.9 %pack_keys.1 = bf16[2,8,128,128]{3,2,1,0:T(8,128)(2,1)} custom-call(bf16[64,2048]{1,0:T(8,128)(2,1)} %key_ref.1, bf16[64,2048]{1,0:T(8,128)(2,1)} %value_ref.1), custom_call_target="tpu_custom_call" | custom-call | tf_op jit(solution)/shard_map/pack_keys/pallas_call | solution.py:47
  2.5 7.8 %all-to-all-start = ((bf16[16,128,128]{2,1,0:T(8,128)(2,1)}), bf16[16,128,128]{2,1,0:T(8,128)(2,1)S(1)}, u32[]{:S(2)}, u32[]{:S(2)}) async-start(bf16[16,128,128]{2,1,0:T(8,128)(2,1)} %bitcast.6), calls=%async_computation | async-start | bytes 1048576 | tf_op jit(solution)/shard_map/all_to_all | solution.py:299
  10.3 4.3 %pack_queries.1 = bf16[2,8,272,128]{3,2,1,0:T(8,128)(2,1)} custom-call(s32[1]{0:T(128)} %bitcast.1.parity_ref, bf16[64,4096]{1,0:T(8,128)(2,1)} %query_ref.1, bf16[64,4096]{1,0:T(8,128)(2,1)} %grad_ref.1, bf16[64,4096]{1,0:T(8,128)(2,1)} %row_ref.1, f32[32,64]{1,0:T(8,128)} %lse_ref.1), custom_call_target="tpu_custom_call" | custom-call | tf_op jit(solution)/shard_map/pack_queries/pallas_call | solution.py:100
  14.6 10.5 %all-to-all-done.kv_ref = bf16[16,128,128]{2,1,0:T(8,128)(2,1)S(1)} async-done(((bf16[16,128,128]{2,1,0:T(8,128)(2,1)}), bf16[16,128,128]{2,1,0:T(8,128)(2,1)S(1)}, u32[]{:S(2)}, u32[]{:S(2)}) %all-to-all-start) | async-done | bytes 524320 | tf_op jit(solution)/shard_map/all_to_all | solution.py:299
  25.1 0.0 copy-start
  25.1 5.6 %all-to-all-start.1 = ((bf16[16,272,128]{2,1,0:T(8,128)(2,1)}), bf16[16,272,128]{2,1,0:T(8,128)(2,1)S(1)}, u32[]{:S(2)}, u32[]{:S(2)}) async-start(bf16[16,272,128]{2,1,0:T(8,128)(2,1)} %bitcast.5), calls=%async_computation.1 | async-start | bytes 2228224 | tf_op jit(solution)/shard_map/all_to_all | solution.py:299
  30.6 0.0 copy-done
  30.7 4.0 %collective-permute-start = (bf16[16,128,128]{2,1,0:T(8,128)(2,1)S(1)}, bf16[16,128,128]{2,1,0:T(8,128)(2,1)S(1)}, u32[]{:S(2)}, u32[]{:S(2)}) collective-permute-start(bf16[16,128,128]{2,1,0:T(8,128)(2,1)S(1)} %all-to-all-done.kv_ref), channel_id=1, source_target_pairs={{0,16},{16,32},{32,48},{48,64},{64,80},{80,96},{96,112},{112,128},... | collective-permute-start | bytes 1572872 | tf_op jit(solution)/shard_map/ppermute | solution.py:313
  34.7 1.0 %convert_reduce_fusion = s32[1024]{0:T(1024)S(1)} fusion(s32[1024]{0:T(1024)S(1)} %pad_dynamic-slice_fusion, s32[2048]{0:T(1024)S(1)} %pad_dynamic-slice_fusion.1), kind=kLoop, calls=%fused_computation | loop fusion | flops 6290432 | bytes 16384 | tf_op jit(solution)/shard_map/reduce_sum | solution.py:292
  35.7 18.1 %collective-permute-done.kv_ref = bf16[16,128,128]{2,1,0:T(8,128)(2,1)S(1)} collective-permute-done((bf16[16,128,128]{2,1,0:T(8,128)(2,1)S(1)}, bf16[16,128,128]{2,1,0:T(8,128)(2,1)S(1)}, u32[]{:S(2)}, u32[]{:S(2)}) %collective-permute-start) | collective-permute-done | bytes 524320 | tf_op jit(solution)/shard_map/ppermute | solution.py:313
  53.8 4.8 %all-to-all-done.1.q_ref = bf16[16,272,128]{2,1,0:T(8,128)(2,1)S(1)} async-done(((bf16[16,272,128]{2,1,0:T(8,128)(2,1)}), bf16[16,272,128]{2,1,0:T(8,128)(2,1)S(1)}, u32[]{:S(2)}, u32[]{:S(2)}) %all-to-all-start.1) | async-done | bytes 1114144 | tf_op jit(solution)/shard_map/all_to_all | solution.py:299
  58.5 2.8 %cross_near.1 = (f32[2,1024,128]{2,1,0:T(8,128)S(1)}, bf16[2,512,128]{2,1,0:T(8,128)(2,1)S(1)}) custom-call(s32[1]{0:T(128)} %bitcast.4.core_ref, bf16[16,128,128]{2,1,0:T(8,128)(2,1)S(1)} %collective-permute-done.kv_ref, bf16[16,272,128]{2,1,0:T(8,128)(2,1)S(1)} %all-to-all-done.1.q_ref, s32[8,1,128]{2,1,0:T(1,128)S(1)} %add_maximum_fusion.lo_ref), custom_call_target="tpu_custom_call" | custom-call | flops 1342177280 | bytes 4194304 | tf_op jit(solution)/shard_map/cross_near/pallas_call | solution.py:217
  61.4 10.9 %collective-permute-start.2 = (bf16[2,512,128]{2,1,0:T(8,128)(2,1)S(1)}, bf16[2,512,128]{2,1,0:T(8,128)(2,1)S(1)}, u32[]{:S(2)}, u32[]{:S(2)}) collective-permute-start(bf16[2,512,128]{2,1,0:T(8,128)(2,1)S(1)} %get-tuple-element.18), channel_id=1, source_target_pairs={{16,0},{32,16},{48,32},{64,48},{80,64},{96,80},{112,96},{128,112},... | collective-permute-start | bytes 786440 | tf_op jit(solution)/shard_map/ppermute | solution.py:315
  72.3 1.4 %cross_far.1 = (f32[2,1024,128]{2,1,0:T(8,128)S(1)}, bf16[2,512,128]{2,1,0:T(8,128)(2,1)S(1)}) custom-call(s32[1]{0:T(128)} %bitcast.4.core_ref, bf16[16,128,128]{2,1,0:T(8,128)(2,1)S(1)} %collective-permute-done.kv_ref, bf16[16,272,128]{2,1,0:T(8,128)(2,1)S(1)} %all-to-all-done.1.q_ref, s32[8,1,128]{2,1,0:T(1,128)S(1)} %add_maximum_fusion.lo_ref, ...), custom_call_target="tpu_custom_call" | custom-call | flops 1342177280 | bytes 4194304 | tf_op jit(solution)/shard_map/cross_far/pallas_call | solution.py:217
  73.7 2.5 %collective-permute-start.1 = (bf16[2,512,128]{2,1,0:T(8,128)(2,1)S(1)}, bf16[2,512,128]{2,1,0:T(8,128)(2,1)S(1)}, u32[]{:S(2)}, u32[]{:S(2)}) collective-permute-start(bf16[2,512,128]{2,1,0:T(8,128)(2,1)S(1)} %get-tuple-element.17), channel_id=1, source_target_pairs={{16,8},{24,0},{32,24},{40,16},{48,40},{56,32},{64,56},{72,48},{80,... | collective-permute-start | bytes 786440 | tf_op jit(solution)/shard_map/ppermute | solution.py:317
  76.2 3.9 %own_terms.1 = bf16[2,4,512,128]{3,2,1,0:T(8,128)(2,1)S(1)} custom-call(bf16[16,128,128]{2,1,0:T(8,128)(2,1)S(1)} %all-to-all-done.kv_ref, bf16[16,272,128]{2,1,0:T(8,128)(2,1)S(1)} %all-to-all-done.1.q_ref, s32[8,1,128]{2,1,0:T(1,128)S(1)} %add_maximum_fusion.lo_ref, f32[2,1024,128]{2,1,0:T(8,128)S(1)} %get-tuple-element.16.part_ref), custom_call_target="tpu_custom_call" | custom-call | flops 1342177280 | bytes 4194304 | tf_op jit(solution)/shard_map/own_terms/pallas_call | solution.py:233
  80.0 4.5 %all_to_all.15.own_ref = bf16[2,4,512,128]{3,2,1,0:T(8,128)(2,1)S(1)} all-to-all(bf16[2,4,512,128]{3,2,1,0:T(8,128)(2,1)S(1)} %own_terms.1), channel_id=1, replica_groups=mesh['chip'=32,'core'=2,'head'=8] {'core'}, dimensions={0} | all-to-all | bytes 2097152 | tf_op jit(solution)/shard_map/all_to_all | solution.py:323
  84.5 0.9 %join_queries.1 = bf16[512,512]{1,0:T(8,128)(2,1)} custom-call(bf16[2,4,512,128]{3,2,1,0:T(8,128)(2,1)S(1)} %all_to_all.15.own_ref), custom_call_target="tpu_custom_call" | custom-call | tf_op jit(solution)/shard_map/join_queries/pallas_call | solution.py:278
  85.4 0.0 collective-permute-done.2.back_ref
  85.4 0.1 join_near.1
  85.5 0.0 collective-permute-done.1.back_ref
  85.5 0.9 %join_far.1 = (bf16[512,256]{1,0:T(8,128)(2,1)}, bf16[512,256]{1,0:T(8,128)(2,1)}) custom-call(s32[1]{0:T(128)} %bitcast.4.core_ref, bf16[2,4,512,128]{3,2,1,0:T(8,128)(2,1)S(1)} %all_to_all.15.own_ref, bf16[2,512,128]{2,1,0:T(8,128)(2,1)S(1)} %collective-permute-done.1.back_ref, bf16[512,256]{1,0:T(8,128)(2,1)S(1)} %get-tuple-element.19.refs_0_, ...), custom_call_target="tpu_custom_call" | custom-call | tf_op jit(solution)/shard_map/join_far/pallas_call | solution.py:260
  (3 shorter events, 0.0 us)
Async XLA Ops:
  2.5 22.6 %all-to-all-start = ((bf16[16,128,128]{2,1,0:T(8,128)(2,1)}), bf16[16,128,128]{2,1,0:T(8,128)(2,1)S(1)}, u32[]{:S(2)}, u32[]{:S(2)}) async-start(bf16[16,128,128]{2,1,0:T(8,128)(2,1)} %bitcast.6), calls=%async_computation | async-start | bytes 1048576 | tf_op jit(solution)/shard_map/all_to_all | solution.py:299
  25.1 5.6 %copy-start = (s32[32768]{0:T(1024)S(1)}, s32[32768]{0:T(1024)}, u32[]{:S(2)}) copy-start(s32[32768]{0:T(1024)} %param.13) | copy-start | bytes 393220
  25.1 33.5 %all-to-all-start.1 = ((bf16[16,272,128]{2,1,0:T(8,128)(2,1)}), bf16[16,272,128]{2,1,0:T(8,128)(2,1)S(1)}, u32[]{:S(2)}, u32[]{:S(2)}) async-start(bf16[16,272,128]{2,1,0:T(8,128)(2,1)} %bitcast.5), calls=%async_computation.1 | async-start | bytes 2228224 | tf_op jit(solution)/shard_map/all_to_all | solution.py:299
  30.7 23.1 %collective-permute-start = (bf16[16,128,128]{2,1,0:T(8,128)(2,1)S(1)}, bf16[16,128,128]{2,1,0:T(8,128)(2,1)S(1)}, u32[]{:S(2)}, u32[]{:S(2)}) collective-permute-start(bf16[16,128,128]{2,1,0:T(8,128)(2,1)S(1)} %all-to-all-done.kv_ref), channel_id=1, source_target_pairs={{0,16},{16,32},{32,48},{48,64},{64,80},{80,96},{96,112},{112,128},... | collective-permute-start | bytes 1572872 | tf_op jit(solution)/shard_map/ppermute | solution.py:313
  61.4 24.0 %collective-permute-start.2 = (bf16[2,512,128]{2,1,0:T(8,128)(2,1)S(1)}, bf16[2,512,128]{2,1,0:T(8,128)(2,1)S(1)}, u32[]{:S(2)}, u32[]{:S(2)}) collective-permute-start(bf16[2,512,128]{2,1,0:T(8,128)(2,1)S(1)} %get-tuple-element.18), channel_id=1, source_target_pairs={{16,0},{32,16},{48,32},{64,48},{80,64},{96,80},{112,96},{128,112},... | collective-permute-start | bytes 786440 | tf_op jit(solution)/shard_map/ppermute | solution.py:315
  73.7 11.8 %collective-permute-start.1 = (bf16[2,512,128]{2,1,0:T(8,128)(2,1)S(1)}, bf16[2,512,128]{2,1,0:T(8,128)(2,1)S(1)}, u32[]{:S(2)}, u32[]{:S(2)}) collective-permute-start(bf16[2,512,128]{2,1,0:T(8,128)(2,1)S(1)} %get-tuple-element.17), channel_id=1, source_target_pairs={{16,8},{24,0},{32,24},{40,16},{48,40},{56,32},{64,56},{72,48},{80,... | collective-permute-start | bytes 786440 | tf_op jit(solution)/shard_map/ppermute | solution.py:317

commit v4 on v3

v4 whole, which is shorter than its diff:
```python
import functools
import math

import jax
import jax.numpy as jnp
from jax import lax
from jax.experimental import pallas as pl
from jax.experimental.pallas import tpu as pltpu
from jax.sharding import Mesh
from jax.sharding import PartitionSpec as P

HEAD_SIZE = 128
LOOKBACK_SPAN = 1024
CORES = 2
PIECE = 64
META_ROWS = 8
CHUNK = 128

score_scale = 168.0 ** (-0.5)
log2_e = math.log2(math.e)

f32 = jnp.float32
bf16 = jnp.bfloat16


def dot_t(left, right):
    return lax.dot_general(left, right, (((1,), (1,)), ((), ())), preferred_element_type=f32)


def dot_n(left, right):
    return lax.dot_general(left, right, (((1,), (0,)), ((), ())), preferred_element_type=f32)


def t_dot(left, right):
    return lax.dot_general(left, right, (((0,), (0,)), ((), ())), preferred_element_type=f32)


def pack_keys_kernel(key_ref, value_ref, out_ref):
    for at in range(out_ref.shape[0]):
        columns = slice(at * HEAD_SIZE, (at + 1) * HEAD_SIZE)
        out_ref[at, 0:PIECE, :] = key_ref[:, columns]
        out_ref[at, PIECE : 2 * PIECE, :] = value_ref[:, columns]


def pack_keys(keys, values, steps=2):
    heads = keys.shape[1] // HEAD_SIZE
    return pl.pallas_call(
        pack_keys_kernel,
        grid=(steps,),
        in_specs=[pl.BlockSpec((PIECE, keys.shape[1] // steps), lambda i: (0, i))] * 2,
        out_specs=pl.BlockSpec((heads // steps, 2 * PIECE, HEAD_SIZE), lambda i: (i, 0, 0)),
        out_shape=jax.ShapeDtypeStruct((heads, 2 * PIECE, HEAD_SIZE), bf16),
        name="pack_keys",
    )(keys, values)


def three_parts(value):
    high = value.astype(bf16)
    rest = value - high.astype(f32)
    middle = rest.astype(bf16)
    return [high, middle, (rest - middle.astype(f32)).astype(bf16)]


def pack_queries_kernel(core_ref, query_ref, grad_ref, row_ref, lse_ref, keep_ref, give_ref):
    groups = keep_ref.shape[0]
    heads = 2 * CORES * groups
    width = heads * HEAD_SIZE
    for core in range(CORES):

        @pl.when(core_ref[0] == core)
        def _():
            for out_ref, to in ((keep_ref, core), (give_ref, 1 - core)):
                for group in range(groups):
                    for a in range(2):
                        head = 2 * (CORES * group + to) + a
                        columns = slice(head * HEAD_SIZE, (head + 1) * HEAD_SIZE)
                        out_ref[group, a * PIECE : (a + 1) * PIECE, :] = query_ref[:, columns]
                        out_ref[group, (2 + a) * PIECE : (3 + a) * PIECE, :] = grad_ref[:, columns]

    product = grad_ref[...].astype(f32) * row_ref[...].astype(f32)
    product_high = product.astype(bf16)
    product_low = (product - product_high.astype(f32)).astype(bf16)
    which = lax.broadcasted_iota(jnp.int32, (heads, width), 1) // HEAD_SIZE
    member = jnp.where(which == lax.broadcasted_iota(jnp.int32, (heads, width), 0), 1.0, 0.0).astype(bf16)
    delta = dot_t(member, product_high) + dot_t(member, product_low)
    parts = three_parts(lse_ref[...]) + three_parts(delta)
    rows = jnp.concatenate([p.astype(f32) for p in parts], axis=0).astype(bf16)
    total = groups * META_ROWS
    row_at = lax.broadcasted_iota(jnp.int32, (total, 6 * heads), 0)
    column_at = lax.broadcasted_iota(jnp.int32, (total, 6 * heads), 1)
    for out_ref, to in ((keep_ref, core_ref[0]), (give_ref, 1 - core_ref[0])):
        first_head = 2 * (CORES * (row_at // META_ROWS) + to)
        halves = []
        for half in range(2):
            m = 2 * (row_at % META_ROWS) + half
            source = ((m // 6) * 3 + m % 3) * heads + first_head + (m // 3) % 2
            pick = jnp.where((m < 12) & (column_at == source), 1.0, 0.0).astype(bf16)
            halves.append(dot_n(pick, rows))
        meta = jnp.concatenate(halves, axis=1).reshape(groups, META_ROWS, HEAD_SIZE)
        for group in range(groups):
            out_ref[group, 4 * PIECE : 4 * PIECE + META_ROWS, :] = meta[group].astype(bf16)


def pack_queries(core, queries, grads, rows, lse, groups, steps=4):
    width = queries.shape[1] // steps
    height = 4 * PIECE + META_ROWS
    return pl.pallas_call(
        pack_queries_kernel,
        grid=(steps,),
        in_specs=[pl.BlockSpec(memory_space=pltpu.SMEM)]
        + [pl.BlockSpec((PIECE, width), lambda i: (0, i))] * 3
        + [pl.BlockSpec((lse.shape[0] // steps, PIECE), lambda i: (i, 0))],
        out_specs=[pl.BlockSpec((groups // steps, height, HEAD_SIZE), lambda i: (i, 0, 0))] * 2,
        out_shape=[jax.ShapeDtypeStruct((groups, height, HEAD_SIZE), bf16)] * 2,
        name="pack_queries",
    )(core, queries, grads, rows, lse)


def chunk_rows(ref, slots, first, last, row):
    per_block = LOOKBACK_SPAN // CORES // CHUNK
    pieces = CHUNK // PIECE
    found = []
    for block in range(CORES):
        start, end = max(first, block * per_block), min(last, (block + 1) * per_block)
        if start < end:
            at = slice((start - block * per_block) * pieces, (end - block * per_block) * pieces)
            rows = ref[at, slots[block], row : row + PIECE, :]
            found.append(rows.reshape((end - start) * CHUNK, HEAD_SIZE))
    return found[0] if len(found) == 1 else jnp.concatenate(found)


def chunk_meta(ref, slots, at):
    per_block = LOOKBACK_SPAN // CORES // CHUNK
    piece = (at % per_block) * (CHUNK // PIECE)
    meta = [
        ref[piece + i, slots[at // per_block], 4 * PIECE : 4 * PIECE + META_ROWS, :].astype(f32) for i in range(2)
    ]
    turned = [pltpu.roll(m, PIECE, 1) for m in meta]
    left = lax.broadcasted_iota(jnp.int32, meta[0].shape, 1) < PIECE
    halves = (jnp.where(left, meta[0], turned[1]), jnp.where(left, turned[0], meta[1]))
    pieces = [halves[m % 2][m // 2 : m // 2 + 1] for m in range(12)]
    rows = [pieces[3 * r] + pieces[3 * r + 1] + pieces[3 * r + 2] for r in range(4)]
    return jnp.concatenate(rows[0:2], axis=1), jnp.concatenate(rows[2:4], axis=1)


def sweep(strips, causal, key_base, key_slots, q_slots, kv_ref, q_ref, lo_ref, dk_ref, dv_ref, dq_ref, part_ref):
    base = strips[0][1]
    for n, (at, first, last) in enumerate(strips):
        strip = slice((first - base) * CHUNK, (last - base) * CHUNK)
        height = (last - first) * CHUNK
        key = chunk_rows(kv_ref, key_slots, first, last, 0)
        value = chunk_rows(kv_ref, key_slots, first, last, PIECE)
        query, grad = [
            jnp.concatenate([chunk_rows(q_ref, q_slots, at, at + 1, (row + a) * PIECE) for a in range(2)])
            for row in (0, 2)
        ]
        lse, delta = chunk_meta(q_ref, q_slots, at)
        lse = lse * log2_e
        lo = lo_ref[at] - (key_base + first * CHUNK)
        lo = jnp.concatenate([lo, lo], axis=1)
        key_at = lax.broadcasted_iota(jnp.int32, (height, 2 * CHUNK), 0)
        allowed = key_at >= lo
        if causal:
            query_at = lax.broadcasted_iota(jnp.int32, (1, 2 * CHUNK), 1) % CHUNK + at * CHUNK
            allowed = allowed & (key_at <= query_at)
        scores = dot_t(key, query)
        prob = jnp.where(allowed, jnp.exp2(scores * (score_scale * log2_e) - lse), 0.0)
        prob_grad = dot_t(value, grad)
        score_grad = ((prob * score_scale) * (prob_grad - delta)).astype(bf16)
        dv = dot_n(prob.astype(bf16), grad)
        dk = dot_n(score_grad, query)
        if n == 0:
            dv_ref[strip, :] = dv
            dk_ref[strip, :] = dk
        else:
            dv_ref[strip, :] += dv
            dk_ref[strip, :] += dk
        dq = t_dot(score_grad, key)
        for a in range(2):
            mine = dq[a * CHUNK : (a + 1) * CHUNK]
            if part_ref is not None:
                mine = mine + part_ref[a, at * CHUNK : (at + 1) * CHUNK, :]
            dq_ref[a, at * CHUNK : (at + 1) * CHUNK, :] = mine


def cross_kernel(near, core_ref, kv_ref, q_ref, lo_ref, *refs):
    part_ref = None if near else refs[0]
    dq_ref, out_ref, dk_ref, dv_ref = refs[-4:]
    chunks = LOOKBACK_SPAN // CHUNK
    for block in range(CORES):
        core = block if near else 1 - block

        @pl.when(core_ref[0] == core)
        def _():
            start, end = block * chunks // CORES, (block + 1) * chunks // CORES
            sweep(
                [(at, max(at, start), end) for at in range(end)],
                False, 0, (0, 0), (core, 1 - core), kv_ref, q_ref, lo_ref, dk_ref, dv_ref, dq_ref, part_ref,
            )
            rest = slice(end * CHUNK, LOOKBACK_SPAN)
            if end < chunks:
                dq_ref[:, rest, :] = jnp.zeros_like(dq_ref[:, rest, :]) if near else part_ref[:, rest, :]
            out_ref[0] = dk_ref[...].astype(bf16)
            out_ref[1] = dv_ref[...].astype(bf16)


def own_kernel(core_ref, kv_near_ref, kv_far_ref, q_ref, lo_ref, part_ref, out_ref, dk_ref, dv_ref, dq_ref, kv_ref):
    kv_ref[:, 0] = kv_near_ref[...]
    kv_ref[:, 1] = kv_far_ref[...]
    chunks = LOOKBACK_SPAN // CHUNK
    slots = (core_ref[0], 1 - core_ref[0])
    sweep(
        [(at, 0, at + 1) for at in range(chunks - 1, -1, -1)],
        True, LOOKBACK_SPAN, slots, slots, kv_ref, q_ref, lo_ref, dk_ref, dv_ref, dq_ref, part_ref,
    )
    for core in range(CORES):
        block = slice(core * HALF, (core + 1) * HALF)
        out_ref[core, 0] = dq_ref[0, block, :].astype(bf16)
        out_ref[core, 1] = dq_ref[1, block, :].astype(bf16)
        out_ref[core, 2] = dk_ref[block, :].astype(bf16)
        out_ref[core, 3] = dv_ref[block, :].astype(bf16)


def vmem_spec():
    return pl.BlockSpec(memory_space=pltpu.VMEM)


def smem_spec():
    return pl.BlockSpec(memory_space=pltpu.SMEM)


HALF = LOOKBACK_SPAN // CORES


def rows_scratch(rows):
    return [pltpu.VMEM((rows, HEAD_SIZE), f32)] * 2


def cost():
    pairs = LOOKBACK_SPAN * LOOKBACK_SPAN
    return pl.CostEstimate(flops=pairs * 5 * 2 * HEAD_SIZE, transcendentals=pairs, bytes_accessed=4 << 20)


def cross_terms(near, core, kv, q, lo, *part):
    return pl.pallas_call(
        functools.partial(cross_kernel, near),
        in_specs=[smem_spec()] + [vmem_spec()] * (3 + len(part)),
        out_specs=[vmem_spec()] * 2,
        out_shape=[
            jax.ShapeDtypeStruct((2, LOOKBACK_SPAN, HEAD_SIZE), f32),
            jax.ShapeDtypeStruct((2, HALF, HEAD_SIZE), bf16),
        ],
        scratch_shapes=rows_scratch(HALF),
        compiler_params=pltpu.CompilerParams(vmem_limit_bytes=40 << 20),
        cost_estimate=cost(),
        name="cross_near" if near else "cross_far",
    )(core, kv, q, lo, *part)


def own_terms(core, kv_near, kv_far, q, lo, part):
    return pl.pallas_call(
        own_kernel,
        in_specs=[smem_spec()] + [vmem_spec()] * 5,
        out_specs=vmem_spec(),
        out_shape=jax.ShapeDtypeStruct((CORES, 4, HALF, HEAD_SIZE), bf16),
        scratch_shapes=rows_scratch(LOOKBACK_SPAN)
        + [
            pltpu.VMEM((2, LOOKBACK_SPAN, HEAD_SIZE), f32),
            pltpu.VMEM((HALF // PIECE, CORES, 2 * PIECE, HEAD_SIZE), bf16),
        ],
        compiler_params=pltpu.CompilerParams(vmem_limit_bytes=40 << 20),
        cost_estimate=cost(),
        name="own_terms",
    )(core, kv_near, kv_far, q, lo, part)


def join_kernel(near, core_ref, own_ref, back_ref, *refs):
    dk_ref, dv_ref = refs[-2:]
    if near:
        dq_ref = refs[0]
        for core in range(CORES):
            for a in range(2):
                at = 2 * core + a
                dq_ref[:, at * HEAD_SIZE : (at + 1) * HEAD_SIZE] = own_ref[core, a]
    for k in range(CORES):

        @pl.when(core_ref[0] == (k if near else 1 - k))
        def _():
            columns = slice(k * HEAD_SIZE, (k + 1) * HEAD_SIZE)
            for i, out_ref in enumerate((dk_ref, dv_ref)):
                if not near:
                    others = slice((1 - k) * HEAD_SIZE, (2 - k) * HEAD_SIZE)
                    out_ref[:, others] = refs[i][:, others]
                out_ref[:, columns] = (own_ref[k, 2 + i].astype(f32) + back_ref[i].astype(f32)).astype(bf16)


def join(near, core, own, back, *halves):
    shapes = [jax.ShapeDtypeStruct((HALF, 2 * HEAD_SIZE), bf16)] * 2
    if near:
        shapes = [jax.ShapeDtypeStruct((HALF, 4 * HEAD_SIZE), bf16)] + shapes
    return pl.pallas_call(
        functools.partial(join_kernel, near),
        in_specs=[smem_spec()] + [vmem_spec()] * (2 + len(halves)),
        out_specs=[vmem_spec()] * len(shapes),
        out_shape=shapes,
        compiler_params=pltpu.CompilerParams(vmem_limit_bytes=16 << 20),
        name="join_near" if near else "join_far",
    )(core, own, back, *halves)


def first_allowed(doc_ids, chip):
    padded = jnp.concatenate([jnp.full((LOOKBACK_SPAN,), -1, jnp.int32), doc_ids])
    window = lax.dynamic_slice_in_dim(padded, chip * LOOKBACK_SPAN, 2 * LOOKBACK_SPAN, 0)
    own = window[LOOKBACK_SPAN:]
    document_start = jnp.sum((window[:, None] < own[None, :]).astype(jnp.int32), axis=0)
    reach_start = jnp.arange(1, LOOKBACK_SPAN + 1, dtype=jnp.int32)
    return jnp.maximum(document_start, reach_start).reshape(LOOKBACK_SPAN // CHUNK, 1, CHUNK)


def exchange(value):
    return lax.all_to_all(value, "head", split_axis=0, concat_axis=0, tiled=True)


def other_core(value):
    return lax.ppermute(value, "core", [(0, 1), (1, 0)])


def next_chip(value, step, cross):
    chips = lax.axis_size("chip")
    pairs = [
        (CORES * c + k, CORES * (c + step) + (1 - k if cross else k))
        for c in range(max(0, -step), min(chips, chips - step))
        for k in range(CORES)
    ]
    return lax.ppermute(value, ("chip", "core"), pairs)


def on_device(queries, keys, values, rows, grads, lse, doc_ids):
    groups = lax.axis_size("head")
    chip = lax.axis_index("chip")
    core_at = lax.axis_index("core").astype(jnp.int32)
    core = core_at.reshape(1)
    lo = first_allowed(doc_ids, chip)
    kv = exchange(pack_keys(keys, values).reshape(groups, CORES, 2 * PIECE, HEAD_SIZE))
    keep, give = pack_queries(core, queries, grads, rows, lse, groups)
    packed = jnp.stack([keep, other_core(give)], axis=1)
    kv, packed = lax.optimization_barrier((kv, packed))
    q = exchange(packed)
    kv_mine = jnp.where(core_at == 0, kv[:, 0], kv[:, 1])
    kv_other = jnp.where(core_at == 0, kv[:, 1], kv[:, 0])
    before_near = next_chip(kv_mine, 1, False)[:, None]
    before_far = next_chip(kv_other, 1, True)[:, None]
    kv_far = other_core(kv_other)
    dq_part, near = cross_terms(True, core, before_near, q, lo)
    back_near = next_chip(near, -1, False)
    dq_part, far = cross_terms(False, core, before_far, q, lo, dq_part)
    back_far = next_chip(far, -1, True)
    own = own_terms(core, kv_mine, kv_far, q, lo, dq_part)
    own = lax.all_to_all(own, "core", split_axis=0, concat_axis=0, tiled=True)
    query_grad, *halves = join(True, core, own, back_near)
    key_grad, value_grad = join(False, core, own, back_far, *halves)
    return query_grad, key_grad, value_grad


def solution(mesh):
    seq, head = mesh.devices.shape
    fine = Mesh(mesh.devices.reshape(seq // CORES, CORES, head), ("chip", "core", "head"))
    tokens = ("chip", "core", "head")
    return jax.shard_map(
        on_device,
        mesh=fine,
        in_specs=(P(tokens), P(tokens), P(tokens), P(tokens), P(tokens), P(None, tokens), P()),
        out_specs=(P(("chip", "core"), "head"),) * 3,
        check_vma=False,
    )
```

time: 87.3 us -> 89.5 us (1.025)
  starting transfers between devices: 30.8 us -> 37.8 us
  waiting for transfers between devices: 33.3 us -> 26.6 us
  other arithmetic: 0.99 us -> 3.25 us
    ppermute x3 -> x6, waiting for transfers between devices: 18.1 us -> 7.31 us  [the longest x4 5.56 us: next_chip(): return lax.ppermute(value, ('chip', 'core'), pairs)]
    ppermute x3 -> x6, starting transfers between devices: 17.4 us -> 27.4 us  [the longest x4 22.6 us: next_chip(): return lax.ppermute(value, ('chip', 'core'), pairs)]
    all_to_all x2, waiting for transfers between devices: 15.3 us -> 19.3 us  [exchange(): lax.all_to_all(value, 'head', split_axis=0, concat_axis=0, tiled=True)]
    all_to_all x2, starting transfers between devices: 13.4 us -> 10.4 us  [exchange(): lax.all_to_all(value, 'head', split_axis=0, concat_axis=0, tiled=True)]
    another operation x0 -> x1, other arithmetic: none -> 2.13 us  [on_device(): packed = jnp.stack([keep, other_core(give)], axis=1)]
    pallas_call x2 -> x1, Pallas kernels: 4.73 us -> 3.86 us  [own_terms(): pl.pallas_call(own_kernel, in_specs=[smem_spec()] + [vmem_spec()] * 5, ou...]
  transfers between devices with their start and end apart: 5 -> 8, of which waited for: 3 -> 4; matrix products, arithmetic and copies ran while one was open for 1% -> 4% of each run, Pallas kernels for 12% -> 15%
where the time goes in v4:
time: 89.5 us; the launch traced here: 88.9 us
  starting transfers between devices  37.8 us (42%)
  waiting for transfers between devices  26.6 us (30%)
  Pallas kernels  16.3 us (18%)
  blocking collectives  4.21 us (5%)
  other arithmetic  3.25 us (4%)
    ppermute x4, starting transfers between devices, next_chip(): return lax.ppermute(value, ('chip', 'core'), pairs)  22.6 us
    all_to_all x2, waiting for transfers between devices, exchange(): lax.all_to_all(value, 'head', split_axis=0, concat_axis=0, tiled=True)  19.3 us
    all_to_all x2, starting transfers between devices, exchange(): lax.all_to_all(value, 'head', split_axis=0, concat_axis=0, tiled=True)  10.4 us
    ppermute x4, waiting for transfers between devices, next_chip(): return lax.ppermute(value, ('chip', 'core'), pairs)  5.56 us
    ppermute x2, starting transfers between devices, other_core(): return lax.ppermute(value, 'core', [(0, 1), (1, 0)])  4.78 us
    pallas_call x1, Pallas kernels, pack_queries(): pl.pallas_call(pack_queries_kernel, grid=(steps,), in_specs=[pl.BlockSpec...  4.43 us
    pallas_call x2, Pallas kernels, cross_terms(): pl.pallas_call(functools.partial(cross_kernel, near), in_specs=[smem_spec...  4.27 us
    all_to_all x1, blocking collectives, on_device(): own = lax.all_to_all(own, 'core', split_axis=0, concat_axis=0, tiled=True)  4.21 us
  transfers between devices with their start and end apart: 8, of which 4 were waited for; matrix products, arithmetic and copies ran while one was open for 4% of the time, Pallas kernels for 15%

profile of v4, /device:TPU:7, one launch (start us, length us, event | category | flops | bytes accessed | tf_op | source)
XLA Modules:
  0.0 88.9 jit_solution(18249607055939535246)
XLA Ops:
  0.6 1.9 %pack_keys.1 = bf16[16,128,128]{2,1,0:T(8,128)(2,1)} custom-call(bf16[64,2048]{1,0:T(8,128)(2,1)} %key_ref.1, bf16[64,2048]{1,0:T(8,128)(2,1)} %value_ref.1), custom_call_target="tpu_custom_call" | custom-call | tf_op jit(solution)/shard_map/pack_keys/pallas_call | solution.py:47
  2.5 6.8 %all-to-all-start = ((bf16[8,2,128,128]{3,2,1,0:T(8,128)(2,1)}), bf16[8,2,128,128]{3,2,1,0:T(8,128)(2,1)S(1)}, u32[]{:S(2)}, u32[]{:S(2)}) async-start(bf16[8,2,128,128]{3,2,1,0:T(8,128)(2,1)} %bitcast.17), calls=%async_computation | async-start | bytes 1048576 | tf_op jit(solution)/shard_map/all_to_all | solution.py:321
  9.3 4.4 %pack_queries.1 = (bf16[8,264,128]{2,1,0:T(8,128)(2,1)}, bf16[8,264,128]{2,1,0:T(8,128)(2,1)}) custom-call(s32[1]{0:T(128)} %bitcast.core_ref, bf16[64,4096]{1,0:T(8,128)(2,1)} %query_ref.1, bf16[64,4096]{1,0:T(8,128)(2,1)} %grad_ref.1, bf16[64,4096]{1,0:T(8,128)(2,1)} %row_ref.1, f32[32,64]{1,0:T(8,128)} %lse_ref.1), custom_call_target="tpu_custom_call" | custom-call | tf_op jit(solution)/shard_map/pack_queries/pallas_call | solution.py:107
  13.7 2.9 %collective-permute-start = (bf16[8,264,128]{2,1,0:T(8,128)(2,1)}, bf16[8,264,128]{2,1,0:T(8,128)(2,1)S(1)}, u32[]{:S(2)}, u32[]{:S(2)}) collective-permute-start(bf16[8,264,128]{2,1,0:T(8,128)(2,1)} %get-tuple-element.17), channel_id=1, source_target_pairs={{0,8},{8,0},{1,9},{9,1},{2,10},{10,2},{3,11},{11,3},{4,12},{12,4},... | collective-permute-start | bytes 1622024 | tf_op jit(solution)/shard_map/ppermute | solution.py:325
  16.6 1.7 %collective-permute-done = bf16[8,264,128]{2,1,0:T(8,128)(2,1)S(1)} collective-permute-done((bf16[8,264,128]{2,1,0:T(8,128)(2,1)}, bf16[8,264,128]{2,1,0:T(8,128)(2,1)S(1)}, u32[]{:S(2)}, u32[]{:S(2)}) %collective-permute-start) | collective-permute-done | bytes 540704 | tf_op jit(solution)/shard_map/ppermute | solution.py:325
  18.4 2.1 %pad_maximum_fusion = bf16[8,2,264,128]{3,2,1,0:T(8,128)(2,1)} fusion(bf16[8,1,264,128]{3,2,1,0:T(8,128)(2,1)S(1)} %bitcast.19, bf16[8,1,264,128]{3,2,1,0:T(8,128)(2,1)} %bitcast.18), kind=kLoop, calls=%fused_computation.1 | loop fusion | flops 540672 | bytes 2162688 | tf_op jit(solution)/shard_map/stack | solution.py:346
  20.5 0.0 copy-start
  20.5 6.8 %all-to-all-done = bf16[8,2,128,128]{3,2,1,0:T(8,128)(2,1)S(1)} async-done(((bf16[8,2,128,128]{3,2,1,0:T(8,128)(2,1)}), bf16[8,2,128,128]{3,2,1,0:T(8,128)(2,1)S(1)}, u32[]{:S(2)}, u32[]{:S(2)}) %all-to-all-start) | async-done | bytes 524320 | tf_op jit(solution)/shard_map/all_to_all | solution.py:321
  27.3 3.6 %all-to-all-start.1 = ((bf16[8,2,264,128]{3,2,1,0:T(8,128)(2,1)}), bf16[8,2,264,128]{3,2,1,0:T(8,128)(2,1)S(1)}, u32[]{:S(2)}, u32[]{:S(2)}) async-start(bf16[8,2,264,128]{3,2,1,0:T(8,128)(2,1)} %pad_maximum_fusion), calls=%async_computation.1 | async-start | bytes 2162688 | tf_op jit(solution)/shard_map/all_to_all | solution.py:321
  30.9 0.0 copy-done
  30.9 0.1 select_bitcast_fusion
  31.0 4.0 %collective-permute-start.3 = (bf16[8,128,128]{2,1,0:T(8,128)(2,1)S(1)}, bf16[8,128,128]{2,1,0:T(8,128)(2,1)S(1)}, u32[]{:S(2)}, u32[]{:S(2)}) collective-permute-start(bf16[8,128,128]{2,1,0:T(8,128)(2,1)S(1)} %get-tuple-element.30.kv_near_ref), channel_id=1, source_target_pairs={{0,16},{8,24},{16,32},{24,40},{32,48},{40,56},{48,64},{56,72},{64,... | collective-permute-start | bytes 786440 | tf_op jit(solution)/shard_map/ppermute | solution.py:335
  35.0 1.0 %convert_reduce_fusion = s32[1024]{0:T(1024)S(1)} fusion(s32[1024]{0:T(1024)S(1)} %pad_dynamic-slice_fusion, s32[2048]{0:T(1024)S(1)} %pad_dynamic-slice_fusion.1), kind=kLoop, calls=%fused_computation | loop fusion | flops 6290432 | bytes 16384 | tf_op jit(solution)/shard_map/reduce_sum | solution.py:315
  36.0 4.7 %collective-permute-start.2 = (bf16[8,128,128]{2,1,0:T(8,128)(2,1)S(1)}, bf16[8,128,128]{2,1,0:T(8,128)(2,1)S(1)}, u32[]{:S(2)}, u32[]{:S(2)}) collective-permute-start(bf16[8,128,128]{2,1,0:T(8,128)(2,1)S(1)} %get-tuple-element.29), channel_id=1, source_target_pairs={{0,24},{8,16},{16,40},{24,32},{32,56},{40,48},{48,72},{56,64},{64,... | collective-permute-start | bytes 786440 | tf_op jit(solution)/shard_map/ppermute | solution.py:335
  40.7 1.9 %collective-permute-start.1 = (bf16[8,128,128]{2,1,0:T(8,128)(2,1)S(1)}, bf16[8,128,128]{2,1,0:T(8,128)(2,1)S(1)}, u32[]{:S(2)}, u32[]{:S(2)}) collective-permute-start(bf16[8,128,128]{2,1,0:T(8,128)(2,1)S(1)} %get-tuple-element.29), channel_id=1, source_target_pairs={{0,8},{8,0},{1,9},{9,1},{2,10},{10,2},{3,11},{11,3},{4,12},{12,4},... | collective-permute-start | bytes 786440 | tf_op jit(solution)/shard_map/ppermute | solution.py:325
  42.6 5.6 %collective-permute-done.3 = bf16[8,128,128]{2,1,0:T(8,128)(2,1)S(1)} collective-permute-done((bf16[8,128,128]{2,1,0:T(8,128)(2,1)S(1)}, bf16[8,128,128]{2,1,0:T(8,128)(2,1)S(1)}, u32[]{:S(2)}, u32[]{:S(2)}) %collective-permute-start.3) | collective-permute-done | bytes 262176 | tf_op jit(solution)/shard_map/ppermute | solution.py:335
  48.2 12.5 %all-to-all-done.1.q_ref = bf16[8,2,264,128]{3,2,1,0:T(8,128)(2,1)S(1)} async-done(((bf16[8,2,264,128]{3,2,1,0:T(8,128)(2,1)}), bf16[8,2,264,128]{3,2,1,0:T(8,128)(2,1)S(1)}, u32[]{:S(2)}, u32[]{:S(2)}) %all-to-all-start.1) | async-done | bytes 1081376 | tf_op jit(solution)/shard_map/all_to_all | solution.py:321
  60.7 2.9 %cross_near.1 = (f32[2,1024,128]{2,1,0:T(8,128)S(1)}, bf16[2,512,128]{2,1,0:T(8,128)(2,1)S(1)}) custom-call(s32[1]{0:T(128)} %bitcast.core_ref, bf16[8,1,128,128]{3,2,1,0:T(8,128)(2,1)S(1)} %bitcast.16, bf16[8,2,264,128]{3,2,1,0:T(8,128)(2,1)S(1)} %all-to-all-done.1.q_ref, s32[8,1,128]{2,1,0:T(1,128)S(1)} %add_maximum_fusion.lo_ref), custom_call_target="tpu_custom_call" | custom-call | flops 1342177280 | bytes 4194304 | tf_op jit(solution)/shard_map/cross_near/pallas_call | solution.py:245
  63.6 10.9 %collective-permute-start.4 = (bf16[2,512,128]{2,1,0:T(8,128)(2,1)S(1)}, bf16[2,512,128]{2,1,0:T(8,128)(2,1)S(1)}, u32[]{:S(2)}, u32[]{:S(2)}) collective-permute-start(bf16[2,512,128]{2,1,0:T(8,128)(2,1)S(1)} %get-tuple-element.22), channel_id=1, source_target_pairs={{16,0},{24,8},{32,16},{40,24},{48,32},{56,40},{64,48},{72,56},{80,... | collective-permute-start | bytes 786440 | tf_op jit(solution)/shard_map/ppermute | solution.py:335
  74.5 0.0 collective-permute-done.2
  74.6 1.4 %cross_far.1 = (f32[2,1024,128]{2,1,0:T(8,128)S(1)}, bf16[2,512,128]{2,1,0:T(8,128)(2,1)S(1)}) custom-call(s32[1]{0:T(128)} %bitcast.core_ref, bf16[8,1,128,128]{3,2,1,0:T(8,128)(2,1)S(1)} %bitcast.15, bf16[8,2,264,128]{3,2,1,0:T(8,128)(2,1)S(1)} %all-to-all-done.1.q_ref, s32[8,1,128]{2,1,0:T(1,128)S(1)} %add_maximum_fusion.lo_ref, ...), custom_call_target="tpu_custom_call" | custom-call | flops 1342177280 | bytes 4194304 | tf_op jit(solution)/shard_map/cross_far/pallas_call | solution.py:245
  76.0 3.0 %collective-permute-start.5 = (bf16[2,512,128]{2,1,0:T(8,128)(2,1)S(1)}, bf16[2,512,128]{2,1,0:T(8,128)(2,1)S(1)}, u32[]{:S(2)}, u32[]{:S(2)}) collective-permute-start(bf16[2,512,128]{2,1,0:T(8,128)(2,1)S(1)} %get-tuple-element.24), channel_id=1, source_target_pairs={{16,8},{24,0},{32,24},{40,16},{48,40},{56,32},{64,56},{72,48},{80,... | collective-permute-start | bytes 786440 | tf_op jit(solution)/shard_map/ppermute | solution.py:335
  79.0 0.0 collective-permute-done.1.kv_far_ref
  79.0 3.9 %own_terms.1 = bf16[2,4,512,128]{3,2,1,0:T(8,128)(2,1)S(1)} custom-call(s32[1]{0:T(128)} %bitcast.core_ref, bf16[8,128,128]{2,1,0:T(8,128)(2,1)S(1)} %get-tuple-element.30.kv_near_ref, bf16[8,128,128]{2,1,0:T(8,128)(2,1)S(1)} %collective-permute-done.1.kv_far_ref, bf16[8,2,264,128]{3,2,1,0:T(8,128)(2,1)S(1)} %all-to-all-done.1.q_ref, ...), custom_call_target="tpu_custom_call" | custom-call | flops 1342177280 | bytes 4194304 | tf_op jit(solution)/shard_map/own_terms/pallas_call | solution.py:261
  82.9 4.2 %all_to_all.15.own_ref = bf16[2,4,512,128]{3,2,1,0:T(8,128)(2,1)S(1)} all-to-all(bf16[2,4,512,128]{3,2,1,0:T(8,128)(2,1)S(1)} %own_terms.1), channel_id=1, replica_groups=mesh['chip'=32,'core'=2,'head'=8] {'core'}, dimensions={0} | all-to-all | bytes 2097152 | tf_op jit(solution)/shard_map/all_to_all | solution.py:359
  87.1 0.0 collective-permute-done.4.back_ref
  87.1 1.0 %join_near.1 = (bf16[512,512]{1,0:T(8,128)(2,1)}, bf16[512,256]{1,0:T(8,128)(2,1)S(1)}, bf16[512,256]{1,0:T(8,128)(2,1)S(1)}) custom-call(s32[1]{0:T(128)} %bitcast.core_ref, bf16[2,4,512,128]{3,2,1,0:T(8,128)(2,1)S(1)} %all_to_all.15.own_ref, bf16[2,512,128]{2,1,0:T(8,128)(2,1)S(1)} %collective-permute-done.4.back_ref), custom_call_target="tpu_custom_call" | custom-call | tf_op jit(solution)/shard_map/join_near/pallas_call | solution.py:301
  88.0 0.0 collective-permute-done.5.back_ref
  88.1 0.9 %join_far.1 = (bf16[512,256]{1,0:T(8,128)(2,1)}, bf16[512,256]{1,0:T(8,128)(2,1)}) custom-call(s32[1]{0:T(128)} %bitcast.core_ref, bf16[2,4,512,128]{3,2,1,0:T(8,128)(2,1)S(1)} %all_to_all.15.own_ref, bf16[2,512,128]{2,1,0:T(8,128)(2,1)S(1)} %collective-permute-done.5.back_ref, bf16[512,256]{1,0:T(8,128)(2,1)S(1)} %get-tuple-element.25.refs_0_, ...), custom_call_target="tpu_custom_call" | custom-call | tf_op jit(solution)/shard_map/join_far/pallas_call | solution.py:301
  (3 shorter events, 0.0 us)
Async XLA Ops:
  2.5 24.8 %all-to-all-start = ((bf16[8,2,128,128]{3,2,1,0:T(8,128)(2,1)}), bf16[8,2,128,128]{3,2,1,0:T(8,128)(2,1)S(1)}, u32[]{:S(2)}, u32[]{:S(2)}) async-start(bf16[8,2,128,128]{3,2,1,0:T(8,128)(2,1)} %bitcast.17), calls=%async_computation | async-start | bytes 1048576 | tf_op jit(solution)/shard_map/all_to_all | solution.py:321
  13.7 4.6 %collective-permute-start = (bf16[8,264,128]{2,1,0:T(8,128)(2,1)}, bf16[8,264,128]{2,1,0:T(8,128)(2,1)S(1)}, u32[]{:S(2)}, u32[]{:S(2)}) collective-permute-start(bf16[8,264,128]{2,1,0:T(8,128)(2,1)} %get-tuple-element.17), channel_id=1, source_target_pairs={{0,8},{8,0},{1,9},{9,1},{2,10},{10,2},{3,11},{11,3},{4,12},{12,4},... | collective-permute-start | bytes 1622024 | tf_op jit(solution)/shard_map/ppermute | solution.py:325
  20.5 10.4 %copy-start = (s32[32768]{0:T(1024)S(1)}, s32[32768]{0:T(1024)}, u32[]{:S(2)}) copy-start(s32[32768]{0:T(1024)} %param.13) | copy-start | bytes 393220
  27.3 33.5 %all-to-all-start.1 = ((bf16[8,2,264,128]{3,2,1,0:T(8,128)(2,1)}), bf16[8,2,264,128]{3,2,1,0:T(8,128)(2,1)S(1)}, u32[]{:S(2)}, u32[]{:S(2)}) async-start(bf16[8,2,264,128]{3,2,1,0:T(8,128)(2,1)} %pad_maximum_fusion), calls=%async_computation.1 | async-start | bytes 2162688 | tf_op jit(solution)/shard_map/all_to_all | solution.py:321
  31.0 17.2 %collective-permute-start.3 = (bf16[8,128,128]{2,1,0:T(8,128)(2,1)S(1)}, bf16[8,128,128]{2,1,0:T(8,128)(2,1)S(1)}, u32[]{:S(2)}, u32[]{:S(2)}) collective-permute-start(bf16[8,128,128]{2,1,0:T(8,128)(2,1)S(1)} %get-tuple-element.30.kv_near_ref), channel_id=1, source_target_pairs={{0,16},{8,24},{16,32},{24,40},{32,48},{40,56},{48,64},{56,72},{64,... | collective-permute-start | bytes 786440 | tf_op jit(solution)/shard_map/ppermute | solution.py:335
  36.0 38.5 %collective-permute-start.2 = (bf16[8,128,128]{2,1,0:T(8,128)(2,1)S(1)}, bf16[8,128,128]{2,1,0:T(8,128)(2,1)S(1)}, u32[]{:S(2)}, u32[]{:S(2)}) collective-permute-start(bf16[8,128,128]{2,1,0:T(8,128)(2,1)S(1)} %get-tuple-element.29), channel_id=1, source_target_pairs={{0,24},{8,16},{16,40},{24,32},{32,56},{40,48},{48,72},{56,64},{64,... | collective-permute-start | bytes 786440 | tf_op jit(solution)/shard_map/ppermute | solution.py:335
  40.7 38.3 %collective-permute-start.1 = (bf16[8,128,128]{2,1,0:T(8,128)(2,1)S(1)}, bf16[8,128,128]{2,1,0:T(8,128)(2,1)S(1)}, u32[]{:S(2)}, u32[]{:S(2)}) collective-permute-start(bf16[8,128,128]{2,1,0:T(8,128)(2,1)S(1)} %get-tuple-element.29), channel_id=1, source_target_pairs={{0,8},{8,0},{1,9},{9,1},{2,10},{10,2},{3,11},{11,3},{4,12},{12,4},... | collective-permute-start | bytes 786440 | tf_op jit(solution)/shard_map/ppermute | solution.py:325
  63.6 23.5 %collective-permute-start.4 = (bf16[2,512,128]{2,1,0:T(8,128)(2,1)S(1)}, bf16[2,512,128]{2,1,0:T(8,128)(2,1)S(1)}, u32[]{:S(2)}, u32[]{:S(2)}) collective-permute-start(bf16[2,512,128]{2,1,0:T(8,128)(2,1)S(1)} %get-tuple-element.22), channel_id=1, source_target_pairs={{16,0},{24,8},{32,16},{40,24},{48,32},{56,40},{64,48},{72,56},{80,... | collective-permute-start | bytes 786440 | tf_op jit(solution)/shard_map/ppermute | solution.py:335
  76.0 12.1 %collective-permute-start.5 = (bf16[2,512,128]{2,1,0:T(8,128)(2,1)S(1)}, bf16[2,512,128]{2,1,0:T(8,128)(2,1)S(1)}, u32[]{:S(2)}, u32[]{:S(2)}) collective-permute-start(bf16[2,512,128]{2,1,0:T(8,128)(2,1)S(1)} %get-tuple-element.24), channel_id=1, source_target_pairs={{16,8},{24,0},{32,24},{40,16},{48,40},{56,32},{64,56},{72,48},{80,... | collective-permute-start | bytes 786440 | tf_op jit(solution)/shard_map/ppermute | solution.py:335

commit v5 on v2

--- a/solution.py
+++ b/solution.py
@@ -12,7 +12,7 @@
 LOOKBACK_SPAN = 1024
 CORES = 2
 PIECE = 64
-META_ROWS = 16
+META_ROWS = 8
 CHUNK = 128
 
 score_scale = 168.0 ** (-0.5)
@@ -60,7 +60,7 @@
     return [high, middle, (rest - middle.astype(f32)).astype(bf16)]
 
 
-def pack_queries_kernel(parity_ref, query_ref, grad_ref, row_ref, lse_ref, out_ref):
+def pack_queries_kernel(query_ref, grad_ref, row_ref, lse_ref, out_ref):
     groups = out_ref.shape[1]
     receivers = CORES * groups
     heads = 2 * receivers
@@ -78,34 +78,45 @@
     member = jnp.where(which == lax.broadcasted_iota(jnp.int32, (heads, width), 0), 1.0, 0.0).astype(bf16)
     delta = dot_t(member, product_high) + dot_t(member, product_low)
     parts = three_parts(lse_ref[...]) + three_parts(delta)
-    rows = jnp.concatenate([p.astype(f32) for p in parts], axis=0)
-    rows = jnp.concatenate([rows, rows], axis=1)
-    lane = lax.broadcasted_iota(jnp.int32, rows.shape, 1) // PIECE
-    rows = jnp.where(lane == parity_ref[0], rows, 0.0).astype(bf16)
+    rows = jnp.concatenate([p.astype(f32) for p in parts], axis=0).astype(bf16)
     total = receivers * META_ROWS
     row_at = lax.broadcasted_iota(jnp.int32, (total, 6 * heads), 0)
     column_at = lax.broadcasted_iota(jnp.int32, (total, 6 * heads), 1)
     receiver = (row_at // META_ROWS) % groups * CORES + row_at // (META_ROWS * groups)
-    t = row_at % META_ROWS
-    source = ((t // 6) * 3 + t % 3) * heads + 2 * receiver + (t // 3) % 2
-    pick = jnp.where((t < 12) & (column_at == source), 1.0, 0.0).astype(bf16)
-    meta = dot_n(pick, rows).astype(bf16)
-    out_ref[:, :, 4 * PIECE : 4 * PIECE + META_ROWS, :] = meta.reshape(CORES, groups, META_ROWS, HEAD_SIZE)
-
-
-def pack_queries(parity, queries, grads, rows, lse, groups, steps=4):
+    halves = []
+    for half in range(2):
+        m = 2 * (row_at % META_ROWS) + half
+        source = ((m // 6) * 3 + m % 3) * heads + 2 * receiver + (m // 3) % 2
+        pick = jnp.where((m < 12) & (column_at == source), 1.0, 0.0).astype(bf16)
+        halves.append(dot_n(pick, rows))
+    meta = jnp.concatenate(halves, axis=1).reshape(CORES, groups, META_ROWS, HEAD_SIZE)
+    for core in range(CORES):
+        for group in range(groups):
+            out_ref[core, group, 4 * PIECE : 4 * PIECE + META_ROWS, :] = meta[core, group].astype(bf16)
+
+
+def pack_queries(queries, grads, rows, lse, groups, steps=4):
     width = queries.shape[1] // steps
     height = 4 * PIECE + META_ROWS
     return pl.pallas_call(
         pack_queries_kernel,
         grid=(steps,),
-        in_specs=[pl.BlockSpec(memory_space=pltpu.SMEM)]
-        + [pl.BlockSpec((PIECE, width), lambda i: (0, i))] * 3
+        in_specs=[pl.BlockSpec((PIECE, width), lambda i: (0, i))] * 3
         + [pl.BlockSpec((lse.shape[0] // steps, PIECE), lambda i: (i, 0))],
         out_specs=pl.BlockSpec((CORES, groups // steps, height, HEAD_SIZE), lambda i: (0, i, 0, 0)),
         out_shape=jax.ShapeDtypeStruct((CORES, groups, height, HEAD_SIZE), bf16),
         name="pack_queries",
-    )(parity, queries, grads, rows, lse)
+    )(queries, grads, rows, lse)
+
+
+def chunk_meta(ref, at):
+    meta = [ref[2 * at + i, 4 * PIECE : 4 * PIECE + META_ROWS, :].astype(f32) for i in range(2)]
+    turned = [pltpu.roll(m, PIECE, 1) for m in meta]
+    left = lax.broadcasted_iota(jnp.int32, meta[0].shape, 1) < PIECE
+    halves = (jnp.where(left, meta[0], turned[1]), jnp.where(left, turned[0], meta[1]))
+    pieces = [halves[m % 2][m // 2 : m // 2 + 1] for m in range(12)]
+    rows = [pieces[3 * r] + pieces[3 * r + 1] + pieces[3 * r + 2] for r in range(4)]
+    return jnp.concatenate(rows[0:2], axis=1), jnp.concatenate(rows[2:4], axis=1)
 
 
 def sweep(causal, key_base, kv_ref, q_ref, lo_ref, dk_ref, dv_ref, dq_ref, part_ref):
@@ -128,11 +139,8 @@
 
         query = both(0)
         grad = both(2)
-        meta = q_ref[sources, 4 * PIECE : 4 * PIECE + META_ROWS, :].astype(f32)
-        meta = meta[0] + meta[1]
-        rows = [meta[3 * r : 3 * r + 1] + meta[3 * r + 1 : 3 * r + 2] + meta[3 * r + 2 : 3 * r + 3] for r in range(4)]
-        lse = jnp.concatenate(rows[0:2], axis=1) * log2_e
-        delta = jnp.concatenate(rows[2:4], axis=1)
+        lse, delta = chunk_meta(q_ref, at)
+        lse = lse * log2_e
         lo = lo_ref[at] - (key_base + first * CHUNK)
         lo = jnp.concatenate([lo, lo], axis=1)
         key_at = lax.broadcasted_iota(jnp.int32, (height, 2 * CHUNK), 0)
@@ -171,14 +179,17 @@
     far_ref[1] = dv_ref[far, :].astype(bf16)
 
 
-def own_kernel(kv_ref, q_ref, lo_ref, part_ref, out_ref, dk_ref, dv_ref, dq_ref):
+def own_kernel(core_ref, kv_ref, q_ref, lo_ref, part_ref, near_dq_ref, near_ref, far_ref, dk_ref, dv_ref, dq_ref):
     sweep(True, LOOKBACK_SPAN, kv_ref, q_ref, lo_ref, dk_ref, dv_ref, dq_ref, part_ref)
-    for core in range(CORES):
-        block = slice(core * HALF, (core + 1) * HALF)
-        out_ref[core, 0] = dq_ref[0, block, :].astype(bf16)
-        out_ref[core, 1] = dq_ref[1, block, :].astype(bf16)
-        out_ref[core, 2] = dk_ref[block, :].astype(bf16)
-        out_ref[core, 3] = dv_ref[block, :].astype(bf16)
+    near = pl.ds(pl.multiple_of(core_ref[0] * HALF, HALF), HALF)
+    far = pl.ds(pl.multiple_of((1 - core_ref[0]) * HALF, HALF), HALF)
+    for a in range(2):
+        near_dq_ref[a] = dq_ref[a, near, :].astype(bf16)
+        far_ref[a] = dq_ref[a, far, :].astype(bf16)
+    near_ref[0] = dk_ref[near, :]
+    near_ref[1] = dv_ref[near, :]
+    far_ref[2] = dk_ref[far, :].astype(bf16)
+    far_ref[3] = dv_ref[far, :].astype(bf16)
 
 
 def vmem_spec():
@@ -218,49 +229,60 @@
     )(core, kv, q, lo)
 
 
-def own_terms(kv, q, lo, part):
+def own_terms(core, kv, q, lo, part):
     return pl.pallas_call(
         own_kernel,
-        in_specs=[vmem_spec()] * 4,
-        out_specs=vmem_spec(),
-        out_shape=jax.ShapeDtypeStruct((CORES, 4, HALF, HEAD_SIZE), bf16),
+        in_specs=[smem_spec()] + [vmem_spec()] * 4,
+        out_specs=[vmem_spec()] * 3,
+        out_shape=[
+            jax.ShapeDtypeStruct((2, HALF, HEAD_SIZE), bf16),
+            jax.ShapeDtypeStruct((2, HALF, HEAD_SIZE), f32),
+            jax.ShapeDtypeStruct((4, HALF, HEAD_SIZE), bf16),
+        ],
         scratch_shapes=SPAN_SCRATCH + [pltpu.VMEM((2, LOOKBACK_SPAN, HEAD_SIZE), f32)],
         compiler_params=pltpu.CompilerParams(vmem_limit_bytes=40 << 20),
         cost_estimate=cost(),
         name="own_terms",
-    )(kv, q, lo, part)
-
-
-def join_kernel(core_ref, own_ref, near_ref, far_ref, dq_ref, dk_ref, dv_ref):
-    for core in range(CORES):
-        for a in range(2):
-            at = 2 * core + a
-            dq_ref[:, at * HEAD_SIZE : (at + 1) * HEAD_SIZE] = own_ref[core, a]
-
+    )(core, kv, q, lo, part)
+
+
+def join_near_kernel(core_ref, near_ref, back_ref, dk_ref, dv_ref):
     for core in range(CORES):
 
         @pl.when(core_ref[0] == core)
         def _():
+            columns = slice(core * HEAD_SIZE, (core + 1) * HEAD_SIZE)
             for i, out_ref in enumerate((dk_ref, dv_ref)):
-                for k in range(CORES):
-                    back_ref = near_ref if k == core else far_ref
-                    total = own_ref[k, 2 + i].astype(f32) + back_ref[i].astype(f32)
-                    out_ref[:, k * HEAD_SIZE : (k + 1) * HEAD_SIZE] = total.astype(bf16)
-
-
-def join(core, own, back_near, back_far):
-    return pl.pallas_call(
-        join_kernel,
-        in_specs=[smem_spec()] + [vmem_spec()] * 3,
-        out_specs=[vmem_spec()] * 3,
-        out_shape=[
-            jax.ShapeDtypeStruct((HALF, 4 * HEAD_SIZE), bf16),
-            jax.ShapeDtypeStruct((HALF, 2 * HEAD_SIZE), bf16),
-            jax.ShapeDtypeStruct((HALF, 2 * HEAD_SIZE), bf16),
-        ],
+                out_ref[:, columns] = (near_ref[i] + back_ref[i].astype(f32)).astype(bf16)
+
+
+def join_far_kernel(core_ref, near_dq_ref, swapped_ref, back_ref, near_dk_ref, near_dv_ref, dq_ref, dk_ref, dv_ref):
+    for core in range(CORES):
+
+        @pl.when(core_ref[0] == core)
+        def _():
+            for a in range(2):
+                at = 2 * core + a
+                dq_ref[:, at * HEAD_SIZE : (at + 1) * HEAD_SIZE] = near_dq_ref[a]
+                at = 2 * (1 - core) + a
+                dq_ref[:, at * HEAD_SIZE : (at + 1) * HEAD_SIZE] = swapped_ref[a]
+            near = slice(core * HEAD_SIZE, (core + 1) * HEAD_SIZE)
+            far = slice((1 - core) * HEAD_SIZE, (2 - core) * HEAD_SIZE)
+            for i, (half_ref, out_ref) in enumerate(((near_dk_ref, dk_ref), (near_dv_ref, dv_ref))):
+                out_ref[:, near] = half_ref[:, near]
+                out_ref[:, far] = (swapped_ref[2 + i].astype(f32) + back_ref[i].astype(f32)).astype(bf16)
+
+
+def join(kernel, name, shapes, steps, *operands):
+    return pl.pallas_call(
+        kernel,
+        in_specs=[smem_spec()] + [vmem_spec()] * (len(operands) - 1),
+        out_specs=[vmem_spec()] * len(shapes),
+        out_shape=shapes,
         compiler_params=pltpu.CompilerParams(vmem_limit_bytes=16 << 20),
-        name="join",
-    )(core, own, back_near, back_far)
+        cost_estimate=pl.CostEstimate(flops=steps << 20, transcendentals=0, bytes_accessed=1 << 20),
+        name=name,
+    )(*operands)
 
 
 def first_allowed(doc_ids, chip):
@@ -282,10 +304,9 @@
     groups = lax.axis_size("head")
     chip = lax.axis_index("chip")
     core = lax.axis_index("core").astype(jnp.int32).reshape(1)
-    parity = (lax.axis_index("head") % 2).astype(jnp.int32).reshape(1)
     lo = first_allowed(doc_ids, chip)
     kv = exchange(pack_keys(keys, values, groups))
-    packed = pack_queries(parity, queries, grads, rows, lse, groups)
+    packed = pack_queries(queries, grads, rows, lse, groups)
     kv, packed = lax.optimization_barrier((kv, packed))
     q = exchange(packed)
     kv_before = lax.ppermute(kv, "chip", [(c, c + 1) for c in range(chips - 1)])
@@ -296,9 +317,17 @@
         ("chip", "core"),
         [(CORES * (c + 1) + k, CORES * c + 1 - k) for c in range(chips - 1) for k in range(CORES)],
     )
-    own = own_terms(kv, q, lo, dq_part)
-    own = lax.all_to_all(own, "core", split_axis=0, concat_axis=0, tiled=True)
-    return join(core, own, back_near, back_far)
+    near_dq, own_near, own_far = own_terms(core, kv, q, lo, dq_part)
+    swapped = lax.ppermute(own_far, "core", [(0, 1), (1, 0)])
+    keys_shape = jax.ShapeDtypeStruct((HALF, 2 * HEAD_SIZE), bf16)
+    queries_shape = jax.ShapeDtypeStruct((HALF, 4 * HEAD_SIZE), bf16)
+    halves = join(join_near_kernel, "join_near", [keys_shape] * 2, 10000, core, own_near, back_near)
+    return tuple(
+        join(
+            join_far_kernel, "join_far", [queries_shape, keys_shape, keys_shape], 1,
+            core, near_dq, swapped, back_far, *halves,
+        )
+    )
 
 
 def solution(mesh):

time: 86.4 us -> 85.7 us (level)
  blocking collectives: 4.5 us -> 0 us
  starting transfers between devices: 30.6 us -> 32.8 us
  waiting for transfers between devices: 34.1 us -> 35.6 us
    all_to_all x1 -> x0, blocking collectives: 4.5 us -> none  [on_device(): own = lax.all_to_all(own, 'core', split_axis=0, concat_axis=0, tiled=True)]
    ppermute x0 -> x1, starting transfers between devices: none -> 2.25 us  [on_device(): swapped = lax.ppermute(own_far, 'core', [(0, 1), (1, 0)])]
    ppermute x1, waiting for transfers between devices: 0.76 us -> 2.97 us  [on_device(): lax.ppermute(far, ('chip', 'core'), [(CORES * (c + 1) + k, CORES * c + 1...]
    pallas_call x2 -> x3, Pallas kernels: 5.05 us -> 5.12 us  [the longest x1 3.89 us: own_terms(): pl.pallas_call(own_kernel, in_specs=[smem_spec()] + [vmem_spec()] * 4, ou...]
  transfers between devices with their start and end apart: 5 -> 6, of which waited for: 4 -> 4; matrix products, arithmetic and copies ran while one was open for 1% -> 1% of each run, Pallas kernels for 9% -> 10%
where the time goes in v5:
time: 85.7 us; the launch traced here: 85.2 us
  waiting for transfers between devices  35.6 us (42%)
  starting transfers between devices  32.8 us (38%)
  Pallas kernels  15 us (18%)
  other arithmetic  0.99 us (1%)
    ppermute x1, waiting for transfers between devices, on_device(): kv_before = lax.ppermute(kv, 'chip', [(c, c + 1) for c in range(chips - 1)])  18.1 us
    all_to_all x2, waiting for transfers between devices, exchange(): lax.all_to_all(value, ('core', 'head'), split_axis=0, concat_axis=0, tile...  14.6 us
    all_to_all x2, starting transfers between devices, exchange(): lax.all_to_all(value, ('core', 'head'), split_axis=0, concat_axis=0, tile...  13.4 us
    ppermute x1, starting transfers between devices, on_device(): lax.ppermute(near, 'chip', [(c + 1, c) for c in range(chips - 1)])  10.9 us
    pallas_call x1, Pallas kernels, pack_queries(): pl.pallas_call(pack_queries_kernel, grid=(steps,), in_specs=[pl.BlockSpec...  4.27 us
    ppermute x1, starting transfers between devices, on_device(): kv_before = lax.ppermute(kv, 'chip', [(c, c + 1) for c in range(chips - 1)])  4.03 us
    pallas_call x1, Pallas kernels, own_terms(): pl.pallas_call(own_kernel, in_specs=[smem_spec()] + [vmem_spec()] * 4, ou...  3.89 us
    pallas_call x1, Pallas kernels, cross_terms(): pl.pallas_call(cross_kernel, in_specs=[smem_spec()] + [vmem_spec()] * 3,...  3.76 us
  transfers between devices with their start and end apart: 6, of which 4 were waited for; matrix products, arithmetic and copies ran while one was open for 1% of the time, Pallas kernels for 10%

profile of v5, /device:TPU:7, one launch (start us, length us, event | category | flops | bytes accessed | tf_op | source)
XLA Modules:
  0.0 85.2 jit_solution(6848784143978328522)
XLA Ops:
  0.6 1.9 %pack_keys.1 = bf16[2,8,128,128]{3,2,1,0:T(8,128)(2,1)} custom-call(bf16[64,2048]{1,0:T(8,128)(2,1)} %key_ref.1, bf16[64,2048]{1,0:T(8,128)(2,1)} %value_ref.1), custom_call_target="tpu_custom_call" | custom-call | tf_op jit(solution)/shard_map/pack_keys/pallas_call | solution.py:46
  2.5 7.8 %all-to-all-start = ((bf16[16,128,128]{2,1,0:T(8,128)(2,1)}), bf16[16,128,128]{2,1,0:T(8,128)(2,1)S(1)}, u32[]{:S(2)}, u32[]{:S(2)}) async-start(bf16[16,128,128]{2,1,0:T(8,128)(2,1)} %bitcast.5), calls=%async_computation | async-start | bytes 1048576 | tf_op jit(solution)/shard_map/all_to_all | solution.py:299
  10.3 4.3 %pack_queries.1 = bf16[2,8,264,128]{3,2,1,0:T(8,128)(2,1)} custom-call(bf16[64,4096]{1,0:T(8,128)(2,1)} %query_ref.1, bf16[64,4096]{1,0:T(8,128)(2,1)} %grad_ref.1, bf16[64,4096]{1,0:T(8,128)(2,1)} %row_ref.1, f32[32,64]{1,0:T(8,128)} %lse_ref.1), custom_call_target="tpu_custom_call" | custom-call | tf_op jit(solution)/shard_map/pack_queries/pallas_call | solution.py:101
  14.6 10.5 %all-to-all-done.kv_ref = bf16[16,128,128]{2,1,0:T(8,128)(2,1)S(1)} async-done(((bf16[16,128,128]{2,1,0:T(8,128)(2,1)}), bf16[16,128,128]{2,1,0:T(8,128)(2,1)S(1)}, u32[]{:S(2)}, u32[]{:S(2)}) %all-to-all-start) | async-done | bytes 524320 | tf_op jit(solution)/shard_map/all_to_all | solution.py:299
  25.1 0.0 copy-start
  25.1 5.6 %all-to-all-start.1 = ((bf16[16,264,128]{2,1,0:T(8,128)(2,1)}), bf16[16,264,128]{2,1,0:T(8,128)(2,1)S(1)}, u32[]{:S(2)}, u32[]{:S(2)}) async-start(bf16[16,264,128]{2,1,0:T(8,128)(2,1)} %bitcast.4), calls=%async_computation.1 | async-start | bytes 2162688 | tf_op jit(solution)/shard_map/all_to_all | solution.py:299
  30.6 0.0 copy-done
  30.7 4.0 %collective-permute-start = (bf16[16,128,128]{2,1,0:T(8,128)(2,1)S(1)}, bf16[16,128,128]{2,1,0:T(8,128)(2,1)S(1)}, u32[]{:S(2)}, u32[]{:S(2)}) collective-permute-start(bf16[16,128,128]{2,1,0:T(8,128)(2,1)S(1)} %all-to-all-done.kv_ref), channel_id=1, source_target_pairs={{0,16},{16,32},{32,48},{48,64},{64,80},{80,96},{96,112},{112,128},... | collective-permute-start | bytes 1572872 | tf_op jit(solution)/shard_map/ppermute | solution.py:312
  34.7 1.0 %convert_reduce_fusion = s32[1024]{0:T(1024)S(1)} fusion(s32[1024]{0:T(1024)S(1)} %pad_dynamic-slice_fusion, s32[2048]{0:T(1024)S(1)} %pad_dynamic-slice_fusion.1), kind=kLoop, calls=%fused_computation | loop fusion | flops 6290432 | bytes 16384 | tf_op jit(solution)/shard_map/reduce_sum | solution.py:292
  35.7 18.1 %collective-permute-done.kv_ref = bf16[16,128,128]{2,1,0:T(8,128)(2,1)S(1)} collective-permute-done((bf16[16,128,128]{2,1,0:T(8,128)(2,1)S(1)}, bf16[16,128,128]{2,1,0:T(8,128)(2,1)S(1)}, u32[]{:S(2)}, u32[]{:S(2)}) %collective-permute-start) | collective-permute-done | bytes 524320 | tf_op jit(solution)/shard_map/ppermute | solution.py:312
  53.8 4.1 %all-to-all-done.1.q_ref = bf16[16,264,128]{2,1,0:T(8,128)(2,1)S(1)} async-done(((bf16[16,264,128]{2,1,0:T(8,128)(2,1)}), bf16[16,264,128]{2,1,0:T(8,128)(2,1)S(1)}, u32[]{:S(2)}, u32[]{:S(2)}) %all-to-all-start.1) | async-done | bytes 1081376 | tf_op jit(solution)/shard_map/all_to_all | solution.py:299
  57.9 3.8 %cross_terms.1 = (f32[2,1024,128]{2,1,0:T(8,128)S(1)}, bf16[2,512,128]{2,1,0:T(8,128)(2,1)S(1)}, bf16[2,512,128]{2,1,0:T(8,128)(2,1)S(1)}) custom-call(s32[1]{0:T(128)} %bitcast.core_ref, bf16[16,128,128]{2,1,0:T(8,128)(2,1)S(1)} %collective-permute-done.kv_ref, bf16[16,264,128]{2,1,0:T(8,128)(2,1)S(1)} %all-to-all-done.1.q_ref, ...), custom_call_target="tpu_custom_call" | custom-call | flops 1342177280 | bytes 4194304 | tf_op jit(solution)/shard_map/cross_terms/pallas_call | solution.py:216
  61.7 10.9 %collective-permute-start.3 = (bf16[2,512,128]{2,1,0:T(8,128)(2,1)S(1)}, bf16[2,512,128]{2,1,0:T(8,128)(2,1)S(1)}, u32[]{:S(2)}, u32[]{:S(2)}) collective-permute-start(bf16[2,512,128]{2,1,0:T(8,128)(2,1)S(1)} %get-tuple-element.20), channel_id=1, source_target_pairs={{16,0},{32,16},{48,32},{64,48},{80,64},{96,80},{112,96},{128,112},... | collective-permute-start | bytes 786440 | tf_op jit(solution)/shard_map/ppermute | solution.py:314
  72.6 2.2 %collective-permute-start.2 = (bf16[2,512,128]{2,1,0:T(8,128)(2,1)S(1)}, bf16[2,512,128]{2,1,0:T(8,128)(2,1)S(1)}, u32[]{:S(2)}, u32[]{:S(2)}) collective-permute-start(bf16[2,512,128]{2,1,0:T(8,128)(2,1)S(1)} %get-tuple-element.18), channel_id=1, source_target_pairs={{16,8},{24,0},{32,24},{40,16},{48,40},{56,32},{64,56},{72,48},{80,... | collective-permute-start | bytes 786440 | tf_op jit(solution)/shard_map/ppermute | solution.py:315
  74.8 3.9 %own_terms.1 = (bf16[2,512,128]{2,1,0:T(8,128)(2,1)S(1)}, f32[2,512,128]{2,1,0:T(8,128)S(1)}, bf16[4,512,128]{2,1,0:T(8,128)(2,1)S(1)}) custom-call(s32[1]{0:T(128)} %bitcast.core_ref, bf16[16,128,128]{2,1,0:T(8,128)(2,1)S(1)} %all-to-all-done.kv_ref, bf16[16,264,128]{2,1,0:T(8,128)(2,1)S(1)} %all-to-all-done.1.q_ref, ...), custom_call_target="tpu_custom_call" | custom-call | flops 1342177280 | bytes 4194304 | tf_op jit(solution)/shard_map/own_terms/pallas_call | solution.py:233
  78.7 2.2 %collective-permute-start.1 = (bf16[4,512,128]{2,1,0:T(8,128)(2,1)S(1)}, bf16[4,512,128]{2,1,0:T(8,128)(2,1)S(1)}, u32[]{:S(2)}, u32[]{:S(2)}) collective-permute-start(bf16[4,512,128]{2,1,0:T(8,128)(2,1)S(1)} %get-tuple-element.17), channel_id=1, source_target_pairs={{0,8},{8,0},{1,9},{9,1},{2,10},{10,2},{3,11},{11,3},{4,12},{12,4},... | collective-permute-start | bytes 1572872 | tf_op jit(solution)/shard_map/ppermute | solution.py:321
  81.0 0.0 collective-permute-done.3.back_ref
  81.0 0.1 join_near.1
  81.1 3.0 %collective-permute-done.2.back_ref = bf16[2,512,128]{2,1,0:T(8,128)(2,1)S(1)} collective-permute-done((bf16[2,512,128]{2,1,0:T(8,128)(2,1)S(1)}, bf16[2,512,128]{2,1,0:T(8,128)(2,1)S(1)}, u32[]{:S(2)}, u32[]{:S(2)}) %collective-permute-start.2) | collective-permute-done | bytes 262176 | tf_op jit(solution)/shard_map/ppermute | solution.py:315
  84.1 0.0 collective-permute-done.1.swapped_ref
  84.1 1.2 %join_far.1 = (bf16[512,512]{1,0:T(8,128)(2,1)}, bf16[512,256]{1,0:T(8,128)(2,1)}, bf16[512,256]{1,0:T(8,128)(2,1)}) custom-call(s32[1]{0:T(128)} %bitcast.core_ref, bf16[2,512,128]{2,1,0:T(8,128)(2,1)S(1)} %get-tuple-element.16.near_dq_ref, bf16[4,512,128]{2,1,0:T(8,128)(2,1)S(1)} %collective-permute-done.1.swapped_ref, ...), custom_call_target="tpu_custom_call" | custom-call | flops 1048576 | bytes 1048576 | tf_op jit(solution)/shard_map/join_far/pallas_call | solution.py:277
  (3 shorter events, 0.0 us)
Async XLA Ops:
  2.5 22.6 %all-to-all-start = ((bf16[16,128,128]{2,1,0:T(8,128)(2,1)}), bf16[16,128,128]{2,1,0:T(8,128)(2,1)S(1)}, u32[]{:S(2)}, u32[]{:S(2)}) async-start(bf16[16,128,128]{2,1,0:T(8,128)(2,1)} %bitcast.5), calls=%async_computation | async-start | bytes 1048576 | tf_op jit(solution)/shard_map/all_to_all | solution.py:299
  25.1 5.6 %copy-start = (s32[32768]{0:T(1024)S(1)}, s32[32768]{0:T(1024)}, u32[]{:S(2)}) copy-start(s32[32768]{0:T(1024)} %param.13) | copy-start | bytes 393220
  25.1 32.8 %all-to-all-start.1 = ((bf16[16,264,128]{2,1,0:T(8,128)(2,1)}), bf16[16,264,128]{2,1,0:T(8,128)(2,1)S(1)}, u32[]{:S(2)}, u32[]{:S(2)}) async-start(bf16[16,264,128]{2,1,0:T(8,128)(2,1)} %bitcast.4), calls=%async_computation.1 | async-start | bytes 2162688 | tf_op jit(solution)/shard_map/all_to_all | solution.py:299
  30.7 23.1 %collective-permute-start = (bf16[16,128,128]{2,1,0:T(8,128)(2,1)S(1)}, bf16[16,128,128]{2,1,0:T(8,128)(2,1)S(1)}, u32[]{:S(2)}, u32[]{:S(2)}) collective-permute-start(bf16[16,128,128]{2,1,0:T(8,128)(2,1)S(1)} %all-to-all-done.kv_ref), channel_id=1, source_target_pairs={{0,16},{16,32},{32,48},{48,64},{64,80},{80,96},{96,112},{112,128},... | collective-permute-start | bytes 1572872 | tf_op jit(solution)/shard_map/ppermute | solution.py:312
  61.7 19.3 %collective-permute-start.3 = (bf16[2,512,128]{2,1,0:T(8,128)(2,1)S(1)}, bf16[2,512,128]{2,1,0:T(8,128)(2,1)S(1)}, u32[]{:S(2)}, u32[]{:S(2)}) collective-permute-start(bf16[2,512,128]{2,1,0:T(8,128)(2,1)S(1)} %get-tuple-element.20), channel_id=1, source_target_pairs={{16,0},{32,16},{48,32},{64,48},{80,64},{96,80},{112,96},{128,112},... | collective-permute-start | bytes 786440 | tf_op jit(solution)/shard_map/ppermute | solution.py:314
  72.6 11.5 %collective-permute-start.2 = (bf16[2,512,128]{2,1,0:T(8,128)(2,1)S(1)}, bf16[2,512,128]{2,1,0:T(8,128)(2,1)S(1)}, u32[]{:S(2)}, u32[]{:S(2)}) collective-permute-start(bf16[2,512,128]{2,1,0:T(8,128)(2,1)S(1)} %get-tuple-element.18), channel_id=1, source_target_pairs={{16,8},{24,0},{32,24},{40,16},{48,40},{56,32},{64,56},{72,48},{80,... | collective-permute-start | bytes 786440 | tf_op jit(solution)/shard_map/ppermute | solution.py:315
  78.7 5.3 %collective-permute-start.1 = (bf16[4,512,128]{2,1,0:T(8,128)(2,1)S(1)}, bf16[4,512,128]{2,1,0:T(8,128)(2,1)S(1)}, u32[]{:S(2)}, u32[]{:S(2)}) collective-permute-start(bf16[4,512,128]{2,1,0:T(8,128)(2,1)S(1)} %get-tuple-element.17), channel_id=1, source_target_pairs={{0,8},{8,0},{1,9},{9,1},{2,10},{10,2},{3,11},{11,3},{4,12},{12,4},... | collective-permute-start | bytes 1572872 | tf_op jit(solution)/shard_map/ppermute | solution.py:321

commit v6 on v5

--- a/solution.py
+++ b/solution.py
@@ -168,28 +168,38 @@
             dq_ref[a, at * CHUNK : (at + 1) * CHUNK, :] = mine
 
 
-def cross_kernel(core_ref, kv_ref, q_ref, lo_ref, dq_ref, near_ref, far_ref, dk_ref, dv_ref):
+def cross_kernel(kv_ref, q_ref, lo_ref, dq_ref, back_ref, dk_ref, dv_ref):
     sweep(False, 0, kv_ref, q_ref, lo_ref, dk_ref, dv_ref, dq_ref, None)
-    half = LOOKBACK_SPAN // CORES
-    near = pl.ds(pl.multiple_of(core_ref[0] * half, half), half)
-    far = pl.ds(pl.multiple_of((1 - core_ref[0]) * half, half), half)
-    near_ref[0] = dk_ref[near, :].astype(bf16)
-    near_ref[1] = dv_ref[near, :].astype(bf16)
-    far_ref[0] = dk_ref[far, :].astype(bf16)
-    far_ref[1] = dv_ref[far, :].astype(bf16)
-
-
-def own_kernel(core_ref, kv_ref, q_ref, lo_ref, part_ref, near_dq_ref, near_ref, far_ref, dk_ref, dv_ref, dq_ref):
-    sweep(True, LOOKBACK_SPAN, kv_ref, q_ref, lo_ref, dk_ref, dv_ref, dq_ref, part_ref)
+    back_ref[0] = dk_ref[...].astype(bf16)
+    back_ref[1] = dv_ref[...].astype(bf16)
+
+
+def own_kernel(kv_ref, q_ref, lo_ref, part_ref, dq_ref, sums_ref, sum_ref):
+    sweep(True, LOOKBACK_SPAN, kv_ref, q_ref, lo_ref, sums_ref.at[0], sums_ref.at[1], sum_ref, part_ref)
+    dq_ref[...] = sum_ref[...].astype(bf16)
+
+
+def finish_kernel(core_ref, dq_ref, sums_ref, back_ref, near_ref, far_ref):
     near = pl.ds(pl.multiple_of(core_ref[0] * HALF, HALF), HALF)
     far = pl.ds(pl.multiple_of((1 - core_ref[0]) * HALF, HALF), HALF)
-    for a in range(2):
-        near_dq_ref[a] = dq_ref[a, near, :].astype(bf16)
-        far_ref[a] = dq_ref[a, far, :].astype(bf16)
-    near_ref[0] = dk_ref[near, :]
-    near_ref[1] = dv_ref[near, :]
-    far_ref[2] = dk_ref[far, :].astype(bf16)
-    far_ref[3] = dv_ref[far, :].astype(bf16)
+    for i in range(2):
+        near_ref[i] = dq_ref[i, near, :]
+        far_ref[i] = dq_ref[i, far, :]
+        for rows, out_ref in ((near, near_ref), (far, far_ref)):
+            out_ref[2 + i] = (sums_ref[i, rows, :] + back_ref[i, rows, :].astype(f32)).astype(bf16)
+
+
+def join_kernel(core_ref, near_ref, far_ref, dq_ref, dk_ref, dv_ref):
+    for core in range(CORES):
+
+        @pl.when(core_ref[0] == core)
+        def _():
+            for half_ref, k in ((near_ref, core), (far_ref, 1 - core)):
+                for a in range(2):
+                    at = 2 * k + a
+                    dq_ref[:, at * HEAD_SIZE : (at + 1) * HEAD_SIZE] = half_ref[a]
+                dk_ref[:, k * HEAD_SIZE : (k + 1) * HEAD_SIZE] = half_ref[2]
+                dv_ref[:, k * HEAD_SIZE : (k + 1) * HEAD_SIZE] = half_ref[3]
 
 
 def vmem_spec():
@@ -200,10 +210,6 @@
     return pl.BlockSpec(memory_space=pltpu.SMEM)
 
 
-SPAN_SCRATCH = [
-    pltpu.VMEM((LOOKBACK_SPAN, HEAD_SIZE), f32),
-    pltpu.VMEM((LOOKBACK_SPAN, HEAD_SIZE), f32),
-]
 HALF = LOOKBACK_SPAN // CORES
 
 
@@ -212,77 +218,38 @@
     return pl.CostEstimate(flops=pairs * 5 * 2 * HEAD_SIZE, transcendentals=pairs, bytes_accessed=4 << 20)
 
 
-def cross_terms(core, kv, q, lo):
-    return pl.pallas_call(
-        cross_kernel,
-        in_specs=[smem_spec()] + [vmem_spec()] * 3,
-        out_specs=[vmem_spec()] * 3,
-        out_shape=[
-            jax.ShapeDtypeStruct((2, LOOKBACK_SPAN, HEAD_SIZE), f32),
-            jax.ShapeDtypeStruct((2, HALF, HEAD_SIZE), bf16),
-            jax.ShapeDtypeStruct((2, HALF, HEAD_SIZE), bf16),
-        ],
-        scratch_shapes=SPAN_SCRATCH,
-        compiler_params=pltpu.CompilerParams(vmem_limit_bytes=40 << 20),
-        cost_estimate=cost(),
-        name="cross_terms",
-    )(core, kv, q, lo)
-
-
-def own_terms(core, kv, q, lo, part):
-    return pl.pallas_call(
-        own_kernel,
-        in_specs=[smem_spec()] + [vmem_spec()] * 4,
-        out_specs=[vmem_spec()] * 3,
-        out_shape=[
-            jax.ShapeDtypeStruct((2, HALF, HEAD_SIZE), bf16),
-            jax.ShapeDtypeStruct((2, HALF, HEAD_SIZE), f32),
-            jax.ShapeDtypeStruct((4, HALF, HEAD_SIZE), bf16),
-        ],
-        scratch_shapes=SPAN_SCRATCH + [pltpu.VMEM((2, LOOKBACK_SPAN, HEAD_SIZE), f32)],
-        compiler_params=pltpu.CompilerParams(vmem_limit_bytes=40 << 20),
-        cost_estimate=cost(),
-        name="own_terms",
-    )(core, kv, q, lo, part)
-
-
-def join_near_kernel(core_ref, near_ref, back_ref, dk_ref, dv_ref):
-    for core in range(CORES):
-
-        @pl.when(core_ref[0] == core)
-        def _():
-            columns = slice(core * HEAD_SIZE, (core + 1) * HEAD_SIZE)
-            for i, out_ref in enumerate((dk_ref, dv_ref)):
-                out_ref[:, columns] = (near_ref[i] + back_ref[i].astype(f32)).astype(bf16)
-
-
-def join_far_kernel(core_ref, near_dq_ref, swapped_ref, back_ref, near_dk_ref, near_dv_ref, dq_ref, dk_ref, dv_ref):
-    for core in range(CORES):
-
-        @pl.when(core_ref[0] == core)
-        def _():
-            for a in range(2):
-                at = 2 * core + a
-                dq_ref[:, at * HEAD_SIZE : (at + 1) * HEAD_SIZE] = near_dq_ref[a]
-                at = 2 * (1 - core) + a
-                dq_ref[:, at * HEAD_SIZE : (at + 1) * HEAD_SIZE] = swapped_ref[a]
-            near = slice(core * HEAD_SIZE, (core + 1) * HEAD_SIZE)
-            far = slice((1 - core) * HEAD_SIZE, (2 - core) * HEAD_SIZE)
-            for i, (half_ref, out_ref) in enumerate(((near_dk_ref, dk_ref), (near_dv_ref, dv_ref))):
-                out_ref[:, near] = half_ref[:, near]
-                out_ref[:, far] = (swapped_ref[2 + i].astype(f32) + back_ref[i].astype(f32)).astype(bf16)
-
-
-def join(kernel, name, shapes, steps, *operands):
+def whole_call(kernel, name, shapes, operands, scratch=(), estimate=None, smem=0):
     return pl.pallas_call(
         kernel,
-        in_specs=[smem_spec()] + [vmem_spec()] * (len(operands) - 1),
+        in_specs=[smem_spec()] * smem + [vmem_spec()] * (len(operands) - smem),
         out_specs=[vmem_spec()] * len(shapes),
-        out_shape=shapes,
+        out_shape=[jax.ShapeDtypeStruct(shape, kind) for shape, kind in shapes],
+        scratch_shapes=scratch,
         compiler_params=pltpu.CompilerParams(vmem_limit_bytes=16 << 20),
-        cost_estimate=pl.CostEstimate(flops=steps << 20, transcendentals=0, bytes_accessed=1 << 20),
+        cost_estimate=estimate,
         name=name,
     )(*operands)
+
+
+def cross_terms(kv, q, lo):
+    shapes = [((2, LOOKBACK_SPAN, HEAD_SIZE), f32), ((2, LOOKBACK_SPAN, HEAD_SIZE), bf16)]
+    scratch = [pltpu.VMEM((LOOKBACK_SPAN, HEAD_SIZE), f32)] * 2
+    return whole_call(cross_kernel, "cross_terms", shapes, (kv, q, lo), scratch, cost())
+
+
+def own_terms(kv, q, lo, part):
+    shapes = [((2, LOOKBACK_SPAN, HEAD_SIZE), bf16), ((2, LOOKBACK_SPAN, HEAD_SIZE), f32)]
+    scratch = [pltpu.VMEM((2, LOOKBACK_SPAN, HEAD_SIZE), f32)]
+    return whole_call(own_kernel, "own_terms", shapes, (kv, q, lo, part), scratch, cost())
+
+
+def finish(core, dq, sums, back):
+    return whole_call(finish_kernel, "finish", [((4, HALF, HEAD_SIZE), bf16)] * 2, (core, dq, sums, back), smem=1)
+
+
+def join(core, near, far):
+    shapes = [((HALF, heads * HEAD_SIZE), bf16) for heads in (4, 2, 2)]
+    return whole_call(join_kernel, "join", shapes, (core, near, far), smem=1)
 
 
 def first_allowed(doc_ids, chip):
@@ -310,24 +277,12 @@
     kv, packed = lax.optimization_barrier((kv, packed))
     q = exchange(packed)
     kv_before = lax.ppermute(kv, "chip", [(c, c + 1) for c in range(chips - 1)])
-    dq_part, near, far = cross_terms(core, kv_before, q, lo)
-    back_near = lax.ppermute(near, "chip", [(c + 1, c) for c in range(chips - 1)])
-    back_far = lax.ppermute(
-        far,
-        ("chip", "core"),
-        [(CORES * (c + 1) + k, CORES * c + 1 - k) for c in range(chips - 1) for k in range(CORES)],
-    )
-    near_dq, own_near, own_far = own_terms(core, kv, q, lo, dq_part)
-    swapped = lax.ppermute(own_far, "core", [(0, 1), (1, 0)])
-    keys_shape = jax.ShapeDtypeStruct((HALF, 2 * HEAD_SIZE), bf16)
-    queries_shape = jax.ShapeDtypeStruct((HALF, 4 * HEAD_SIZE), bf16)
-    halves = join(join_near_kernel, "join_near", [keys_shape] * 2, 10000, core, own_near, back_near)
-    return tuple(
-        join(
-            join_far_kernel, "join_far", [queries_shape, keys_shape, keys_shape], 1,
-            core, near_dq, swapped, back_far, *halves,
-        )
-    )
+    dq_part, back = cross_terms(kv_before, q, lo)
+    back = lax.ppermute(back, "chip", [(c + 1, c) for c in range(chips - 1)])
+    dq, sums = own_terms(kv, q, lo, dq_part)
+    near, far = finish(core, dq, sums, back)
+    far = lax.ppermute(far, "core", [(0, 1), (1, 0)])
+    return tuple(join(core, near, far))
 
 
 def solution(mesh):

time: 85.7 us -> 90.8 us (1.060)
  waiting for transfers between devices: 35.6 us -> 40.6 us
  local copies, waits for them, and re-layouts: 0.03 us -> 2.22 us
  starting transfers between devices: 32.8 us -> 30.9 us
    ppermute x3 -> x2, waiting for transfers between devices: 2.97 us -> 7.89 us  [the longest x1 6.38 us: on_device(): back = lax.ppermute(back, 'chip', [(c + 1, c) for c in range(chips - 1)])]
    unnamed x2 -> x6, local copies, waits for them, and re-layouts: 0.01 us -> 2.19 us
    ppermute x3 -> x2, starting transfers between devices: 15.4 us -> 13.5 us  [the longest x1 10.9 us: on_device(): back = lax.ppermute(back, 'chip', [(c + 1, c) for c in range(chips - 1)])]
  transfers between devices with their start and end apart: 6 -> 5, of which waited for: 4 -> 5; matrix products, arithmetic and copies ran while one was open for 1% -> 1% of each run, Pallas kernels for 10% -> 9%
where the time goes in v6:
time: 90.8 us; the launch traced here: 90.3 us
  waiting for transfers between devices  40.6 us (45%)
  starting transfers between devices  30.9 us (34%)
  Pallas kernels  15 us (17%)
  local copies, waits for them, and re-layouts  2.22 us (2%)
  other arithmetic  0.99 us (1%)
    ppermute x1, waiting for transfers between devices, on_device(): kv_before = lax.ppermute(kv, 'chip', [(c, c + 1) for c in range(chips - 1)])  18.1 us
    all_to_all x2, waiting for transfers between devices, exchange(): lax.all_to_all(value, ('core', 'head'), split_axis=0, concat_axis=0, tile...  14.6 us
    all_to_all x2, starting transfers between devices, exchange(): lax.all_to_all(value, ('core', 'head'), split_axis=0, concat_axis=0, tile...  13.4 us
    ppermute x1, starting transfers between devices, on_device(): back = lax.ppermute(back, 'chip', [(c + 1, c) for c in range(chips - 1)])  10.9 us
    pallas_call x4, Pallas kernels, whole_call(): pl.pallas_call(kernel, in_specs=[smem_spec()] * smem + [vmem_spec()] * (l...  8.83 us
    ppermute x1, waiting for transfers between devices, on_device(): back = lax.ppermute(back, 'chip', [(c + 1, c) for c in range(chips - 1)])  6.38 us
    pallas_call x1, Pallas kernels, pack_queries(): pl.pallas_call(pack_queries_kernel, grid=(steps,), in_specs=[pl.BlockSpec...  4.28 us
    ppermute x1, starting transfers between devices, on_device(): kv_before = lax.ppermute(kv, 'chip', [(c, c + 1) for c in range(chips - 1)])  4.03 us
  transfers between devices with their start and end apart: 5, of which 5 were waited for; matrix products, arithmetic and copies ran while one was open for 1% of the time, Pallas kernels for 9%

profile of v6, /device:TPU:7, one launch (start us, length us, event | category | flops | bytes accessed | tf_op | source)
XLA Modules:
  0.0 90.3 jit_solution(6397417861694591521)
XLA Ops:
  0.6 1.9 %pack_keys.1 = bf16[2,8,128,128]{3,2,1,0:T(8,128)(2,1)} custom-call(bf16[64,2048]{1,0:T(8,128)(2,1)} %key_ref.1, bf16[64,2048]{1,0:T(8,128)(2,1)} %value_ref.1), custom_call_target="tpu_custom_call" | custom-call | tf_op jit(solution)/shard_map/pack_keys/pallas_call | solution.py:46
  2.5 7.8 %all-to-all-start = ((bf16[16,128,128]{2,1,0:T(8,128)(2,1)}), bf16[16,128,128]{2,1,0:T(8,128)(2,1)S(1)}, u32[]{:S(2)}, u32[]{:S(2)}) async-start(bf16[16,128,128]{2,1,0:T(8,128)(2,1)} %bitcast.5), calls=%async_computation | async-start | bytes 1048576 | tf_op jit(solution)/shard_map/all_to_all | solution.py:266
  10.3 4.3 %pack_queries.1 = bf16[2,8,264,128]{3,2,1,0:T(8,128)(2,1)} custom-call(bf16[64,4096]{1,0:T(8,128)(2,1)} %query_ref.1, bf16[64,4096]{1,0:T(8,128)(2,1)} %grad_ref.1, bf16[64,4096]{1,0:T(8,128)(2,1)} %row_ref.1, f32[32,64]{1,0:T(8,128)} %lse_ref.1), custom_call_target="tpu_custom_call" | custom-call | tf_op jit(solution)/shard_map/pack_queries/pallas_call | solution.py:101
  14.6 10.5 %all-to-all-done.kv_ref = bf16[16,128,128]{2,1,0:T(8,128)(2,1)S(1)} async-done(((bf16[16,128,128]{2,1,0:T(8,128)(2,1)}), bf16[16,128,128]{2,1,0:T(8,128)(2,1)S(1)}, u32[]{:S(2)}, u32[]{:S(2)}) %all-to-all-start) | async-done | bytes 524320 | tf_op jit(solution)/shard_map/all_to_all | solution.py:266
  25.1 0.0 copy-start.2
  25.1 5.6 %all-to-all-start.1 = ((bf16[16,264,128]{2,1,0:T(8,128)(2,1)}), bf16[16,264,128]{2,1,0:T(8,128)(2,1)S(1)}, u32[]{:S(2)}, u32[]{:S(2)}) async-start(bf16[16,264,128]{2,1,0:T(8,128)(2,1)} %bitcast.4), calls=%async_computation.1 | async-start | bytes 2162688 | tf_op jit(solution)/shard_map/all_to_all | solution.py:266
  30.6 0.0 copy-done.2
  30.7 4.0 %collective-permute-start = (bf16[16,128,128]{2,1,0:T(8,128)(2,1)S(1)}, bf16[16,128,128]{2,1,0:T(8,128)(2,1)S(1)}, u32[]{:S(2)}, u32[]{:S(2)}) collective-permute-start(bf16[16,128,128]{2,1,0:T(8,128)(2,1)S(1)} %all-to-all-done.kv_ref), channel_id=1, source_target_pairs={{0,16},{16,32},{32,48},{48,64},{64,80},{80,96},{96,112},{112,128},... | collective-permute-start | bytes 1572872 | tf_op jit(solution)/shard_map/ppermute | solution.py:279
  34.7 1.0 %convert_reduce_fusion = s32[1024]{0:T(1024)S(1)} fusion(s32[1024]{0:T(1024)S(1)} %pad_dynamic-slice_fusion, s32[2048]{0:T(1024)S(1)} %pad_dynamic-slice_fusion.1), kind=kLoop, calls=%fused_computation | loop fusion | flops 6290432 | bytes 16384 | tf_op jit(solution)/shard_map/reduce_sum | solution.py:259
  35.7 18.1 %collective-permute-done.kv_ref = bf16[16,128,128]{2,1,0:T(8,128)(2,1)S(1)} collective-permute-done((bf16[16,128,128]{2,1,0:T(8,128)(2,1)S(1)}, bf16[16,128,128]{2,1,0:T(8,128)(2,1)S(1)}, u32[]{:S(2)}, u32[]{:S(2)}) %collective-permute-start) | collective-permute-done | bytes 524320 | tf_op jit(solution)/shard_map/ppermute | solution.py:279
  53.8 4.1 %all-to-all-done.1.q_ref = bf16[16,264,128]{2,1,0:T(8,128)(2,1)S(1)} async-done(((bf16[16,264,128]{2,1,0:T(8,128)(2,1)}), bf16[16,264,128]{2,1,0:T(8,128)(2,1)S(1)}, u32[]{:S(2)}, u32[]{:S(2)}) %all-to-all-start.1) | async-done | bytes 1081376 | tf_op jit(solution)/shard_map/all_to_all | solution.py:266
  57.9 3.7 %cross_terms.1 = (f32[2,1024,128]{2,1,0:T(8,128)S(1)}, bf16[2,1024,128]{2,1,0:T(8,128)(2,1)S(1)}) custom-call(bf16[16,128,128]{2,1,0:T(8,128)(2,1)S(1)} %collective-permute-done.kv_ref, bf16[16,264,128]{2,1,0:T(8,128)(2,1)S(1)} %all-to-all-done.1.q_ref, s32[8,1,128]{2,1,0:T(1,128)S(1)} %add_maximum_fusion.lo_ref), custom_call_target="tpu_custom_call" | custom-call | flops 1342177280 | bytes 4194304 | tf_op jit(solution)/shard_map/cross_terms/pallas_call | solution.py:222
  61.6 0.0 copy-start
  61.6 1.0 %copy-done = f32[2,1024,128]{2,1,0:T(8,128)} copy-done((f32[2,1024,128]{2,1,0:T(8,128)}, f32[2,1024,128]{2,1,0:T(8,128)S(1)}, u32[]{:S(2)}) %copy-start) | copy-done | bytes 1048600
  62.6 10.9 %collective-permute-start.1 = (bf16[2,1024,128]{2,1,0:T(8,128)(2,1)S(1)}, bf16[2,1024,128]{2,1,0:T(8,128)(2,1)S(1)}, u32[]{:S(2)}, u32[]{:S(2)}) collective-permute-start(bf16[2,1024,128]{2,1,0:T(8,128)(2,1)S(1)} %get-tuple-element.16), channel_id=1, source_target_pairs={{16,0},{32,16},{48,32},{64,48},{80,64},{96,80},{112,96},{128,112},... | collective-permute-start | bytes 1572872 | tf_op jit(solution)/shard_map/ppermute | solution.py:281
  73.5 0.0 copy-start.1
  73.6 1.2 %copy-done.1 = f32[2,1024,128]{2,1,0:T(8,128)S(1)} copy-done((f32[2,1024,128]{2,1,0:T(8,128)S(1)}, f32[2,1024,128]{2,1,0:T(8,128)}, u32[]{:S(2)}) %copy-start.1) | copy-done | bytes 1048600
  74.8 3.8 %own_terms.1 = (bf16[2,1024,128]{2,1,0:T(8,128)(2,1)S(1)}, f32[2,1024,128]{2,1,0:T(8,128)S(1)}) custom-call(bf16[16,128,128]{2,1,0:T(8,128)(2,1)S(1)} %all-to-all-done.kv_ref, bf16[16,264,128]{2,1,0:T(8,128)(2,1)S(1)} %all-to-all-done.1.q_ref, s32[8,1,128]{2,1,0:T(1,128)S(1)} %add_maximum_fusion.lo_ref, f32[2,1024,128]{2,1,0:T(8,128)S(1)} %copy-done.1), custom_call_target="tpu_custom_call" | custom-call | flops 1342177280 | bytes 4194304 | tf_op jit(solution)/shard_map/own_terms/pallas_call | solution.py:222
  78.6 6.4 %collective-permute-done.1.back_ref = bf16[2,1024,128]{2,1,0:T(8,128)(2,1)S(1)} collective-permute-done((bf16[2,1024,128]{2,1,0:T(8,128)(2,1)S(1)}, bf16[2,1024,128]{2,1,0:T(8,128)(2,1)S(1)}, u32[]{:S(2)}, u32[]{:S(2)}) %collective-permute-start.1) | collective-permute-done | bytes 524320 | tf_op jit(solution)/shard_map/ppermute | solution.py:281
  85.0 0.1 finish.1
  85.1 2.6 %collective-permute-start.2 = (bf16[4,512,128]{2,1,0:T(8,128)(2,1)S(1)}, bf16[4,512,128]{2,1,0:T(8,128)(2,1)S(1)}, u32[]{:S(2)}, u32[]{:S(2)}) collective-permute-start(bf16[4,512,128]{2,1,0:T(8,128)(2,1)S(1)} %get-tuple-element.18), channel_id=1, source_target_pairs={{0,8},{8,0},{1,9},{9,1},{2,10},{10,2},{3,11},{11,3},{4,12},{12,4},... | collective-permute-start | bytes 1572872 | tf_op jit(solution)/shard_map/ppermute | solution.py:284
  87.7 1.5 %collective-permute-done.2.far_ref = bf16[4,512,128]{2,1,0:T(8,128)(2,1)S(1)} collective-permute-done((bf16[4,512,128]{2,1,0:T(8,128)(2,1)S(1)}, bf16[4,512,128]{2,1,0:T(8,128)(2,1)S(1)}, u32[]{:S(2)}, u32[]{:S(2)}) %collective-permute-start.2) | collective-permute-done | bytes 524320 | tf_op jit(solution)/shard_map/ppermute | solution.py:284
  89.2 1.1 %join.1 = (bf16[512,512]{1,0:T(8,128)(2,1)}, bf16[512,256]{1,0:T(8,128)(2,1)}, bf16[512,256]{1,0:T(8,128)(2,1)}) custom-call(s32[1]{0:T(128)} %bitcast.core_ref, bf16[4,512,128]{2,1,0:T(8,128)(2,1)S(1)} %get-tuple-element.17.near_ref, bf16[4,512,128]{2,1,0:T(8,128)(2,1)S(1)} %collective-permute-done.2.far_ref), custom_call_target="tpu_custom_call" | custom-call | tf_op jit(solution)/shard_map/join/pallas_call | solution.py:222
  (3 shorter events, 0.0 us)
Async XLA Ops:
  2.5 22.6 %all-to-all-start = ((bf16[16,128,128]{2,1,0:T(8,128)(2,1)}), bf16[16,128,128]{2,1,0:T(8,128)(2,1)S(1)}, u32[]{:S(2)}, u32[]{:S(2)}) async-start(bf16[16,128,128]{2,1,0:T(8,128)(2,1)} %bitcast.5), calls=%async_computation | async-start | bytes 1048576 | tf_op jit(solution)/shard_map/all_to_all | solution.py:266
  25.1 5.6 %copy-start.2 = (s32[32768]{0:T(1024)S(1)}, s32[32768]{0:T(1024)}, u32[]{:S(2)}) copy-start(s32[32768]{0:T(1024)} %param.13) | copy-start | bytes 393220
  25.1 32.8 %all-to-all-start.1 = ((bf16[16,264,128]{2,1,0:T(8,128)(2,1)}), bf16[16,264,128]{2,1,0:T(8,128)(2,1)S(1)}, u32[]{:S(2)}, u32[]{:S(2)}) async-start(bf16[16,264,128]{2,1,0:T(8,128)(2,1)} %bitcast.4), calls=%async_computation.1 | async-start | bytes 2162688 | tf_op jit(solution)/shard_map/all_to_all | solution.py:266
  30.7 23.1 %collective-permute-start = (bf16[16,128,128]{2,1,0:T(8,128)(2,1)S(1)}, bf16[16,128,128]{2,1,0:T(8,128)(2,1)S(1)}, u32[]{:S(2)}, u32[]{:S(2)}) collective-permute-start(bf16[16,128,128]{2,1,0:T(8,128)(2,1)S(1)} %all-to-all-done.kv_ref), channel_id=1, source_target_pairs={{0,16},{16,32},{32,48},{48,64},{64,80},{80,96},{96,112},{112,128},... | collective-permute-start | bytes 1572872 | tf_op jit(solution)/shard_map/ppermute | solution.py:279
  61.6 1.0 %copy-start = (f32[2,1024,128]{2,1,0:T(8,128)}, f32[2,1024,128]{2,1,0:T(8,128)S(1)}, u32[]{:S(2)}) copy-start(f32[2,1024,128]{2,1,0:T(8,128)S(1)} %get-tuple-element.13.part_ref) | copy-start | bytes 3145732
  62.6 22.4 %collective-permute-start.1 = (bf16[2,1024,128]{2,1,0:T(8,128)(2,1)S(1)}, bf16[2,1024,128]{2,1,0:T(8,128)(2,1)S(1)}, u32[]{:S(2)}, u32[]{:S(2)}) collective-permute-start(bf16[2,1024,128]{2,1,0:T(8,128)(2,1)S(1)} %get-tuple-element.16), channel_id=1, source_target_pairs={{16,0},{32,16},{48,32},{64,48},{80,64},{96,80},{112,96},{128,112},... | collective-permute-start | bytes 1572872 | tf_op jit(solution)/shard_map/ppermute | solution.py:281
  73.5 1.2 %copy-start.1 = (f32[2,1024,128]{2,1,0:T(8,128)S(1)}, f32[2,1024,128]{2,1,0:T(8,128)}, u32[]{:S(2)}) copy-start(f32[2,1024,128]{2,1,0:T(8,128)} %copy-done) | copy-start | bytes 3145732
  85.1 4.1 %collective-permute-start.2 = (bf16[4,512,128]{2,1,0:T(8,128)(2,1)S(1)}, bf16[4,512,128]{2,1,0:T(8,128)(2,1)S(1)}, u32[]{:S(2)}, u32[]{:S(2)}) collective-permute-start(bf16[4,512,128]{2,1,0:T(8,128)(2,1)S(1)} %get-tuple-element.18), channel_id=1, source_target_pairs={{0,8},{8,0},{1,9},{9,1},{2,10},{10,2},{3,11},{11,3},{4,12},{12,4},... | collective-permute-start | bytes 1572872 | tf_op jit(solution)/shard_map/ppermute | solution.py:284

commit v7 on v5

--- a/solution.py
+++ b/solution.py
@@ -1,3 +1,4 @@
+import functools
 import math
 
 import jax
@@ -119,13 +120,11 @@
     return jnp.concatenate(rows[0:2], axis=1), jnp.concatenate(rows[2:4], axis=1)
 
 
-def sweep(causal, key_base, kv_ref, q_ref, lo_ref, dk_ref, dv_ref, dq_ref, part_ref):
+def sweep(strips, causal, key_base, kv_ref, q_ref, lo_ref, dk_ref, dv_ref, dq_ref, part_ref):
     pieces = CHUNK // PIECE
-    chunks = LOOKBACK_SPAN // CHUNK
-    order = range(chunks - 1, -1, -1) if causal else range(chunks)
-    for n, at in enumerate(order):
-        first, last = (0, at + 1) if causal else (at, chunks)
-        strip = slice(first * CHUNK, last * CHUNK)
+    base = strips[0][1]
+    for n, (at, first, last) in enumerate(strips):
+        strip = slice((first - base) * CHUNK, (last - base) * CHUNK)
         height = (last - first) * CHUNK
         sources = slice(first * pieces, last * pieces)
         key = kv_ref[sources, 0:PIECE, :].reshape(height, HEAD_SIZE)
@@ -168,19 +167,32 @@
             dq_ref[a, at * CHUNK : (at + 1) * CHUNK, :] = mine
 
 
-def cross_kernel(core_ref, kv_ref, q_ref, lo_ref, dq_ref, near_ref, far_ref, dk_ref, dv_ref):
-    sweep(False, 0, kv_ref, q_ref, lo_ref, dk_ref, dv_ref, dq_ref, None)
-    half = LOOKBACK_SPAN // CORES
-    near = pl.ds(pl.multiple_of(core_ref[0] * half, half), half)
-    far = pl.ds(pl.multiple_of((1 - core_ref[0]) * half, half), half)
-    near_ref[0] = dk_ref[near, :].astype(bf16)
-    near_ref[1] = dv_ref[near, :].astype(bf16)
-    far_ref[0] = dk_ref[far, :].astype(bf16)
-    far_ref[1] = dv_ref[far, :].astype(bf16)
+def cross_kernel(near, core_ref, kv_ref, q_ref, lo_ref, *refs):
+    part_ref = None if near else refs[0]
+    dq_ref, out_ref, dk_ref, dv_ref = refs[-4:]
+    chunks = LOOKBACK_SPAN // CHUNK
+    for block in range(CORES):
+
+        @pl.when(core_ref[0] == (block if near else 1 - block))
+        def _():
+            start, end = block * chunks // CORES, (block + 1) * chunks // CORES
+            sweep(
+                [(at, max(at, start), end) for at in range(end)],
+                False, 0, kv_ref, q_ref, lo_ref, dk_ref, dv_ref, dq_ref, part_ref,
+            )
+            rest = slice(end * CHUNK, LOOKBACK_SPAN)
+            if end < chunks:
+                dq_ref[:, rest, :] = jnp.zeros_like(dq_ref[:, rest, :]) if near else part_ref[:, rest, :]
+            out_ref[0] = dk_ref[...].astype(bf16)
+            out_ref[1] = dv_ref[...].astype(bf16)
 
 
 def own_kernel(core_ref, kv_ref, q_ref, lo_ref, part_ref, near_dq_ref, near_ref, far_ref, dk_ref, dv_ref, dq_ref):
-    sweep(True, LOOKBACK_SPAN, kv_ref, q_ref, lo_ref, dk_ref, dv_ref, dq_ref, part_ref)
+    chunks = LOOKBACK_SPAN // CHUNK
+    sweep(
+        [(at, 0, at + 1) for at in range(chunks - 1, -1, -1)],
+        True, LOOKBACK_SPAN, kv_ref, q_ref, lo_ref, dk_ref, dv_ref, dq_ref, part_ref,
+    )
     near = pl.ds(pl.multiple_of(core_ref[0] * HALF, HALF), HALF)
     far = pl.ds(pl.multiple_of((1 - core_ref[0]) * HALF, HALF), HALF)
     for a in range(2):
@@ -200,11 +212,11 @@
     return pl.BlockSpec(memory_space=pltpu.SMEM)
 
 
-SPAN_SCRATCH = [
-    pltpu.VMEM((LOOKBACK_SPAN, HEAD_SIZE), f32),
-    pltpu.VMEM((LOOKBACK_SPAN, HEAD_SIZE), f32),
-]
 HALF = LOOKBACK_SPAN // CORES
+
+
+def rows_scratch(rows):
+    return [pltpu.VMEM((rows, HEAD_SIZE), f32)] * 2
 
 
 def cost():
@@ -212,21 +224,20 @@
     return pl.CostEstimate(flops=pairs * 5 * 2 * HEAD_SIZE, transcendentals=pairs, bytes_accessed=4 << 20)
 
 
-def cross_terms(core, kv, q, lo):
-    return pl.pallas_call(
-        cross_kernel,
-        in_specs=[smem_spec()] + [vmem_spec()] * 3,
-        out_specs=[vmem_spec()] * 3,
+def cross_terms(near, core, kv, q, lo, *part):
+    return pl.pallas_call(
+        functools.partial(cross_kernel, near),
+        in_specs=[smem_spec()] + [vmem_spec()] * (3 + len(part)),
+        out_specs=[vmem_spec()] * 2,
         out_shape=[
             jax.ShapeDtypeStruct((2, LOOKBACK_SPAN, HEAD_SIZE), f32),
             jax.ShapeDtypeStruct((2, HALF, HEAD_SIZE), bf16),
-            jax.ShapeDtypeStruct((2, HALF, HEAD_SIZE), bf16),
         ],
-        scratch_shapes=SPAN_SCRATCH,
-        compiler_params=pltpu.CompilerParams(vmem_limit_bytes=40 << 20),
+        scratch_shapes=rows_scratch(HALF),
+        compiler_params=pltpu.CompilerParams(vmem_limit_bytes=20 << 20),
         cost_estimate=cost(),
-        name="cross_terms",
-    )(core, kv, q, lo)
+        name="cross_near" if near else "cross_far",
+    )(core, kv, q, lo, *part)
 
 
 def own_terms(core, kv, q, lo, part):
@@ -239,8 +250,8 @@
             jax.ShapeDtypeStruct((2, HALF, HEAD_SIZE), f32),
             jax.ShapeDtypeStruct((4, HALF, HEAD_SIZE), bf16),
         ],
-        scratch_shapes=SPAN_SCRATCH + [pltpu.VMEM((2, LOOKBACK_SPAN, HEAD_SIZE), f32)],
-        compiler_params=pltpu.CompilerParams(vmem_limit_bytes=40 << 20),
+        scratch_shapes=rows_scratch(LOOKBACK_SPAN) + [pltpu.VMEM((2, LOOKBACK_SPAN, HEAD_SIZE), f32)],
+        compiler_params=pltpu.CompilerParams(vmem_limit_bytes=20 << 20),
         cost_estimate=cost(),
         name="own_terms",
     )(core, kv, q, lo, part)
@@ -310,8 +321,9 @@
     kv, packed = lax.optimization_barrier((kv, packed))
     q = exchange(packed)
     kv_before = lax.ppermute(kv, "chip", [(c, c + 1) for c in range(chips - 1)])
-    dq_part, near, far = cross_terms(core, kv_before, q, lo)
+    dq_part, near = cross_terms(True, core, kv_before, q, lo)
     back_near = lax.ppermute(near, "chip", [(c + 1, c) for c in range(chips - 1)])
+    dq_part, far = cross_terms(False, core, kv_before, q, lo, dq_part)
     back_far = lax.ppermute(
         far,
         ("chip", "core"),

time: 85.7 us -> 85.7 us (level)
  waiting for transfers between devices: 35.6 us -> 34.1 us
    ppermute x1, waiting for transfers between devices: 2.97 us -> 1.32 us  [on_device(): lax.ppermute(far, ('chip', 'core'), [(CORES * (c + 1) + k, CORES * c + 1...]
    pallas_call x1 -> x2, Pallas kernels: 3.76 us -> 4.27 us  [cross_terms(): pl.pallas_call(functools.partial(cross_kernel, near), in_specs=[smem_spec...]
  transfers between devices with their start and end apart: 6 -> 6, of which waited for: 4 -> 5; matrix products, arithmetic and copies ran while one was open for 1% -> 1% of each run, Pallas kernels for 10% -> 11%
where the time goes in v7:
time: 85.7 us; the launch traced here: 84.4 us
  waiting for transfers between devices  34.1 us (40%)
  starting transfers between devices  33 us (39%)
  Pallas kernels  15.5 us (18%)
  other arithmetic  0.99 us (1%)
    ppermute x1, waiting for transfers between devices, on_device(): kv_before = lax.ppermute(kv, 'chip', [(c, c + 1) for c in range(chips - 1)])  18.1 us
    all_to_all x2, waiting for transfers between devices, exchange(): lax.all_to_all(value, ('core', 'head'), split_axis=0, concat_axis=0, tile...  14.6 us
    all_to_all x2, starting transfers between devices, exchange(): lax.all_to_all(value, ('core', 'head'), split_axis=0, concat_axis=0, tile...  13.4 us
    ppermute x1, starting transfers between devices, on_device(): lax.ppermute(near, 'chip', [(c + 1, c) for c in range(chips - 1)])  10.9 us
    pallas_call x1, Pallas kernels, pack_queries(): pl.pallas_call(pack_queries_kernel, grid=(steps,), in_specs=[pl.BlockSpec...  4.28 us
    pallas_call x2, Pallas kernels, cross_terms(): pl.pallas_call(functools.partial(cross_kernel, near), in_specs=[smem_spec...  4.27 us
    ppermute x1, starting transfers between devices, on_device(): kv_before = lax.ppermute(kv, 'chip', [(c, c + 1) for c in range(chips - 1)])  4.03 us
    pallas_call x1, Pallas kernels, own_terms(): pl.pallas_call(own_kernel, in_specs=[smem_spec()] + [vmem_spec()] * 4, ou...  3.9 us
  transfers between devices with their start and end apart: 6, of which 5 were waited for; matrix products, arithmetic and copies ran while one was open for 1% of the time, Pallas kernels for 11%

profile of v7, /device:TPU:7, one launch (start us, length us, event | category | flops | bytes accessed | tf_op | source)
XLA Modules:
  0.0 84.4 jit_solution(5502423848996967733)
XLA Ops:
  0.6 1.9 %pack_keys.1 = bf16[2,8,128,128]{3,2,1,0:T(8,128)(2,1)} custom-call(bf16[64,2048]{1,0:T(8,128)(2,1)} %key_ref.1, bf16[64,2048]{1,0:T(8,128)(2,1)} %value_ref.1), custom_call_target="tpu_custom_call" | custom-call | tf_op jit(solution)/shard_map/pack_keys/pallas_call | solution.py:47
  2.5 7.8 %all-to-all-start = ((bf16[16,128,128]{2,1,0:T(8,128)(2,1)}), bf16[16,128,128]{2,1,0:T(8,128)(2,1)S(1)}, u32[]{:S(2)}, u32[]{:S(2)}) async-start(bf16[16,128,128]{2,1,0:T(8,128)(2,1)} %bitcast.5), calls=%async_computation | async-start | bytes 1048576 | tf_op jit(solution)/shard_map/all_to_all | solution.py:310
  10.3 4.3 %pack_queries.1 = bf16[2,8,264,128]{3,2,1,0:T(8,128)(2,1)} custom-call(bf16[64,4096]{1,0:T(8,128)(2,1)} %query_ref.1, bf16[64,4096]{1,0:T(8,128)(2,1)} %grad_ref.1, bf16[64,4096]{1,0:T(8,128)(2,1)} %row_ref.1, f32[32,64]{1,0:T(8,128)} %lse_ref.1), custom_call_target="tpu_custom_call" | custom-call | tf_op jit(solution)/shard_map/pack_queries/pallas_call | solution.py:102
  14.6 10.5 %all-to-all-done.kv_ref = bf16[16,128,128]{2,1,0:T(8,128)(2,1)S(1)} async-done(((bf16[16,128,128]{2,1,0:T(8,128)(2,1)}), bf16[16,128,128]{2,1,0:T(8,128)(2,1)S(1)}, u32[]{:S(2)}, u32[]{:S(2)}) %all-to-all-start) | async-done | bytes 524320 | tf_op jit(solution)/shard_map/all_to_all | solution.py:310
  25.1 0.0 copy-start
  25.1 5.6 %all-to-all-start.1 = ((bf16[16,264,128]{2,1,0:T(8,128)(2,1)}), bf16[16,264,128]{2,1,0:T(8,128)(2,1)S(1)}, u32[]{:S(2)}, u32[]{:S(2)}) async-start(bf16[16,264,128]{2,1,0:T(8,128)(2,1)} %bitcast.4), calls=%async_computation.1 | async-start | bytes 2162688 | tf_op jit(solution)/shard_map/all_to_all | solution.py:310
  30.6 0.0 copy-done
  30.7 4.0 %collective-permute-start = (bf16[16,128,128]{2,1,0:T(8,128)(2,1)S(1)}, bf16[16,128,128]{2,1,0:T(8,128)(2,1)S(1)}, u32[]{:S(2)}, u32[]{:S(2)}) collective-permute-start(bf16[16,128,128]{2,1,0:T(8,128)(2,1)S(1)} %all-to-all-done.kv_ref), channel_id=1, source_target_pairs={{0,16},{16,32},{32,48},{48,64},{64,80},{80,96},{96,112},{112,128},... | collective-permute-start | bytes 1572872 | tf_op jit(solution)/shard_map/ppermute | solution.py:323
  34.7 1.0 %convert_reduce_fusion = s32[1024]{0:T(1024)S(1)} fusion(s32[1024]{0:T(1024)S(1)} %pad_dynamic-slice_fusion, s32[2048]{0:T(1024)S(1)} %pad_dynamic-slice_fusion.1), kind=kLoop, calls=%fused_computation | loop fusion | flops 6290432 | bytes 16384 | tf_op jit(solution)/shard_map/reduce_sum | solution.py:303
  35.7 18.1 %collective-permute-done.kv_ref = bf16[16,128,128]{2,1,0:T(8,128)(2,1)S(1)} collective-permute-done((bf16[16,128,128]{2,1,0:T(8,128)(2,1)S(1)}, bf16[16,128,128]{2,1,0:T(8,128)(2,1)S(1)}, u32[]{:S(2)}, u32[]{:S(2)}) %collective-permute-start) | collective-permute-done | bytes 524320 | tf_op jit(solution)/shard_map/ppermute | solution.py:323
  53.8 4.1 %all-to-all-done.1.q_ref = bf16[16,264,128]{2,1,0:T(8,128)(2,1)S(1)} async-done(((bf16[16,264,128]{2,1,0:T(8,128)(2,1)}), bf16[16,264,128]{2,1,0:T(8,128)(2,1)S(1)}, u32[]{:S(2)}, u32[]{:S(2)}) %all-to-all-start.1) | async-done | bytes 1081376 | tf_op jit(solution)/shard_map/all_to_all | solution.py:310
  57.9 2.9 %cross_near.1 = (f32[2,1024,128]{2,1,0:T(8,128)S(1)}, bf16[2,512,128]{2,1,0:T(8,128)(2,1)S(1)}) custom-call(s32[1]{0:T(128)} %bitcast.core_ref, bf16[16,128,128]{2,1,0:T(8,128)(2,1)S(1)} %collective-permute-done.kv_ref, bf16[16,264,128]{2,1,0:T(8,128)(2,1)S(1)} %all-to-all-done.1.q_ref, s32[8,1,128]{2,1,0:T(1,128)S(1)} %add_maximum_fusion.lo_ref), custom_call_target="tpu_custom_call" | custom-call | flops 1342177280 | bytes 4194304 | tf_op jit(solution)/shard_map/cross_near/pallas_call | solution.py:228
  60.8 10.9 %collective-permute-start.3 = (bf16[2,512,128]{2,1,0:T(8,128)(2,1)S(1)}, bf16[2,512,128]{2,1,0:T(8,128)(2,1)S(1)}, u32[]{:S(2)}, u32[]{:S(2)}) collective-permute-start(bf16[2,512,128]{2,1,0:T(8,128)(2,1)S(1)} %get-tuple-element.22), channel_id=1, source_target_pairs={{16,0},{32,16},{48,32},{64,48},{80,64},{96,80},{112,96},{128,112},... | collective-permute-start | bytes 786440 | tf_op jit(solution)/shard_map/ppermute | solution.py:325
  71.7 1.4 %cross_far.1 = (f32[2,1024,128]{2,1,0:T(8,128)S(1)}, bf16[2,512,128]{2,1,0:T(8,128)(2,1)S(1)}) custom-call(s32[1]{0:T(128)} %bitcast.core_ref, bf16[16,128,128]{2,1,0:T(8,128)(2,1)S(1)} %collective-permute-done.kv_ref, bf16[16,264,128]{2,1,0:T(8,128)(2,1)S(1)} %all-to-all-done.1.q_ref, s32[8,1,128]{2,1,0:T(1,128)S(1)} %add_maximum_fusion.lo_ref, ...), custom_call_target="tpu_custom_call" | custom-call | flops 1342177280 | bytes 4194304 | tf_op jit(solution)/shard_map/cross_far/pallas_call | solution.py:228
  73.1 2.4 %collective-permute-start.2 = (bf16[2,512,128]{2,1,0:T(8,128)(2,1)S(1)}, bf16[2,512,128]{2,1,0:T(8,128)(2,1)S(1)}, u32[]{:S(2)}, u32[]{:S(2)}) collective-permute-start(bf16[2,512,128]{2,1,0:T(8,128)(2,1)S(1)} %get-tuple-element.20), channel_id=1, source_target_pairs={{16,8},{24,0},{32,24},{40,16},{48,40},{56,32},{64,56},{72,48},{80,... | collective-permute-start | bytes 786440 | tf_op jit(solution)/shard_map/ppermute | solution.py:327
  75.5 3.9 %own_terms.1 = (bf16[2,512,128]{2,1,0:T(8,128)(2,1)S(1)}, f32[2,512,128]{2,1,0:T(8,128)S(1)}, bf16[4,512,128]{2,1,0:T(8,128)(2,1)S(1)}) custom-call(s32[1]{0:T(128)} %bitcast.core_ref, bf16[16,128,128]{2,1,0:T(8,128)(2,1)S(1)} %all-to-all-done.kv_ref, bf16[16,264,128]{2,1,0:T(8,128)(2,1)S(1)} %all-to-all-done.1.q_ref, ...), custom_call_target="tpu_custom_call" | custom-call | flops 1342177280 | bytes 4194304 | tf_op jit(solution)/shard_map/own_terms/pallas_call | solution.py:244
  79.5 2.2 %collective-permute-start.1 = (bf16[4,512,128]{2,1,0:T(8,128)(2,1)S(1)}, bf16[4,512,128]{2,1,0:T(8,128)(2,1)S(1)}, u32[]{:S(2)}, u32[]{:S(2)}) collective-permute-start(bf16[4,512,128]{2,1,0:T(8,128)(2,1)S(1)} %get-tuple-element.19), channel_id=1, source_target_pairs={{0,8},{8,0},{1,9},{9,1},{2,10},{10,2},{3,11},{11,3},{4,12},{12,4},... | collective-permute-start | bytes 1572872 | tf_op jit(solution)/shard_map/ppermute | solution.py:333
  81.7 0.0 collective-permute-done.3.back_ref
  81.7 0.1 join_near.1
  81.8 1.3 %collective-permute-done.2.back_ref = bf16[2,512,128]{2,1,0:T(8,128)(2,1)S(1)} collective-permute-done((bf16[2,512,128]{2,1,0:T(8,128)(2,1)S(1)}, bf16[2,512,128]{2,1,0:T(8,128)(2,1)S(1)}, u32[]{:S(2)}, u32[]{:S(2)}) %collective-permute-start.2) | collective-permute-done | bytes 262176 | tf_op jit(solution)/shard_map/ppermute | solution.py:327
  83.1 0.2 collective-permute-done.1.swapped_ref
  83.3 1.2 %join_far.1 = (bf16[512,512]{1,0:T(8,128)(2,1)}, bf16[512,256]{1,0:T(8,128)(2,1)}, bf16[512,256]{1,0:T(8,128)(2,1)}) custom-call(s32[1]{0:T(128)} %bitcast.core_ref, bf16[2,512,128]{2,1,0:T(8,128)(2,1)S(1)} %get-tuple-element.18.near_dq_ref, bf16[4,512,128]{2,1,0:T(8,128)(2,1)S(1)} %collective-permute-done.1.swapped_ref, ...), custom_call_target="tpu_custom_call" | custom-call | flops 1048576 | bytes 1048576 | tf_op jit(solution)/shard_map/join_far/pallas_call | solution.py:288
  (3 shorter events, 0.0 us)
Async XLA Ops:
  2.5 22.6 %all-to-all-start = ((bf16[16,128,128]{2,1,0:T(8,128)(2,1)}), bf16[16,128,128]{2,1,0:T(8,128)(2,1)S(1)}, u32[]{:S(2)}, u32[]{:S(2)}) async-start(bf16[16,128,128]{2,1,0:T(8,128)(2,1)} %bitcast.5), calls=%async_computation | async-start | bytes 1048576 | tf_op jit(solution)/shard_map/all_to_all | solution.py:310
  25.1 5.6 %copy-start = (s32[32768]{0:T(1024)S(1)}, s32[32768]{0:T(1024)}, u32[]{:S(2)}) copy-start(s32[32768]{0:T(1024)} %param.13) | copy-start | bytes 393220
  25.1 32.8 %all-to-all-start.1 = ((bf16[16,264,128]{2,1,0:T(8,128)(2,1)}), bf16[16,264,128]{2,1,0:T(8,128)(2,1)S(1)}, u32[]{:S(2)}, u32[]{:S(2)}) async-start(bf16[16,264,128]{2,1,0:T(8,128)(2,1)} %bitcast.4), calls=%async_computation.1 | async-start | bytes 2162688 | tf_op jit(solution)/shard_map/all_to_all | solution.py:310
  30.7 23.1 %collective-permute-start = (bf16[16,128,128]{2,1,0:T(8,128)(2,1)S(1)}, bf16[16,128,128]{2,1,0:T(8,128)(2,1)S(1)}, u32[]{:S(2)}, u32[]{:S(2)}) collective-permute-start(bf16[16,128,128]{2,1,0:T(8,128)(2,1)S(1)} %all-to-all-done.kv_ref), channel_id=1, source_target_pairs={{0,16},{16,32},{32,48},{48,64},{64,80},{80,96},{96,112},{112,128},... | collective-permute-start | bytes 1572872 | tf_op jit(solution)/shard_map/ppermute | solution.py:323
  60.8 20.9 %collective-permute-start.3 = (bf16[2,512,128]{2,1,0:T(8,128)(2,1)S(1)}, bf16[2,512,128]{2,1,0:T(8,128)(2,1)S(1)}, u32[]{:S(2)}, u32[]{:S(2)}) collective-permute-start(bf16[2,512,128]{2,1,0:T(8,128)(2,1)S(1)} %get-tuple-element.22), channel_id=1, source_target_pairs={{16,0},{32,16},{48,32},{64,48},{80,64},{96,80},{112,96},{128,112},... | collective-permute-start | bytes 786440 | tf_op jit(solution)/shard_map/ppermute | solution.py:325
  73.1 10.0 %collective-permute-start.2 = (bf16[2,512,128]{2,1,0:T(8,128)(2,1)S(1)}, bf16[2,512,128]{2,1,0:T(8,128)(2,1)S(1)}, u32[]{:S(2)}, u32[]{:S(2)}) collective-permute-start(bf16[2,512,128]{2,1,0:T(8,128)(2,1)S(1)} %get-tuple-element.20), channel_id=1, source_target_pairs={{16,8},{24,0},{32,24},{40,16},{48,40},{56,32},{64,56},{72,48},{80,... | collective-permute-start | bytes 786440 | tf_op jit(solution)/shard_map/ppermute | solution.py:327
  79.5 3.8 %collective-permute-start.1 = (bf16[4,512,128]{2,1,0:T(8,128)(2,1)S(1)}, bf16[4,512,128]{2,1,0:T(8,128)(2,1)S(1)}, u32[]{:S(2)}, u32[]{:S(2)}) collective-permute-start(bf16[4,512,128]{2,1,0:T(8,128)(2,1)S(1)} %get-tuple-element.19), channel_id=1, source_target_pairs={{0,8},{8,0},{1,9},{9,1},{2,10},{10,2},{3,11},{11,3},{4,12},{12,4},... | collective-permute-start | bytes 1572872 | tf_op jit(solution)/shard_map/ppermute | solution.py:333

commit v8 on v7

--- a/solution.py
+++ b/solution.py
@@ -120,7 +120,7 @@
     return jnp.concatenate(rows[0:2], axis=1), jnp.concatenate(rows[2:4], axis=1)
 
 
-def sweep(strips, causal, key_base, kv_ref, q_ref, lo_ref, dk_ref, dv_ref, dq_ref, part_ref):
+def sweep(strips, causal, key_base, kv_ref, q_ref, lo_ref, dk_ref, dv_ref, dq_ref, part_ref, first_query=0):
     pieces = CHUNK // PIECE
     base = strips[0][1]
     for n, (at, first, last) in enumerate(strips):
@@ -145,7 +145,7 @@
         key_at = lax.broadcasted_iota(jnp.int32, (height, 2 * CHUNK), 0)
         allowed = key_at >= lo
         if causal:
-            query_at = lax.broadcasted_iota(jnp.int32, (1, 2 * CHUNK), 1) % CHUNK + at * CHUNK
+            query_at = lax.broadcasted_iota(jnp.int32, (1, 2 * CHUNK), 1) % CHUNK + (at - first) * CHUNK
             allowed = allowed & (key_at <= query_at)
         scores = dot_t(key, query)
         prob = jnp.where(allowed, jnp.exp2(scores * (score_scale * log2_e) - lse), 0.0)
@@ -162,9 +162,10 @@
         dq = t_dot(score_grad, key)
         for a in range(2):
             mine = dq[a * CHUNK : (a + 1) * CHUNK]
+            rows = slice((at - first_query) * CHUNK, (at - first_query + 1) * CHUNK)
             if part_ref is not None:
-                mine = mine + part_ref[a, at * CHUNK : (at + 1) * CHUNK, :]
-            dq_ref[a, at * CHUNK : (at + 1) * CHUNK, :] = mine
+                mine = mine + part_ref[a, rows, :]
+            dq_ref[a, rows, :] = mine
 
 
 def cross_kernel(near, core_ref, kv_ref, q_ref, lo_ref, *refs):
@@ -187,21 +188,44 @@
             out_ref[1] = dv_ref[...].astype(bf16)
 
 
-def own_kernel(core_ref, kv_ref, q_ref, lo_ref, part_ref, near_dq_ref, near_ref, far_ref, dk_ref, dv_ref, dq_ref):
+def own_far_kernel(core_ref, kv_ref, q_ref, lo_ref, part_ref, far_ref, near_dq_ref, near_ref, dk_ref, dv_ref, dq_ref):
     chunks = LOOKBACK_SPAN // CHUNK
-    sweep(
-        [(at, 0, at + 1) for at in range(chunks - 1, -1, -1)],
-        True, LOOKBACK_SPAN, kv_ref, q_ref, lo_ref, dk_ref, dv_ref, dq_ref, part_ref,
-    )
-    near = pl.ds(pl.multiple_of(core_ref[0] * HALF, HALF), HALF)
-    far = pl.ds(pl.multiple_of((1 - core_ref[0]) * HALF, HALF), HALF)
-    for a in range(2):
-        near_dq_ref[a] = dq_ref[a, near, :].astype(bf16)
-        far_ref[a] = dq_ref[a, far, :].astype(bf16)
-    near_ref[0] = dk_ref[near, :]
-    near_ref[1] = dv_ref[near, :]
-    far_ref[2] = dk_ref[far, :].astype(bf16)
-    far_ref[3] = dv_ref[far, :].astype(bf16)
+    half = chunks // CORES
+    upper = [(at, 0, at + 1) for at in range(chunks - 1, half - 1, -1)]
+    across = [(at, 0, half) for at in range(half, chunks)]
+    lower = [(at, 0, at + 1) for at in range(half)]
+    for core, strips in enumerate((upper, across + lower)):
+
+        @pl.when(core_ref[0] == core)
+        def _():
+            sweep(
+                strips, True, LOOKBACK_SPAN, kv_ref, q_ref, lo_ref, dk_ref, dv_ref, dq_ref, part_ref,
+            )
+            near = slice(core * HALF, (core + 1) * HALF)
+            far = slice((1 - core) * HALF, (2 - core) * HALF)
+            near_dq_ref[...] = part_ref[:, near, :] if core == 0 else dq_ref[:, near, :]
+            far_ref[0:2] = dq_ref[:, far, :].astype(bf16)
+            for i, sum_ref in enumerate((dk_ref, dv_ref)):
+                far_ref[2 + i] = sum_ref[far, :].astype(bf16)
+                near_ref[i] = sum_ref[near, :] if core == 0 else jnp.zeros_like(near_ref[i])
+
+
+def own_near_kernel(core_ref, kv_ref, q_ref, lo_ref, part_dq_ref, part_ref, dq_out_ref, near_ref, dk_ref, dv_ref, dq_ref):
+    chunks = LOOKBACK_SPAN // CHUNK
+    half = chunks // CORES
+    for core in range(CORES):
+
+        @pl.when(core_ref[0] == core)
+        def _():
+            start = core * half
+            sweep(
+                [(at, start, at + 1) for at in range(start + half - 1, start - 1, -1)],
+                True, LOOKBACK_SPAN, kv_ref, q_ref, lo_ref, dk_ref, dv_ref, dq_ref, part_dq_ref, start,
+            )
+
+    dq_out_ref[...] = dq_ref[...].astype(bf16)
+    near_ref[0] = part_ref[0] + dk_ref[...]
+    near_ref[1] = part_ref[1] + dv_ref[...]
 
 
 def vmem_spec():
@@ -240,21 +264,17 @@
     )(core, kv, q, lo, *part)
 
 
-def own_terms(core, kv, q, lo, part):
-    return pl.pallas_call(
-        own_kernel,
-        in_specs=[smem_spec()] + [vmem_spec()] * 4,
-        out_specs=[vmem_spec()] * 3,
-        out_shape=[
-            jax.ShapeDtypeStruct((2, HALF, HEAD_SIZE), bf16),
-            jax.ShapeDtypeStruct((2, HALF, HEAD_SIZE), f32),
-            jax.ShapeDtypeStruct((4, HALF, HEAD_SIZE), bf16),
-        ],
-        scratch_shapes=rows_scratch(LOOKBACK_SPAN) + [pltpu.VMEM((2, LOOKBACK_SPAN, HEAD_SIZE), f32)],
+def own_call(kernel, name, shapes, rows, *operands):
+    return pl.pallas_call(
+        kernel,
+        in_specs=[smem_spec()] + [vmem_spec()] * (len(operands) - 1),
+        out_specs=[vmem_spec()] * len(shapes),
+        out_shape=[jax.ShapeDtypeStruct((count, HALF, HEAD_SIZE), kind) for count, kind in shapes],
+        scratch_shapes=rows_scratch(rows) + [pltpu.VMEM((2, rows, HEAD_SIZE), f32)],
         compiler_params=pltpu.CompilerParams(vmem_limit_bytes=20 << 20),
         cost_estimate=cost(),
-        name="own_terms",
-    )(core, kv, q, lo, part)
+        name=name,
+    )(*operands)
 
 
 def join_near_kernel(core_ref, near_ref, back_ref, dk_ref, dv_ref):
@@ -329,8 +349,13 @@
         ("chip", "core"),
         [(CORES * (c + 1) + k, CORES * c + 1 - k) for c in range(chips - 1) for k in range(CORES)],
     )
-    near_dq, own_near, own_far = own_terms(core, kv, q, lo, dq_part)
+    own_far, near_dq, own_near = own_call(
+        own_far_kernel, "own_far", [(4, bf16), (2, f32), (2, f32)], LOOKBACK_SPAN, core, kv, q, lo, dq_part
+    )
     swapped = lax.ppermute(own_far, "core", [(0, 1), (1, 0)])
+    near_dq, own_near = own_call(
+        own_near_kernel, "own_near", [(2, bf16), (2, f32)], HALF, core, kv, q, lo, near_dq, own_near
+    )
     keys_shape = jax.ShapeDtypeStruct((HALF, 2 * HEAD_SIZE), bf16)
     queries_shape = jax.ShapeDtypeStruct((HALF, 4 * HEAD_SIZE), bf16)
     halves = join(join_near_kernel, "join_near", [keys_shape] * 2, 10000, core, own_near, back_near)

time: 85.7 us -> 84.8 us (0.989)
    pallas_call x1 -> x2, Pallas kernels: 3.9 us -> 4.68 us  [own_call(): pl.pallas_call(kernel, in_specs=[smem_spec()] + [vmem_spec()] * (len(oper...]
  transfers between devices with their start and end apart: 6 -> 6, of which waited for: 5 -> 4; matrix products, arithmetic and copies ran while one was open for 1% -> 1% of each run, Pallas kernels for 11% -> 12%
where the time goes in v8:
time: 84.8 us; the launch traced here: 84.3 us
  waiting for transfers between devices  33.7 us (40%)
  starting transfers between devices  32.5 us (38%)
  Pallas kernels  16.3 us (19%)
  other arithmetic  0.99 us (1%)
    ppermute x1, waiting for transfers between devices, on_device(): kv_before = lax.ppermute(kv, 'chip', [(c, c + 1) for c in range(chips - 1)])  18.1 us
    all_to_all x2, waiting for transfers between devices, exchange(): lax.all_to_all(value, ('core', 'head'), split_axis=0, concat_axis=0, tile...  14.6 us
    all_to_all x2, starting transfers between devices, exchange(): lax.all_to_all(value, ('core', 'head'), split_axis=0, concat_axis=0, tile...  13.4 us
    ppermute x1, starting transfers between devices, on_device(): lax.ppermute(near, 'chip', [(c + 1, c) for c in range(chips - 1)])  10.9 us
    pallas_call x2, Pallas kernels, own_call(): pl.pallas_call(kernel, in_specs=[smem_spec()] + [vmem_spec()] * (len(oper...  4.68 us
    pallas_call x2, Pallas kernels, cross_terms(): pl.pallas_call(functools.partial(cross_kernel, near), in_specs=[smem_spec...  4.28 us
    pallas_call x1, Pallas kernels, pack_queries(): pl.pallas_call(pack_queries_kernel, grid=(steps,), in_specs=[pl.BlockSpec...  4.27 us
    ppermute x1, starting transfers between devices, on_device(): kv_before = lax.ppermute(kv, 'chip', [(c, c + 1) for c in range(chips - 1)])  4.03 us
  transfers between devices with their start and end apart: 6, of which 4 were waited for; matrix products, arithmetic and copies ran while one was open for 1% of the time, Pallas kernels for 12%

profile of v8, /device:TPU:7, one launch (start us, length us, event | category | flops | bytes accessed | tf_op | source)
XLA Modules:
  0.0 84.3 jit_solution(17387330899953471142)
XLA Ops:
  0.6 1.9 %pack_keys.1 = bf16[2,8,128,128]{3,2,1,0:T(8,128)(2,1)} custom-call(bf16[64,2048]{1,0:T(8,128)(2,1)} %key_ref.1, bf16[64,2048]{1,0:T(8,128)(2,1)} %value_ref.1), custom_call_target="tpu_custom_call" | custom-call | tf_op jit(solution)/shard_map/pack_keys/pallas_call | solution.py:47
  2.5 7.8 %all-to-all-start = ((bf16[16,128,128]{2,1,0:T(8,128)(2,1)}), bf16[16,128,128]{2,1,0:T(8,128)(2,1)S(1)}, u32[]{:S(2)}, u32[]{:S(2)}) async-start(bf16[16,128,128]{2,1,0:T(8,128)(2,1)} %bitcast.5), calls=%async_computation | async-start | bytes 1048576 | tf_op jit(solution)/shard_map/all_to_all | solution.py:330
  10.3 4.3 %pack_queries.1 = bf16[2,8,264,128]{3,2,1,0:T(8,128)(2,1)} custom-call(bf16[64,4096]{1,0:T(8,128)(2,1)} %query_ref.1, bf16[64,4096]{1,0:T(8,128)(2,1)} %grad_ref.1, bf16[64,4096]{1,0:T(8,128)(2,1)} %row_ref.1, f32[32,64]{1,0:T(8,128)} %lse_ref.1), custom_call_target="tpu_custom_call" | custom-call | tf_op jit(solution)/shard_map/pack_queries/pallas_call | solution.py:102
  14.6 10.5 %all-to-all-done.kv_ref = bf16[16,128,128]{2,1,0:T(8,128)(2,1)S(1)} async-done(((bf16[16,128,128]{2,1,0:T(8,128)(2,1)}), bf16[16,128,128]{2,1,0:T(8,128)(2,1)S(1)}, u32[]{:S(2)}, u32[]{:S(2)}) %all-to-all-start) | async-done | bytes 524320 | tf_op jit(solution)/shard_map/all_to_all | solution.py:330
  25.1 0.0 copy-start
  25.1 5.6 %all-to-all-start.1 = ((bf16[16,264,128]{2,1,0:T(8,128)(2,1)}), bf16[16,264,128]{2,1,0:T(8,128)(2,1)S(1)}, u32[]{:S(2)}, u32[]{:S(2)}) async-start(bf16[16,264,128]{2,1,0:T(8,128)(2,1)} %bitcast.4), calls=%async_computation.1 | async-start | bytes 2162688 | tf_op jit(solution)/shard_map/all_to_all | solution.py:330
  30.6 0.0 copy-done
  30.7 4.0 %collective-permute-start = (bf16[16,128,128]{2,1,0:T(8,128)(2,1)S(1)}, bf16[16,128,128]{2,1,0:T(8,128)(2,1)S(1)}, u32[]{:S(2)}, u32[]{:S(2)}) collective-permute-start(bf16[16,128,128]{2,1,0:T(8,128)(2,1)S(1)} %all-to-all-done.kv_ref), channel_id=1, source_target_pairs={{0,16},{16,32},{32,48},{48,64},{64,80},{80,96},{96,112},{112,128},... | collective-permute-start | bytes 1572872 | tf_op jit(solution)/shard_map/ppermute | solution.py:343
  34.7 1.0 %convert_reduce_fusion = s32[1024]{0:T(1024)S(1)} fusion(s32[1024]{0:T(1024)S(1)} %pad_dynamic-slice_fusion, s32[2048]{0:T(1024)S(1)} %pad_dynamic-slice_fusion.1), kind=kLoop, calls=%fused_computation | loop fusion | flops 6290432 | bytes 16384 | tf_op jit(solution)/shard_map/reduce_sum | solution.py:323
  35.7 18.1 %collective-permute-done.kv_ref = bf16[16,128,128]{2,1,0:T(8,128)(2,1)S(1)} collective-permute-done((bf16[16,128,128]{2,1,0:T(8,128)(2,1)S(1)}, bf16[16,128,128]{2,1,0:T(8,128)(2,1)S(1)}, u32[]{:S(2)}, u32[]{:S(2)}) %collective-permute-start) | collective-permute-done | bytes 524320 | tf_op jit(solution)/shard_map/ppermute | solution.py:343
  53.8 4.1 %all-to-all-done.1.q_ref = bf16[16,264,128]{2,1,0:T(8,128)(2,1)S(1)} async-done(((bf16[16,264,128]{2,1,0:T(8,128)(2,1)}), bf16[16,264,128]{2,1,0:T(8,128)(2,1)S(1)}, u32[]{:S(2)}, u32[]{:S(2)}) %all-to-all-start.1) | async-done | bytes 1081376 | tf_op jit(solution)/shard_map/all_to_all | solution.py:330
  57.9 2.9 %cross_near.1 = (f32[2,1024,128]{2,1,0:T(8,128)S(1)}, bf16[2,512,128]{2,1,0:T(8,128)(2,1)S(1)}) custom-call(s32[1]{0:T(128)} %bitcast.core_ref, bf16[16,128,128]{2,1,0:T(8,128)(2,1)S(1)} %collective-permute-done.kv_ref, bf16[16,264,128]{2,1,0:T(8,128)(2,1)S(1)} %all-to-all-done.1.q_ref, s32[8,1,128]{2,1,0:T(1,128)S(1)} %add_maximum_fusion.lo_ref), custom_call_target="tpu_custom_call" | custom-call | flops 1342177280 | bytes 4194304 | tf_op jit(solution)/shard_map/cross_near/pallas_call | solution.py:252
  60.8 10.9 %collective-permute-start.3 = (bf16[2,512,128]{2,1,0:T(8,128)(2,1)S(1)}, bf16[2,512,128]{2,1,0:T(8,128)(2,1)S(1)}, u32[]{:S(2)}, u32[]{:S(2)}) collective-permute-start(bf16[2,512,128]{2,1,0:T(8,128)(2,1)S(1)} %get-tuple-element.26), channel_id=1, source_target_pairs={{16,0},{32,16},{48,32},{64,48},{80,64},{96,80},{112,96},{128,112},... | collective-permute-start | bytes 786440 | tf_op jit(solution)/shard_map/ppermute | solution.py:345
  71.7 1.4 %cross_far.1 = (f32[2,1024,128]{2,1,0:T(8,128)S(1)}, bf16[2,512,128]{2,1,0:T(8,128)(2,1)S(1)}) custom-call(s32[1]{0:T(128)} %bitcast.core_ref, bf16[16,128,128]{2,1,0:T(8,128)(2,1)S(1)} %collective-permute-done.kv_ref, bf16[16,264,128]{2,1,0:T(8,128)(2,1)S(1)} %all-to-all-done.1.q_ref, s32[8,1,128]{2,1,0:T(1,128)S(1)} %add_maximum_fusion.lo_ref, ...), custom_call_target="tpu_custom_call" | custom-call | flops 1342177280 | bytes 4194304 | tf_op jit(solution)/shard_map/cross_far/pallas_call | solution.py:252
  73.1 2.2 %collective-permute-start.2 = (bf16[2,512,128]{2,1,0:T(8,128)(2,1)S(1)}, bf16[2,512,128]{2,1,0:T(8,128)(2,1)S(1)}, u32[]{:S(2)}, u32[]{:S(2)}) collective-permute-start(bf16[2,512,128]{2,1,0:T(8,128)(2,1)S(1)} %get-tuple-element.24), channel_id=1, source_target_pairs={{16,8},{24,0},{32,24},{40,16},{48,40},{56,32},{64,56},{72,48},{80,... | collective-permute-start | bytes 786440 | tf_op jit(solution)/shard_map/ppermute | solution.py:347
  75.4 3.2 %own_far.1 = (bf16[4,512,128]{2,1,0:T(8,128)(2,1)S(1)}, f32[2,512,128]{2,1,0:T(8,128)S(1)}, f32[2,512,128]{2,1,0:T(8,128)S(1)}) custom-call(s32[1]{0:T(128)} %bitcast.core_ref, bf16[16,128,128]{2,1,0:T(8,128)(2,1)S(1)} %all-to-all-done.kv_ref, bf16[16,264,128]{2,1,0:T(8,128)(2,1)S(1)} %all-to-all-done.1.q_ref, s32[8,1,128]{2,1,0:T(1,128)S(1)} %add_maximum_fusion.lo_ref, ...), custom_call_target="tpu_custom_call" | custom-call | flops 1342177280 | bytes 4194304 | tf_op jit(solution)/shard_map/own_far/pallas_call | solution.py:268
  78.5 1.9 %collective-permute-start.1 = (bf16[4,512,128]{2,1,0:T(8,128)(2,1)S(1)}, bf16[4,512,128]{2,1,0:T(8,128)(2,1)S(1)}, u32[]{:S(2)}, u32[]{:S(2)}) collective-permute-start(bf16[4,512,128]{2,1,0:T(8,128)(2,1)S(1)} %get-tuple-element.23), channel_id=1, source_target_pairs={{0,8},{8,0},{1,9},{9,1},{2,10},{10,2},{3,11},{11,3},{4,12},{12,4},... | collective-permute-start | bytes 1572872 | tf_op jit(solution)/shard_map/ppermute | solution.py:355
  80.5 1.5 %own_near.1 = (bf16[2,512,128]{2,1,0:T(8,128)(2,1)S(1)}, f32[2,512,128]{2,1,0:T(8,128)S(1)}) custom-call(s32[1]{0:T(128)} %bitcast.core_ref, bf16[16,128,128]{2,1,0:T(8,128)(2,1)S(1)} %all-to-all-done.kv_ref, bf16[16,264,128]{2,1,0:T(8,128)(2,1)S(1)} %all-to-all-done.1.q_ref, s32[8,1,128]{2,1,0:T(1,128)S(1)} %add_maximum_fusion.lo_ref, ...), custom_call_target="tpu_custom_call" | custom-call | flops 1342177280 | bytes 4194304 | tf_op jit(solution)/shard_map/own_near/pallas_call | solution.py:268
  82.0 0.0 collective-permute-done.3.back_ref
  82.0 0.1 join_near.1
  82.1 1.0 %collective-permute-done.2.back_ref = bf16[2,512,128]{2,1,0:T(8,128)(2,1)S(1)} collective-permute-done((bf16[2,512,128]{2,1,0:T(8,128)(2,1)S(1)}, bf16[2,512,128]{2,1,0:T(8,128)(2,1)S(1)}, u32[]{:S(2)}, u32[]{:S(2)}) %collective-permute-start.2) | collective-permute-done | bytes 262176 | tf_op jit(solution)/shard_map/ppermute | solution.py:347
  83.1 0.0 collective-permute-done.1.swapped_ref
  83.1 1.2 %join_far.1 = (bf16[512,512]{1,0:T(8,128)(2,1)}, bf16[512,256]{1,0:T(8,128)(2,1)}, bf16[512,256]{1,0:T(8,128)(2,1)}) custom-call(s32[1]{0:T(128)} %bitcast.core_ref, bf16[2,512,128]{2,1,0:T(8,128)(2,1)S(1)} %get-tuple-element.22.near_dq_ref, bf16[4,512,128]{2,1,0:T(8,128)(2,1)S(1)} %collective-permute-done.1.swapped_ref, ...), custom_call_target="tpu_custom_call" | custom-call | flops 1048576 | bytes 1048576 | tf_op jit(solution)/shard_map/join_far/pallas_call | solution.py:308
  (3 shorter events, 0.0 us)
Async XLA Ops:
  2.5 22.6 %all-to-all-start = ((bf16[16,128,128]{2,1,0:T(8,128)(2,1)}), bf16[16,128,128]{2,1,0:T(8,128)(2,1)S(1)}, u32[]{:S(2)}, u32[]{:S(2)}) async-start(bf16[16,128,128]{2,1,0:T(8,128)(2,1)} %bitcast.5), calls=%async_computation | async-start | bytes 1048576 | tf_op jit(solution)/shard_map/all_to_all | solution.py:330
  25.1 5.6 %copy-start = (s32[32768]{0:T(1024)S(1)}, s32[32768]{0:T(1024)}, u32[]{:S(2)}) copy-start(s32[32768]{0:T(1024)} %param.13) | copy-start | bytes 393220
  25.1 32.8 %all-to-all-start.1 = ((bf16[16,264,128]{2,1,0:T(8,128)(2,1)}), bf16[16,264,128]{2,1,0:T(8,128)(2,1)S(1)}, u32[]{:S(2)}, u32[]{:S(2)}) async-start(bf16[16,264,128]{2,1,0:T(8,128)(2,1)} %bitcast.4), calls=%async_computation.1 | async-start | bytes 2162688 | tf_op jit(solution)/shard_map/all_to_all | solution.py:330
  30.7 23.1 %collective-permute-start = (bf16[16,128,128]{2,1,0:T(8,128)(2,1)S(1)}, bf16[16,128,128]{2,1,0:T(8,128)(2,1)S(1)}, u32[]{:S(2)}, u32[]{:S(2)}) collective-permute-start(bf16[16,128,128]{2,1,0:T(8,128)(2,1)S(1)} %all-to-all-done.kv_ref), channel_id=1, source_target_pairs={{0,16},{16,32},{32,48},{48,64},{64,80},{80,96},{96,112},{112,128},... | collective-permute-start | bytes 1572872 | tf_op jit(solution)/shard_map/ppermute | solution.py:343
  60.8 21.2 %collective-permute-start.3 = (bf16[2,512,128]{2,1,0:T(8,128)(2,1)S(1)}, bf16[2,512,128]{2,1,0:T(8,128)(2,1)S(1)}, u32[]{:S(2)}, u32[]{:S(2)}) collective-permute-start(bf16[2,512,128]{2,1,0:T(8,128)(2,1)S(1)} %get-tuple-element.26), channel_id=1, source_target_pairs={{16,0},{32,16},{48,32},{64,48},{80,64},{96,80},{112,96},{128,112},... | collective-permute-start | bytes 786440 | tf_op jit(solution)/shard_map/ppermute | solution.py:345
  73.1 10.0 %collective-permute-start.2 = (bf16[2,512,128]{2,1,0:T(8,128)(2,1)S(1)}, bf16[2,512,128]{2,1,0:T(8,128)(2,1)S(1)}, u32[]{:S(2)}, u32[]{:S(2)}) collective-permute-start(bf16[2,512,128]{2,1,0:T(8,128)(2,1)S(1)} %get-tuple-element.24), channel_id=1, source_target_pairs={{16,8},{24,0},{32,24},{40,16},{48,40},{56,32},{64,56},{72,48},{80,... | collective-permute-start | bytes 786440 | tf_op jit(solution)/shard_map/ppermute | solution.py:347
  78.5 4.6 %collective-permute-start.1 = (bf16[4,512,128]{2,1,0:T(8,128)(2,1)S(1)}, bf16[4,512,128]{2,1,0:T(8,128)(2,1)S(1)}, u32[]{:S(2)}, u32[]{:S(2)}) collective-permute-start(bf16[4,512,128]{2,1,0:T(8,128)(2,1)S(1)} %get-tuple-element.23), channel_id=1, source_target_pairs={{0,8},{8,0},{1,9},{9,1},{2,10},{10,2},{3,11},{11,3},{4,12},{12,4},... | collective-permute-start | bytes 1572872 | tf_op jit(solution)/shard_map/ppermute | solution.py:355

commit v9 on v8

--- a/solution.py
+++ b/solution.py
@@ -36,20 +36,20 @@
 
 
 def pack_keys_kernel(key_ref, value_ref, out_ref):
-    for at in range(CORES * out_ref.shape[1]):
+    for at in range(out_ref.shape[0]):
         columns = slice(at * HEAD_SIZE, (at + 1) * HEAD_SIZE)
-        out_ref[at % CORES, at // CORES, 0:PIECE, :] = key_ref[:, columns]
-        out_ref[at % CORES, at // CORES, PIECE : 2 * PIECE, :] = value_ref[:, columns]
-
-
-def pack_keys(keys, values, groups, steps=2):
-    width = keys.shape[1] // steps
+        out_ref[at, 0:PIECE, :] = key_ref[:, columns]
+        out_ref[at, PIECE : 2 * PIECE, :] = value_ref[:, columns]
+
+
+def pack_keys(keys, values, steps=2):
+    heads = keys.shape[1] // HEAD_SIZE
     return pl.pallas_call(
         pack_keys_kernel,
         grid=(steps,),
-        in_specs=[pl.BlockSpec((PIECE, width), lambda i: (0, i))] * 2,
-        out_specs=pl.BlockSpec((CORES, groups // steps, 2 * PIECE, HEAD_SIZE), lambda i: (0, i, 0, 0)),
-        out_shape=jax.ShapeDtypeStruct((CORES, groups, 2 * PIECE, HEAD_SIZE), bf16),
+        in_specs=[pl.BlockSpec((PIECE, keys.shape[1] // steps), lambda i: (0, i))] * 2,
+        out_specs=pl.BlockSpec((heads // steps, 2 * PIECE, HEAD_SIZE), lambda i: (i, 0, 0)),
+        out_shape=jax.ShapeDtypeStruct((heads, 2 * PIECE, HEAD_SIZE), bf16),
         name="pack_keys",
     )(keys, values)
 
@@ -120,15 +120,26 @@
     return jnp.concatenate(rows[0:2], axis=1), jnp.concatenate(rows[2:4], axis=1)
 
 
-def sweep(strips, causal, key_base, kv_ref, q_ref, lo_ref, dk_ref, dv_ref, dq_ref, part_ref, first_query=0):
+def key_rows(refs, first, last, row):
+    per_block = LOOKBACK_SPAN // CORES // CHUNK
+    pieces = CHUNK // PIECE
+    found = []
+    for block in range(CORES):
+        start, end = max(first, block * per_block), min(last, (block + 1) * per_block)
+        if start < end:
+            at = slice((start - block * per_block) * pieces, (end - block * per_block) * pieces)
+            found.append(refs[block][at, row : row + PIECE, :].reshape((end - start) * CHUNK, HEAD_SIZE))
+    return found[0] if len(found) == 1 else jnp.concatenate(found)
+
+
+def sweep(strips, causal, key_base, kv_refs, q_ref, lo_ref, dk_ref, dv_ref, dq_ref, part_ref, first_query=0):
     pieces = CHUNK // PIECE
     base = strips[0][1]
     for n, (at, first, last) in enumerate(strips):
         strip = slice((first - base) * CHUNK, (last - base) * CHUNK)
         height = (last - first) * CHUNK
-        sources = slice(first * pieces, last * pieces)
-        key = kv_ref[sources, 0:PIECE, :].reshape(height, HEAD_SIZE)
-        value = kv_ref[sources, PIECE : 2 * PIECE, :].reshape(height, HEAD_SIZE)
+        key = key_rows(kv_refs, first, last, 0)
+        value = key_rows(kv_refs, first, last, PIECE)
         sources = slice(at * pieces, (at + 1) * pieces)
 
         def both(row):
@@ -179,7 +190,7 @@
             start, end = block * chunks // CORES, (block + 1) * chunks // CORES
             sweep(
                 [(at, max(at, start), end) for at in range(end)],
-                False, 0, kv_ref, q_ref, lo_ref, dk_ref, dv_ref, dq_ref, part_ref,
+                False, 0, (kv_ref, kv_ref), q_ref, lo_ref, dk_ref, dv_ref, dq_ref, part_ref,
             )
             rest = slice(end * CHUNK, LOOKBACK_SPAN)
             if end < chunks:
@@ -188,7 +199,7 @@
             out_ref[1] = dv_ref[...].astype(bf16)
 
 
-def own_far_kernel(core_ref, kv_ref, q_ref, lo_ref, part_ref, far_ref, near_dq_ref, near_ref, dk_ref, dv_ref, dq_ref):
+def own_far_kernel(core_ref, kv_near_ref, kv_far_ref, q_ref, lo_ref, part_ref, far_ref, near_dq_ref, near_ref, dk_ref, dv_ref, dq_ref):
     chunks = LOOKBACK_SPAN // CHUNK
     half = chunks // CORES
     upper = [(at, 0, at + 1) for at in range(chunks - 1, half - 1, -1)]
@@ -198,8 +209,9 @@
 
         @pl.when(core_ref[0] == core)
         def _():
+            kv_refs = (kv_near_ref, kv_far_ref) if core == 0 else (kv_far_ref, kv_near_ref)
             sweep(
-                strips, True, LOOKBACK_SPAN, kv_ref, q_ref, lo_ref, dk_ref, dv_ref, dq_ref, part_ref,
+                strips, True, LOOKBACK_SPAN, kv_refs, q_ref, lo_ref, dk_ref, dv_ref, dq_ref, part_ref,
             )
             near = slice(core * HALF, (core + 1) * HALF)
             far = slice((1 - core) * HALF, (2 - core) * HALF)
@@ -220,7 +232,7 @@
             start = core * half
             sweep(
                 [(at, start, at + 1) for at in range(start + half - 1, start - 1, -1)],
-                True, LOOKBACK_SPAN, kv_ref, q_ref, lo_ref, dk_ref, dv_ref, dq_ref, part_dq_ref, start,
+                True, LOOKBACK_SPAN, (kv_ref, kv_ref), q_ref, lo_ref, dk_ref, dv_ref, dq_ref, part_dq_ref, start,
             )
 
     dq_out_ref[...] = dq_ref[...].astype(bf16)
@@ -325,36 +337,51 @@
     return jnp.maximum(document_start, reach_start).reshape(LOOKBACK_SPAN // CHUNK, 1, CHUNK)
 
 
-def exchange(value):
-    value = value.reshape((-1,) + value.shape[2:])
-    return lax.all_to_all(value, ("core", "head"), split_axis=0, concat_axis=0, tiled=True)
+def exchange(value, axes):
+    return lax.all_to_all(value, axes, split_axis=0, concat_axis=0, tiled=True)
+
+
+def other_core(value):
+    return lax.ppermute(value, "core", [(0, 1), (1, 0)])
+
+
+def next_chip(value, step, cross):
+    chips = lax.axis_size("chip")
+    pairs = [
+        (CORES * c + k, CORES * (c + step) + (1 - k if cross else k))
+        for c in range(max(0, -step), min(chips, chips - step))
+        for k in range(CORES)
+    ]
+    return lax.ppermute(value, ("chip", "core"), pairs)
 
 
 def on_device(queries, keys, values, rows, grads, lse, doc_ids):
-    chips = lax.axis_size("chip")
     groups = lax.axis_size("head")
     chip = lax.axis_index("chip")
-    core = lax.axis_index("core").astype(jnp.int32).reshape(1)
+    core_at = lax.axis_index("core").astype(jnp.int32)
+    core = core_at.reshape(1)
     lo = first_allowed(doc_ids, chip)
-    kv = exchange(pack_keys(keys, values, groups))
+    kv = exchange(pack_keys(keys, values).reshape(groups, CORES, 2 * PIECE, HEAD_SIZE), "head")
     packed = pack_queries(queries, grads, rows, lse, groups)
+    packed = packed.reshape((-1,) + packed.shape[2:])
     kv, packed = lax.optimization_barrier((kv, packed))
-    q = exchange(packed)
-    kv_before = lax.ppermute(kv, "chip", [(c, c + 1) for c in range(chips - 1)])
-    dq_part, near = cross_terms(True, core, kv_before, q, lo)
-    back_near = lax.ppermute(near, "chip", [(c + 1, c) for c in range(chips - 1)])
-    dq_part, far = cross_terms(False, core, kv_before, q, lo, dq_part)
-    back_far = lax.ppermute(
-        far,
-        ("chip", "core"),
-        [(CORES * (c + 1) + k, CORES * c + 1 - k) for c in range(chips - 1) for k in range(CORES)],
+    q = exchange(packed, ("core", "head"))
+    kv_near = jnp.where(core_at == 0, kv[:, 0], kv[:, 1])
+    kv_give = jnp.where(core_at == 0, kv[:, 1], kv[:, 0])
+    before_near = next_chip(kv_near, 1, False)
+    before_far = next_chip(kv_give, 1, True)
+    kv_far = other_core(kv_give)
+    dq_part, near = cross_terms(True, core, before_near, q, lo)
+    back_near = next_chip(near, -1, False)
+    dq_part, far = cross_terms(False, core, before_far, q, lo, dq_part)
+    back_far = next_chip(far, -1, True)
+    own_far, near_dq, own_near = own_call(
+        own_far_kernel, "own_far", [(4, bf16), (2, f32), (2, f32)], LOOKBACK_SPAN,
+        core, kv_near, kv_far, q, lo, dq_part,
     )
-    own_far, near_dq, own_near = own_call(
-        own_far_kernel, "own_far", [(4, bf16), (2, f32), (2, f32)], LOOKBACK_SPAN, core, kv, q, lo, dq_part
-    )
-    swapped = lax.ppermute(own_far, "core", [(0, 1), (1, 0)])
+    swapped = other_core(own_far)
     near_dq, own_near = own_call(
-        own_near_kernel, "own_near", [(2, bf16), (2, f32)], HALF, core, kv, q, lo, near_dq, own_near
+        own_near_kernel, "own_near", [(2, bf16), (2, f32)], HALF, core, kv_near, q, lo, near_dq, own_near
     )
     keys_shape = jax.ShapeDtypeStruct((HALF, 2 * HEAD_SIZE), bf16)
     queries_shape = jax.ShapeDtypeStruct((HALF, 4 * HEAD_SIZE), bf16)

time: 84.8 us -> 85.7 us (1.011)
  starting transfers between devices: 32.5 us -> 36.5 us
  waiting for transfers between devices: 33.7 us -> 30.5 us
    ppermute x4 -> x6, waiting for transfers between devices: 19.1 us -> 7.2 us  [the longest x4 7.2 us: next_chip(): return lax.ppermute(value, ('chip', 'core'), pairs)]
    all_to_all x2, waiting for transfers between devices: 14.6 us -> 23.3 us  [exchange(): return lax.all_to_all(value, axes, split_axis=0, concat_axis=0, tiled=True)]
    ppermute x4 -> x6, starting transfers between devices: 19.1 us -> 25.5 us  [the longest x4 21.6 us: next_chip(): return lax.ppermute(value, ('chip', 'core'), pairs)]
    all_to_all x2, starting transfers between devices: 13.4 us -> 11 us  [exchange(): return lax.all_to_all(value, axes, split_axis=0, concat_axis=0, tiled=True)]
  transfers between devices with their start and end apart: 6 -> 8, of which waited for: 4 -> 4; matrix products, arithmetic and copies ran while one was open for 1% -> 1% of each run, Pallas kernels for 12% -> 16%
where the time goes in v9:
time: 85.7 us; the launch traced here: 85.2 us
  starting transfers between devices  36.5 us (43%)
  waiting for transfers between devices  30.5 us (36%)
  Pallas kernels  16.3 us (19%)
  other arithmetic  1.1 us (1%)
    all_to_all x2, waiting for transfers between devices, exchange(): return lax.all_to_all(value, axes, split_axis=0, concat_axis=0, tiled=True)  23.3 us
    ppermute x4, starting transfers between devices, next_chip(): return lax.ppermute(value, ('chip', 'core'), pairs)  21.6 us
    all_to_all x2, starting transfers between devices, exchange(): return lax.all_to_all(value, axes, split_axis=0, concat_axis=0, tiled=True)  11 us
    ppermute x4, waiting for transfers between devices, next_chip(): return lax.ppermute(value, ('chip', 'core'), pairs)  7.2 us
    pallas_call x2, Pallas kernels, own_call(): pl.pallas_call(kernel, in_specs=[smem_spec()] + [vmem_spec()] * (len(oper...  4.68 us
    pallas_call x2, Pallas kernels, cross_terms(): pl.pallas_call(functools.partial(cross_kernel, near), in_specs=[smem_spec...  4.29 us
    pallas_call x1, Pallas kernels, pack_queries(): pl.pallas_call(pack_queries_kernel, grid=(steps,), in_specs=[pl.BlockSpec...  4.28 us
    ppermute x2, starting transfers between devices, other_core(): return lax.ppermute(value, 'core', [(0, 1), (1, 0)])  3.87 us
  transfers between devices with their start and end apart: 8, of which 4 were waited for; matrix products, arithmetic and copies ran while one was open for 1% of the time, Pallas kernels for 16%

profile of v9, /device:TPU:7, one launch (start us, length us, event | category | flops | bytes accessed | tf_op | source)
XLA Modules:
  0.0 85.2 jit_solution(4367804677280332259)
XLA Ops:
  0.6 1.9 %pack_keys.1 = bf16[16,128,128]{2,1,0:T(8,128)(2,1)} custom-call(bf16[64,2048]{1,0:T(8,128)(2,1)} %key_ref.1, bf16[64,2048]{1,0:T(8,128)(2,1)} %value_ref.1), custom_call_target="tpu_custom_call" | custom-call | tf_op jit(solution)/shard_map/pack_keys/pallas_call | solution.py:47
  2.5 6.8 %all-to-all-start = ((bf16[8,2,128,128]{3,2,1,0:T(8,128)(2,1)}), bf16[8,2,128,128]{3,2,1,0:T(8,128)(2,1)S(1)}, u32[]{:S(2)}, u32[]{:S(2)}) async-start(bf16[8,2,128,128]{3,2,1,0:T(8,128)(2,1)} %bitcast.9), calls=%async_computation | async-start | bytes 1048576 | tf_op jit(solution)/shard_map/all_to_all | solution.py:341
  9.3 4.3 %pack_queries.1 = bf16[2,8,264,128]{3,2,1,0:T(8,128)(2,1)} custom-call(bf16[64,4096]{1,0:T(8,128)(2,1)} %query_ref.1, bf16[64,4096]{1,0:T(8,128)(2,1)} %grad_ref.1, bf16[64,4096]{1,0:T(8,128)(2,1)} %row_ref.1, f32[32,64]{1,0:T(8,128)} %lse_ref.1), custom_call_target="tpu_custom_call" | custom-call | tf_op jit(solution)/shard_map/pack_queries/pallas_call | solution.py:102
  13.6 13.7 %all-to-all-done = bf16[8,2,128,128]{3,2,1,0:T(8,128)(2,1)S(1)} async-done(((bf16[8,2,128,128]{3,2,1,0:T(8,128)(2,1)}), bf16[8,2,128,128]{3,2,1,0:T(8,128)(2,1)S(1)}, u32[]{:S(2)}, u32[]{:S(2)}) %all-to-all-start) | async-done | bytes 524320 | tf_op jit(solution)/shard_map/all_to_all | solution.py:341
  27.3 0.0 copy-start
  27.3 4.2 %all-to-all-start.1 = ((bf16[16,264,128]{2,1,0:T(8,128)(2,1)}), bf16[16,264,128]{2,1,0:T(8,128)(2,1)S(1)}, u32[]{:S(2)}, u32[]{:S(2)}) async-start(bf16[16,264,128]{2,1,0:T(8,128)(2,1)} %bitcast.8), calls=%async_computation.1 | async-start | bytes 2162688 | tf_op jit(solution)/shard_map/all_to_all | solution.py:341
  31.4 0.0 copy-done
  31.5 0.1 select_bitcast_fusion
  31.6 4.0 %collective-permute-start.2 = (bf16[8,128,128]{2,1,0:T(8,128)(2,1)S(1)}, bf16[8,128,128]{2,1,0:T(8,128)(2,1)S(1)}, u32[]{:S(2)}, u32[]{:S(2)}) collective-permute-start(bf16[8,128,128]{2,1,0:T(8,128)(2,1)S(1)} %get-tuple-element.30.kv_near_ref.kv_ref), channel_id=1, source_target_pairs={{0,16},{8,24},{16,32},{24,40},{32,48},{40,56},{48,64},{56,72},{64,... | collective-permute-start | bytes 786440 | tf_op jit(solution)/shard_map/ppermute | solution.py:355
  35.6 1.0 %convert_reduce_fusion = s32[1024]{0:T(1024)S(1)} fusion(s32[1024]{0:T(1024)S(1)} %pad_dynamic-slice_fusion, s32[2048]{0:T(1024)S(1)} %pad_dynamic-slice_fusion.1), kind=kLoop, calls=%fused_computation | loop fusion | flops 6290432 | bytes 16384 | tf_op jit(solution)/shard_map/reduce_sum | solution.py:335
  36.6 4.4 %collective-permute-start.1 = (bf16[8,128,128]{2,1,0:T(8,128)(2,1)S(1)}, bf16[8,128,128]{2,1,0:T(8,128)(2,1)S(1)}, u32[]{:S(2)}, u32[]{:S(2)}) collective-permute-start(bf16[8,128,128]{2,1,0:T(8,128)(2,1)S(1)} %get-tuple-element.29), channel_id=1, source_target_pairs={{0,24},{8,16},{16,40},{24,32},{32,56},{40,48},{48,72},{56,64},{64,... | collective-permute-start | bytes 786440 | tf_op jit(solution)/shard_map/ppermute | solution.py:355
  40.9 1.9 %collective-permute-start = (bf16[8,128,128]{2,1,0:T(8,128)(2,1)S(1)}, bf16[8,128,128]{2,1,0:T(8,128)(2,1)S(1)}, u32[]{:S(2)}, u32[]{:S(2)}) collective-permute-start(bf16[8,128,128]{2,1,0:T(8,128)(2,1)S(1)} %get-tuple-element.29), channel_id=1, source_target_pairs={{0,8},{8,0},{1,9},{9,1},{2,10},{10,2},{3,11},{11,3},{4,12},{12,4},... | collective-permute-start | bytes 786440 | tf_op jit(solution)/shard_map/ppermute | solution.py:345
  42.9 6.2 %collective-permute-done.2.kv_ref = bf16[8,128,128]{2,1,0:T(8,128)(2,1)S(1)} collective-permute-done((bf16[8,128,128]{2,1,0:T(8,128)(2,1)S(1)}, bf16[8,128,128]{2,1,0:T(8,128)(2,1)S(1)}, u32[]{:S(2)}, u32[]{:S(2)}) %collective-permute-start.2) | collective-permute-done | bytes 262176 | tf_op jit(solution)/shard_map/ppermute | solution.py:355
  49.1 9.6 %all-to-all-done.1.q_ref = bf16[16,264,128]{2,1,0:T(8,128)(2,1)S(1)} async-done(((bf16[16,264,128]{2,1,0:T(8,128)(2,1)}), bf16[16,264,128]{2,1,0:T(8,128)(2,1)S(1)}, u32[]{:S(2)}, u32[]{:S(2)}) %all-to-all-start.1) | async-done | bytes 1081376 | tf_op jit(solution)/shard_map/all_to_all | solution.py:341
  58.7 2.9 %cross_near.1 = (f32[2,1024,128]{2,1,0:T(8,128)S(1)}, bf16[2,512,128]{2,1,0:T(8,128)(2,1)S(1)}) custom-call(s32[1]{0:T(128)} %bitcast.core_ref, bf16[8,128,128]{2,1,0:T(8,128)(2,1)S(1)} %collective-permute-done.2.kv_ref, bf16[16,264,128]{2,1,0:T(8,128)(2,1)S(1)} %all-to-all-done.1.q_ref, s32[8,1,128]{2,1,0:T(1,128)S(1)} %add_maximum_fusion.lo_ref), custom_call_target="tpu_custom_call" | custom-call | flops 1342177280 | bytes 4194304 | tf_op jit(solution)/shard_map/cross_near/pallas_call | solution.py:264
  61.6 10.9 %collective-permute-start.5 = (bf16[2,512,128]{2,1,0:T(8,128)(2,1)S(1)}, bf16[2,512,128]{2,1,0:T(8,128)(2,1)S(1)}, u32[]{:S(2)}, u32[]{:S(2)}) collective-permute-start(bf16[2,512,128]{2,1,0:T(8,128)(2,1)S(1)} %get-tuple-element.26), channel_id=1, source_target_pairs={{16,0},{24,8},{32,16},{40,24},{48,32},{56,40},{64,48},{72,56},{80,... | collective-permute-start | bytes 786440 | tf_op jit(solution)/shard_map/ppermute | solution.py:355
  72.5 0.0 collective-permute-done.1.kv_ref
  72.5 1.4 %cross_far.1 = (f32[2,1024,128]{2,1,0:T(8,128)S(1)}, bf16[2,512,128]{2,1,0:T(8,128)(2,1)S(1)}) custom-call(s32[1]{0:T(128)} %bitcast.core_ref, bf16[8,128,128]{2,1,0:T(8,128)(2,1)S(1)} %collective-permute-done.1.kv_ref, bf16[16,264,128]{2,1,0:T(8,128)(2,1)S(1)} %all-to-all-done.1.q_ref, s32[8,1,128]{2,1,0:T(1,128)S(1)} %add_maximum_fusion.lo_ref, ...), custom_call_target="tpu_custom_call" | custom-call | flops 1342177280 | bytes 4194304 | tf_op jit(solution)/shard_map/cross_far/pallas_call | solution.py:264
  73.9 2.3 %collective-permute-start.4 = (bf16[2,512,128]{2,1,0:T(8,128)(2,1)S(1)}, bf16[2,512,128]{2,1,0:T(8,128)(2,1)S(1)}, u32[]{:S(2)}, u32[]{:S(2)}) collective-permute-start(bf16[2,512,128]{2,1,0:T(8,128)(2,1)S(1)} %get-tuple-element.24), channel_id=1, source_target_pairs={{16,8},{24,0},{32,24},{40,16},{48,40},{56,32},{64,56},{72,48},{80,... | collective-permute-start | bytes 786440 | tf_op jit(solution)/shard_map/ppermute | solution.py:355
  76.3 0.0 collective-permute-done.kv_far_ref
  76.3 3.2 %own_far.1 = (bf16[4,512,128]{2,1,0:T(8,128)(2,1)S(1)}, f32[2,512,128]{2,1,0:T(8,128)S(1)}, f32[2,512,128]{2,1,0:T(8,128)S(1)}) custom-call(s32[1]{0:T(128)} %bitcast.core_ref, bf16[8,128,128]{2,1,0:T(8,128)(2,1)S(1)} %get-tuple-element.30.kv_near_ref.kv_ref, bf16[8,128,128]{2,1,0:T(8,128)(2,1)S(1)} %collective-permute-done.kv_far_ref, ...), custom_call_target="tpu_custom_call" | custom-call | flops 1342177280 | bytes 4194304 | tf_op jit(solution)/shard_map/own_far/pallas_call | solution.py:280
  79.4 1.9 %collective-permute-start.3 = (bf16[4,512,128]{2,1,0:T(8,128)(2,1)S(1)}, bf16[4,512,128]{2,1,0:T(8,128)(2,1)S(1)}, u32[]{:S(2)}, u32[]{:S(2)}) collective-permute-start(bf16[4,512,128]{2,1,0:T(8,128)(2,1)S(1)} %get-tuple-element.23), channel_id=1, source_target_pairs={{0,8},{8,0},{1,9},{9,1},{2,10},{10,2},{3,11},{11,3},{4,12},{12,4},... | collective-permute-start | bytes 1572872 | tf_op jit(solution)/shard_map/ppermute | solution.py:345
  81.4 1.5 %own_near.1 = (bf16[2,512,128]{2,1,0:T(8,128)(2,1)S(1)}, f32[2,512,128]{2,1,0:T(8,128)S(1)}) custom-call(s32[1]{0:T(128)} %bitcast.core_ref, bf16[8,128,128]{2,1,0:T(8,128)(2,1)S(1)} %get-tuple-element.30.kv_near_ref.kv_ref, bf16[16,264,128]{2,1,0:T(8,128)(2,1)S(1)} %all-to-all-done.1.q_ref, s32[8,1,128]{2,1,0:T(1,128)S(1)} %add_maximum_fusion.lo_ref, ...), custom_call_target="tpu_custom_call" | custom-call | flops 1342177280 | bytes 4194304 | tf_op jit(solution)/shard_map/own_near/pallas_call | solution.py:280
  82.9 0.0 collective-permute-done.5.back_ref
  82.9 0.1 join_near.1
  83.0 1.0 %collective-permute-done.4.back_ref = bf16[2,512,128]{2,1,0:T(8,128)(2,1)S(1)} collective-permute-done((bf16[2,512,128]{2,1,0:T(8,128)(2,1)S(1)}, bf16[2,512,128]{2,1,0:T(8,128)(2,1)S(1)}, u32[]{:S(2)}, u32[]{:S(2)}) %collective-permute-start.4) | collective-permute-done | bytes 262176 | tf_op jit(solution)/shard_map/ppermute | solution.py:355
  84.0 0.0 collective-permute-done.3.swapped_ref
  84.0 1.2 %join_far.1 = (bf16[512,512]{1,0:T(8,128)(2,1)}, bf16[512,256]{1,0:T(8,128)(2,1)}, bf16[512,256]{1,0:T(8,128)(2,1)}) custom-call(s32[1]{0:T(128)} %bitcast.core_ref, bf16[2,512,128]{2,1,0:T(8,128)(2,1)S(1)} %get-tuple-element.22.near_dq_ref, bf16[4,512,128]{2,1,0:T(8,128)(2,1)S(1)} %collective-permute-done.3.swapped_ref, ...), custom_call_target="tpu_custom_call" | custom-call | flops 1048576 | bytes 1048576 | tf_op jit(solution)/shard_map/join_far/pallas_call | solution.py:320
  (3 shorter events, 0.0 us)
Async XLA Ops:
  2.5 24.8 %all-to-all-start = ((bf16[8,2,128,128]{3,2,1,0:T(8,128)(2,1)}), bf16[8,2,128,128]{3,2,1,0:T(8,128)(2,1)S(1)}, u32[]{:S(2)}, u32[]{:S(2)}) async-start(bf16[8,2,128,128]{3,2,1,0:T(8,128)(2,1)} %bitcast.9), calls=%async_computation | async-start | bytes 1048576 | tf_op jit(solution)/shard_map/all_to_all | solution.py:341
  27.3 4.2 %copy-start = (s32[32768]{0:T(1024)S(1)}, s32[32768]{0:T(1024)}, u32[]{:S(2)}) copy-start(s32[32768]{0:T(1024)} %param.13) | copy-start | bytes 393220
  27.3 31.4 %all-to-all-start.1 = ((bf16[16,264,128]{2,1,0:T(8,128)(2,1)}), bf16[16,264,128]{2,1,0:T(8,128)(2,1)S(1)}, u32[]{:S(2)}, u32[]{:S(2)}) async-start(bf16[16,264,128]{2,1,0:T(8,128)(2,1)} %bitcast.8), calls=%async_computation.1 | async-start | bytes 2162688 | tf_op jit(solution)/shard_map/all_to_all | solution.py:341
  31.6 17.5 %collective-permute-start.2 = (bf16[8,128,128]{2,1,0:T(8,128)(2,1)S(1)}, bf16[8,128,128]{2,1,0:T(8,128)(2,1)S(1)}, u32[]{:S(2)}, u32[]{:S(2)}) collective-permute-start(bf16[8,128,128]{2,1,0:T(8,128)(2,1)S(1)} %get-tuple-element.30.kv_near_ref.kv_ref), channel_id=1, source_target_pairs={{0,16},{8,24},{16,32},{24,40},{32,48},{40,56},{48,64},{56,72},{64,... | collective-permute-start | bytes 786440 | tf_op jit(solution)/shard_map/ppermute | solution.py:355
  36.6 35.9 %collective-permute-start.1 = (bf16[8,128,128]{2,1,0:T(8,128)(2,1)S(1)}, bf16[8,128,128]{2,1,0:T(8,128)(2,1)S(1)}, u32[]{:S(2)}, u32[]{:S(2)}) collective-permute-start(bf16[8,128,128]{2,1,0:T(8,128)(2,1)S(1)} %get-tuple-element.29), channel_id=1, source_target_pairs={{0,24},{8,16},{16,40},{24,32},{32,56},{40,48},{48,72},{56,64},{64,... | collective-permute-start | bytes 786440 | tf_op jit(solution)/shard_map/ppermute | solution.py:355
  40.9 35.3 %collective-permute-start = (bf16[8,128,128]{2,1,0:T(8,128)(2,1)S(1)}, bf16[8,128,128]{2,1,0:T(8,128)(2,1)S(1)}, u32[]{:S(2)}, u32[]{:S(2)}) collective-permute-start(bf16[8,128,128]{2,1,0:T(8,128)(2,1)S(1)} %get-tuple-element.29), channel_id=1, source_target_pairs={{0,8},{8,0},{1,9},{9,1},{2,10},{10,2},{3,11},{11,3},{4,12},{12,4},... | collective-permute-start | bytes 786440 | tf_op jit(solution)/shard_map/ppermute | solution.py:345
  61.6 21.3 %collective-permute-start.5 = (bf16[2,512,128]{2,1,0:T(8,128)(2,1)S(1)}, bf16[2,512,128]{2,1,0:T(8,128)(2,1)S(1)}, u32[]{:S(2)}, u32[]{:S(2)}) collective-permute-start(bf16[2,512,128]{2,1,0:T(8,128)(2,1)S(1)} %get-tuple-element.26), channel_id=1, source_target_pairs={{16,0},{24,8},{32,16},{40,24},{48,32},{56,40},{64,48},{72,56},{80,... | collective-permute-start | bytes 786440 | tf_op jit(solution)/shard_map/ppermute | solution.py:355
  73.9 10.1 %collective-permute-start.4 = (bf16[2,512,128]{2,1,0:T(8,128)(2,1)S(1)}, bf16[2,512,128]{2,1,0:T(8,128)(2,1)S(1)}, u32[]{:S(2)}, u32[]{:S(2)}) collective-permute-start(bf16[2,512,128]{2,1,0:T(8,128)(2,1)S(1)} %get-tuple-element.24), channel_id=1, source_target_pairs={{16,8},{24,0},{32,24},{40,16},{48,40},{56,32},{64,56},{72,48},{80,... | collective-permute-start | bytes 786440 | tf_op jit(solution)/shard_map/ppermute | solution.py:355
  79.4 4.6 %collective-permute-start.3 = (bf16[4,512,128]{2,1,0:T(8,128)(2,1)S(1)}, bf16[4,512,128]{2,1,0:T(8,128)(2,1)S(1)}, u32[]{:S(2)}, u32[]{:S(2)}) collective-permute-start(bf16[4,512,128]{2,1,0:T(8,128)(2,1)S(1)} %get-tuple-element.23), channel_id=1, source_target_pairs={{0,8},{8,0},{1,9},{9,1},{2,10},{10,2},{3,11},{11,3},{4,12},{12,4},... | collective-permute-start | bytes 1572872 | tf_op jit(solution)/shard_map/ppermute | solution.py:345

commit v10 on v8

--- a/solution.py
+++ b/solution.py
@@ -287,16 +287,22 @@
                 out_ref[:, columns] = (near_ref[i] + back_ref[i].astype(f32)).astype(bf16)
 
 
-def join_far_kernel(core_ref, near_dq_ref, swapped_ref, back_ref, near_dk_ref, near_dv_ref, dq_ref, dk_ref, dv_ref):
-    for core in range(CORES):
-
-        @pl.when(core_ref[0] == core)
-        def _():
-            for a in range(2):
-                at = 2 * core + a
-                dq_ref[:, at * HEAD_SIZE : (at + 1) * HEAD_SIZE] = near_dq_ref[a]
-                at = 2 * (1 - core) + a
-                dq_ref[:, at * HEAD_SIZE : (at + 1) * HEAD_SIZE] = swapped_ref[a]
+def join_queries_kernel(core_ref, near_ref, swapped_ref, dq_ref):
+    for core in range(CORES):
+
+        @pl.when(core_ref[0] == core)
+        def _():
+            for half_ref, k in ((near_ref, core), (swapped_ref, 1 - core)):
+                for a in range(2):
+                    at = 2 * k + a
+                    dq_ref[:, at * HEAD_SIZE : (at + 1) * HEAD_SIZE] = half_ref[a]
+
+
+def join_far_kernel(core_ref, swapped_ref, back_ref, near_dk_ref, near_dv_ref, dk_ref, dv_ref):
+    for core in range(CORES):
+
+        @pl.when(core_ref[0] == core)
+        def _():
             near = slice(core * HEAD_SIZE, (core + 1) * HEAD_SIZE)
             far = slice((1 - core) * HEAD_SIZE, (2 - core) * HEAD_SIZE)
             for i, (half_ref, out_ref) in enumerate(((near_dk_ref, dk_ref), (near_dv_ref, dv_ref))):
@@ -359,12 +365,9 @@
     keys_shape = jax.ShapeDtypeStruct((HALF, 2 * HEAD_SIZE), bf16)
     queries_shape = jax.ShapeDtypeStruct((HALF, 4 * HEAD_SIZE), bf16)
     halves = join(join_near_kernel, "join_near", [keys_shape] * 2, 10000, core, own_near, back_near)
-    return tuple(
-        join(
-            join_far_kernel, "join_far", [queries_shape, keys_shape, keys_shape], 1,
-            core, near_dq, swapped, back_far, *halves,
-        )
-    )
+    (query_grad,) = join(join_queries_kernel, "join_queries", [queries_shape], 1000, core, near_dq, swapped)
+    key_grad, value_grad = join(join_far_kernel, "join_far", [keys_shape] * 2, 1, core, swapped, back_far, *halves)
+    return query_grad, key_grad, value_grad
 
 
 def solution(mesh):

time: 84.8 us -> 85.4 us (level)
    ppermute x1, waiting for transfers between devices: 1.03 us -> 0.01 us  [on_device(): lax.ppermute(far, ('chip', 'core'), [(CORES * (c + 1) + k, CORES * c + 1...]
    pallas_call x2 -> x3, Pallas kernels: 1.22 us -> 1.84 us  [join(): pl.pallas_call(kernel, in_specs=[smem_spec()] + [vmem_spec()] * (len(oper...]
  transfers between devices with their start and end apart: 6 -> 6, of which waited for: 4 -> 4; matrix products, arithmetic and copies ran while one was open for 1% -> 1% of each run, Pallas kernels for 12% -> 13%
where the time goes in v10:
time: 85.4 us; the launch traced here: 84.1 us
  waiting for transfers between devices  32.9 us (39%)
  starting transfers between devices  32.5 us (38%)
  Pallas kernels  17 us (20%)
  other arithmetic  0.99 us (1%)
    ppermute x1, waiting for transfers between devices, on_device(): kv_before = lax.ppermute(kv, 'chip', [(c, c + 1) for c in range(chips - 1)])  18.1 us
    all_to_all x2, waiting for transfers between devices, exchange(): lax.all_to_all(value, ('core', 'head'), split_axis=0, concat_axis=0, tile...  14.6 us
    all_to_all x2, starting transfers between devices, exchange(): lax.all_to_all(value, ('core', 'head'), split_axis=0, concat_axis=0, tile...  13.4 us
    ppermute x1, starting transfers between devices, on_device(): lax.ppermute(near, 'chip', [(c + 1, c) for c in range(chips - 1)])  10.9 us
    pallas_call x2, Pallas kernels, own_call(): pl.pallas_call(kernel, in_specs=[smem_spec()] + [vmem_spec()] * (len(oper...  4.68 us
    pallas_call x1, Pallas kernels, pack_queries(): pl.pallas_call(pack_queries_kernel, grid=(steps,), in_specs=[pl.BlockSpec...  4.3 us
    pallas_call x2, Pallas kernels, cross_terms(): pl.pallas_call(functools.partial(cross_kernel, near), in_specs=[smem_spec...  4.28 us
    ppermute x1, starting transfers between devices, on_device(): kv_before = lax.ppermute(kv, 'chip', [(c, c + 1) for c in range(chips - 1)])  4.03 us
  transfers between devices with their start and end apart: 6, of which 4 were waited for; matrix products, arithmetic and copies ran while one was open for 1% of the time, Pallas kernels for 13%

profile of v10, /device:TPU:7, one launch (start us, length us, event | category | flops | bytes accessed | tf_op | source)
XLA Modules:
  0.0 84.1 jit_solution(5790635529559597029)
XLA Ops:
  0.6 1.9 %pack_keys.1 = bf16[2,8,128,128]{3,2,1,0:T(8,128)(2,1)} custom-call(bf16[64,2048]{1,0:T(8,128)(2,1)} %key_ref.1, bf16[64,2048]{1,0:T(8,128)(2,1)} %value_ref.1), custom_call_target="tpu_custom_call" | custom-call | tf_op jit(solution)/shard_map/pack_keys/pallas_call | solution.py:47
  2.5 7.8 %all-to-all-start = ((bf16[16,128,128]{2,1,0:T(8,128)(2,1)}), bf16[16,128,128]{2,1,0:T(8,128)(2,1)S(1)}, u32[]{:S(2)}, u32[]{:S(2)}) async-start(bf16[16,128,128]{2,1,0:T(8,128)(2,1)} %bitcast.5), calls=%async_computation | async-start | bytes 1048576 | tf_op jit(solution)/shard_map/all_to_all | solution.py:336
  10.3 4.3 %pack_queries.1 = bf16[2,8,264,128]{3,2,1,0:T(8,128)(2,1)} custom-call(bf16[64,4096]{1,0:T(8,128)(2,1)} %query_ref.1, bf16[64,4096]{1,0:T(8,128)(2,1)} %grad_ref.1, bf16[64,4096]{1,0:T(8,128)(2,1)} %row_ref.1, f32[32,64]{1,0:T(8,128)} %lse_ref.1), custom_call_target="tpu_custom_call" | custom-call | tf_op jit(solution)/shard_map/pack_queries/pallas_call | solution.py:102
  14.6 10.5 %all-to-all-done.kv_ref = bf16[16,128,128]{2,1,0:T(8,128)(2,1)S(1)} async-done(((bf16[16,128,128]{2,1,0:T(8,128)(2,1)}), bf16[16,128,128]{2,1,0:T(8,128)(2,1)S(1)}, u32[]{:S(2)}, u32[]{:S(2)}) %all-to-all-start) | async-done | bytes 524320 | tf_op jit(solution)/shard_map/all_to_all | solution.py:336
  25.1 0.0 copy-start
  25.1 5.6 %all-to-all-start.1 = ((bf16[16,264,128]{2,1,0:T(8,128)(2,1)}), bf16[16,264,128]{2,1,0:T(8,128)(2,1)S(1)}, u32[]{:S(2)}, u32[]{:S(2)}) async-start(bf16[16,264,128]{2,1,0:T(8,128)(2,1)} %bitcast.4), calls=%async_computation.1 | async-start | bytes 2162688 | tf_op jit(solution)/shard_map/all_to_all | solution.py:336
  30.6 0.0 copy-done
  30.7 4.0 %collective-permute-start = (bf16[16,128,128]{2,1,0:T(8,128)(2,1)S(1)}, bf16[16,128,128]{2,1,0:T(8,128)(2,1)S(1)}, u32[]{:S(2)}, u32[]{:S(2)}) collective-permute-start(bf16[16,128,128]{2,1,0:T(8,128)(2,1)S(1)} %all-to-all-done.kv_ref), channel_id=1, source_target_pairs={{0,16},{16,32},{32,48},{48,64},{64,80},{80,96},{96,112},{112,128},... | collective-permute-start | bytes 1572872 | tf_op jit(solution)/shard_map/ppermute | solution.py:349
  34.7 1.0 %convert_reduce_fusion = s32[1024]{0:T(1024)S(1)} fusion(s32[1024]{0:T(1024)S(1)} %pad_dynamic-slice_fusion, s32[2048]{0:T(1024)S(1)} %pad_dynamic-slice_fusion.1), kind=kLoop, calls=%fused_computation | loop fusion | flops 6290432 | bytes 16384 | tf_op jit(solution)/shard_map/reduce_sum | solution.py:329
  35.7 18.1 %collective-permute-done.kv_ref = bf16[16,128,128]{2,1,0:T(8,128)(2,1)S(1)} collective-permute-done((bf16[16,128,128]{2,1,0:T(8,128)(2,1)S(1)}, bf16[16,128,128]{2,1,0:T(8,128)(2,1)S(1)}, u32[]{:S(2)}, u32[]{:S(2)}) %collective-permute-start) | collective-permute-done | bytes 524320 | tf_op jit(solution)/shard_map/ppermute | solution.py:349
  53.8 4.1 %all-to-all-done.1.q_ref = bf16[16,264,128]{2,1,0:T(8,128)(2,1)S(1)} async-done(((bf16[16,264,128]{2,1,0:T(8,128)(2,1)}), bf16[16,264,128]{2,1,0:T(8,128)(2,1)S(1)}, u32[]{:S(2)}, u32[]{:S(2)}) %all-to-all-start.1) | async-done | bytes 1081376 | tf_op jit(solution)/shard_map/all_to_all | solution.py:336
  57.9 2.9 %cross_near.1 = (f32[2,1024,128]{2,1,0:T(8,128)S(1)}, bf16[2,512,128]{2,1,0:T(8,128)(2,1)S(1)}) custom-call(s32[1]{0:T(128)} %bitcast.core_ref, bf16[16,128,128]{2,1,0:T(8,128)(2,1)S(1)} %collective-permute-done.kv_ref, bf16[16,264,128]{2,1,0:T(8,128)(2,1)S(1)} %all-to-all-done.1.q_ref, s32[8,1,128]{2,1,0:T(1,128)S(1)} %add_maximum_fusion.lo_ref), custom_call_target="tpu_custom_call" | custom-call | flops 1342177280 | bytes 4194304 | tf_op jit(solution)/shard_map/cross_near/pallas_call | solution.py:252
  60.8 10.9 %collective-permute-start.3 = (bf16[2,512,128]{2,1,0:T(8,128)(2,1)S(1)}, bf16[2,512,128]{2,1,0:T(8,128)(2,1)S(1)}, u32[]{:S(2)}, u32[]{:S(2)}) collective-permute-start(bf16[2,512,128]{2,1,0:T(8,128)(2,1)S(1)} %get-tuple-element.28), channel_id=1, source_target_pairs={{16,0},{32,16},{48,32},{64,48},{80,64},{96,80},{112,96},{128,112},... | collective-permute-start | bytes 786440 | tf_op jit(solution)/shard_map/ppermute | solution.py:351
  71.7 1.4 %cross_far.1 = (f32[2,1024,128]{2,1,0:T(8,128)S(1)}, bf16[2,512,128]{2,1,0:T(8,128)(2,1)S(1)}) custom-call(s32[1]{0:T(128)} %bitcast.core_ref, bf16[16,128,128]{2,1,0:T(8,128)(2,1)S(1)} %collective-permute-done.kv_ref, bf16[16,264,128]{2,1,0:T(8,128)(2,1)S(1)} %all-to-all-done.1.q_ref, s32[8,1,128]{2,1,0:T(1,128)S(1)} %add_maximum_fusion.lo_ref, ...), custom_call_target="tpu_custom_call" | custom-call | flops 1342177280 | bytes 4194304 | tf_op jit(solution)/shard_map/cross_far/pallas_call | solution.py:252
  73.1 2.2 %collective-permute-start.2 = (bf16[2,512,128]{2,1,0:T(8,128)(2,1)S(1)}, bf16[2,512,128]{2,1,0:T(8,128)(2,1)S(1)}, u32[]{:S(2)}, u32[]{:S(2)}) collective-permute-start(bf16[2,512,128]{2,1,0:T(8,128)(2,1)S(1)} %get-tuple-element.26), channel_id=1, source_target_pairs={{16,8},{24,0},{32,24},{40,16},{48,40},{56,32},{64,56},{72,48},{80,... | collective-permute-start | bytes 786440 | tf_op jit(solution)/shard_map/ppermute | solution.py:353
  75.4 3.2 %own_far.1 = (bf16[4,512,128]{2,1,0:T(8,128)(2,1)S(1)}, f32[2,512,128]{2,1,0:T(8,128)S(1)}, f32[2,512,128]{2,1,0:T(8,128)S(1)}) custom-call(s32[1]{0:T(128)} %bitcast.core_ref, bf16[16,128,128]{2,1,0:T(8,128)(2,1)S(1)} %all-to-all-done.kv_ref, bf16[16,264,128]{2,1,0:T(8,128)(2,1)S(1)} %all-to-all-done.1.q_ref, s32[8,1,128]{2,1,0:T(1,128)S(1)} %add_maximum_fusion.lo_ref, ...), custom_call_target="tpu_custom_call" | custom-call | flops 1342177280 | bytes 4194304 | tf_op jit(solution)/shard_map/own_far/pallas_call | solution.py:268
  78.5 1.9 %collective-permute-start.1 = (bf16[4,512,128]{2,1,0:T(8,128)(2,1)S(1)}, bf16[4,512,128]{2,1,0:T(8,128)(2,1)S(1)}, u32[]{:S(2)}, u32[]{:S(2)}) collective-permute-start(bf16[4,512,128]{2,1,0:T(8,128)(2,1)S(1)} %get-tuple-element.25), channel_id=1, source_target_pairs={{0,8},{8,0},{1,9},{9,1},{2,10},{10,2},{3,11},{11,3},{4,12},{12,4},... | collective-permute-start | bytes 1572872 | tf_op jit(solution)/shard_map/ppermute | solution.py:361
  80.5 1.5 %own_near.1 = (bf16[2,512,128]{2,1,0:T(8,128)(2,1)S(1)}, f32[2,512,128]{2,1,0:T(8,128)S(1)}) custom-call(s32[1]{0:T(128)} %bitcast.core_ref, bf16[16,128,128]{2,1,0:T(8,128)(2,1)S(1)} %all-to-all-done.kv_ref, bf16[16,264,128]{2,1,0:T(8,128)(2,1)S(1)} %all-to-all-done.1.q_ref, s32[8,1,128]{2,1,0:T(1,128)S(1)} %add_maximum_fusion.lo_ref, ...), custom_call_target="tpu_custom_call" | custom-call | flops 1342177280 | bytes 4194304 | tf_op jit(solution)/shard_map/own_near/pallas_call | solution.py:268
  82.0 0.0 collective-permute-done.3.back_ref
  82.0 0.1 join_near.1
  82.1 0.3 collective-permute-done.1.swapped_ref
  82.3 0.9 %join_queries.1 = bf16[512,512]{1,0:T(8,128)(2,1)} custom-call(s32[1]{0:T(128)} %bitcast.core_ref, bf16[2,512,128]{2,1,0:T(8,128)(2,1)S(1)} %get-tuple-element.24.near_ref, bf16[4,512,128]{2,1,0:T(8,128)(2,1)S(1)} %collective-permute-done.1.swapped_ref), custom_call_target="tpu_custom_call" | custom-call | flops 1048576000 | bytes 1048576 | tf_op jit(solution)/shard_map/join_queries/pallas_call | solution.py:314
  83.2 0.0 collective-permute-done.2.back_ref
  83.2 0.9 %join_far.1 = (bf16[512,256]{1,0:T(8,128)(2,1)}, bf16[512,256]{1,0:T(8,128)(2,1)}) custom-call(s32[1]{0:T(128)} %bitcast.core_ref, bf16[4,512,128]{2,1,0:T(8,128)(2,1)S(1)} %collective-permute-done.1.swapped_ref, bf16[2,512,128]{2,1,0:T(8,128)(2,1)S(1)} %collective-permute-done.2.back_ref, bf16[512,256]{1,0:T(8,128)(2,1)S(1)} %get-tuple-element.29.near_dk_ref, ...), custom_call_target="tpu_custom_call" | custom-call | flops 1048576 | bytes 1048576 | tf_op jit(solution)/shard_map/join_far/pallas_call | solution.py:314
  (3 shorter events, 0.0 us)
Async XLA Ops:
  2.5 22.6 %all-to-all-start = ((bf16[16,128,128]{2,1,0:T(8,128)(2,1)}), bf16[16,128,128]{2,1,0:T(8,128)(2,1)S(1)}, u32[]{:S(2)}, u32[]{:S(2)}) async-start(bf16[16,128,128]{2,1,0:T(8,128)(2,1)} %bitcast.5), calls=%async_computation | async-start | bytes 1048576 | tf_op jit(solution)/shard_map/all_to_all | solution.py:336
  25.1 5.6 %copy-start = (s32[32768]{0:T(1024)S(1)}, s32[32768]{0:T(1024)}, u32[]{:S(2)}) copy-start(s32[32768]{0:T(1024)} %param.13) | copy-start | bytes 393220
  25.1 32.8 %all-to-all-start.1 = ((bf16[16,264,128]{2,1,0:T(8,128)(2,1)}), bf16[16,264,128]{2,1,0:T(8,128)(2,1)S(1)}, u32[]{:S(2)}, u32[]{:S(2)}) async-start(bf16[16,264,128]{2,1,0:T(8,128)(2,1)} %bitcast.4), calls=%async_computation.1 | async-start | bytes 2162688 | tf_op jit(solution)/shard_map/all_to_all | solution.py:336
  30.7 23.1 %collective-permute-start = (bf16[16,128,128]{2,1,0:T(8,128)(2,1)S(1)}, bf16[16,128,128]{2,1,0:T(8,128)(2,1)S(1)}, u32[]{:S(2)}, u32[]{:S(2)}) collective-permute-start(bf16[16,128,128]{2,1,0:T(8,128)(2,1)S(1)} %all-to-all-done.kv_ref), channel_id=1, source_target_pairs={{0,16},{16,32},{32,48},{48,64},{64,80},{80,96},{96,112},{112,128},... | collective-permute-start | bytes 1572872 | tf_op jit(solution)/shard_map/ppermute | solution.py:349
  60.8 21.2 %collective-permute-start.3 = (bf16[2,512,128]{2,1,0:T(8,128)(2,1)S(1)}, bf16[2,512,128]{2,1,0:T(8,128)(2,1)S(1)}, u32[]{:S(2)}, u32[]{:S(2)}) collective-permute-start(bf16[2,512,128]{2,1,0:T(8,128)(2,1)S(1)} %get-tuple-element.28), channel_id=1, source_target_pairs={{16,0},{32,16},{48,32},{64,48},{80,64},{96,80},{112,96},{128,112},... | collective-permute-start | bytes 786440 | tf_op jit(solution)/shard_map/ppermute | solution.py:351
  73.1 10.1 %collective-permute-start.2 = (bf16[2,512,128]{2,1,0:T(8,128)(2,1)S(1)}, bf16[2,512,128]{2,1,0:T(8,128)(2,1)S(1)}, u32[]{:S(2)}, u32[]{:S(2)}) collective-permute-start(bf16[2,512,128]{2,1,0:T(8,128)(2,1)S(1)} %get-tuple-element.26), channel_id=1, source_target_pairs={{16,8},{24,0},{32,24},{40,16},{48,40},{56,32},{64,56},{72,48},{80,... | collective-permute-start | bytes 786440 | tf_op jit(solution)/shard_map/ppermute | solution.py:353
  78.5 3.8 %collective-permute-start.1 = (bf16[4,512,128]{2,1,0:T(8,128)(2,1)S(1)}, bf16[4,512,128]{2,1,0:T(8,128)(2,1)S(1)}, u32[]{:S(2)}, u32[]{:S(2)}) collective-permute-start(bf16[4,512,128]{2,1,0:T(8,128)(2,1)S(1)} %get-tuple-element.25), channel_id=1, source_target_pairs={{0,8},{8,0},{1,9},{9,1},{2,10},{10,2},{3,11},{11,3},{4,12},{12,4},... | collective-permute-start | bytes 1572872 | tf_op jit(solution)/shard_map/ppermute | solution.py:361
